TPU v7x, 32 devices: a whole 2x2x4 slice. The times are simulated.
32 devices in a mesh: slab: 8 (over y, x, core), grp: 4 (over z).
Axes of the slice: x: 2, y: 2, z: 4, core: 2. Of those that a mesh axis runs over, the one named last changes fastest.
Arguments:
- pressure: float32 [64, 512, 256], P('slab', 'grp'), may hold values from -6 to 6
- velocity: float32 [3, 64, 512, 256], P(None, 'slab', 'grp'), may hold values from -6 to 6
- stiffness: float32 [64, 512, 256], P('slab', 'grp'), may hold values from 1 to 2.5
- buoyancy: float32 [64, 512, 256], P('slab', 'grp'), may hold values from 0.5 to 1
- traces: bfloat16 [1024, 128], P(('slab', 'grp')), may hold values from -6 to 6
- lateral: bfloat16 [1024, 2, 8], P(('slab', 'grp')), may hold values from -1 to 1
- routes: int32 [1024, 2], replicated, may hold values from 0 to 7, all different within a row; in each aligned block of 32 rows (0 to 31, 32 to 63, ...) at most 8 rows name the same one
- ycenter: int32 [1024], replicated, may hold values from 0 to 511
Outputs:
- pressure_out: float32 [64, 512, 256], P('slab', 'grp')
- velocity_out: float32 [3, 64, 512, 256], P(None, 'slab', 'grp')
Inputs may be any that keep to these rules, and one draw needn't show every extreme that they name: `routes`: each sensor lists 2 different slabs; among the 32 sensors held by one device no slab is listed more than 8 times, a bound that some block reaches.
All inputs are finite; a program needn't handle non-finite values.
Results may differ from a plain program's by a relative error of at most 0.0029.
Values may be sent and summed in bfloat16 or wider, within the bound.
No kernel may reach another device: no remote copies, remote signals or barrier semaphores. Data moves between devices by JAX's collectives and lax.ppermute only.
A program may use at most 64 MiB of HBM per device.

v0:
```python
import jax
import jax.numpy as jnp
from jax import lax
from jax.sharding import PartitionSpec as P

CY = 128
TR_DEV = 32
STEPS = 16
CAP = 8


TIME_STEP = 0.3


def passed_along(value, axis, steps):
    count = lax.axis_size(axis)
    first, last = (max(0, -steps), min(count, count - steps))
    return lax.ppermute(value, axis, [(source, source + steps) for source in range(first, last)])


def band_rows(centres, rows_y):
    distance = jnp.abs(rows_y[None, :] - centres[:, None]).astype(jnp.float32)
    return jnp.maximum(0.0, 1.0 - distance / float(CY)).astype(jnp.bfloat16)


def slot_centres(routes, ycenter, block_at, target):
    own_routes = lax.dynamic_slice_in_dim(routes, block_at * TR_DEV, TR_DEV, 0)
    named_by = jnp.any(own_routes == target, axis=1).astype(jnp.int32)
    position = jnp.cumsum(named_by) - named_by
    slot_ids = jnp.arange(CAP, dtype=jnp.int32)
    select = (named_by[None, :] == 1) & (position[None, :] == slot_ids[:, None])
    own_centres = lax.dynamic_slice_in_dim(ycenter, block_at * TR_DEV, TR_DEV, 0)
    return jnp.sum(jnp.where(select, own_centres[None, :], 0), axis=1)


def outer_rows(row_block, lat_block):
    outer_terms = (
        lat_block.astype(jnp.float32)[:, :, :, None] * row_block.astype(jnp.float32)[:, :, None, :]
    ).astype(jnp.bfloat16)
    return outer_terms.reshape(-1, outer_terms.shape[2], outer_terms.shape[3])


def local(pressure, velocity, stiffness, buoyancy, traces, lateral, routes, ycenter):
    slab_count = lax.axis_size("slab")
    group_count = lax.axis_size("grp")
    slab_at = lax.axis_index("slab")
    group_at = lax.axis_index("grp")
    cells_x, cells_y, cells_z = pressure.shape
    samples = traces.shape[1]
    block_at = slab_at * group_count + group_at
    own_routes = lax.dynamic_slice_in_dim(routes, block_at * TR_DEV, TR_DEV, 0)
    targets = jnp.arange(slab_count, dtype=jnp.int32)
    matches = own_routes[:, :, None] == targets[None, None, :]
    named_by = jnp.any(matches, axis=1).astype(jnp.int32)
    position = jnp.cumsum(named_by, axis=0) - named_by
    slot_ids = jnp.arange(CAP, dtype=jnp.int32)
    select = (
        (named_by.T[:, None, :] == 1) & (position.T[:, None, :] == slot_ids[None, :, None])
    ).astype(jnp.float32)
    send_rows = jnp.einsum("dct,tz->dcz", select, traces.astype(jnp.float32)).astype(jnp.bfloat16)
    lat_target = jnp.einsum(
        "tkd,tkx->tdx", matches.astype(jnp.float32), lateral.astype(jnp.float32)
    )
    send_lat = jnp.einsum("dct,tdx->dcx", select, lat_target).astype(jnp.bfloat16)
    got_rows, got_lat = (
        lax.all_to_all(send_rows, "slab", split_axis=0, concat_axis=0, tiled=True),
        lax.all_to_all(send_lat, "slab", split_axis=0, concat_axis=0, tiled=True),
    )
    centres = jax.vmap(
        lambda source_slab: slot_centres(
            routes, ycenter, source_slab * group_count + group_at, slab_at
        )
    )(targets).reshape(-1)
    outer_terms = outer_rows(got_rows, got_lat)
    rows_y = jnp.arange(cells_y * lax.axis_size("grp"), dtype=jnp.int32)
    profile = band_rows(centres, rows_y)
    injected = lax.psum_scatter(
        jnp.einsum("ry,rxz->yxz", profile, outer_terms, preferred_element_type=jnp.float32).astype(
            jnp.bfloat16
        ),
        "grp",
        scatter_dimension=0,
        tiled=True,
    ).astype(jnp.float32)
    source = jnp.pad(jnp.transpose(injected, (1, 0, 2)), ((0, 0), (0, 0), (cells_z - samples, 0)))

    def advance(step_at, fields):
        pres_now, vel_now = fields
        ahead_x = passed_along(pres_now[:1], "slab", -1)
        ahead_y = passed_along(pres_now[:, :1], "grp", -1)
        zero_z = jnp.zeros_like(pres_now[:, :, :1])
        grad_x = jnp.concatenate([pres_now[1:], ahead_x], 0) - pres_now
        grad_y = jnp.concatenate([pres_now[:, 1:], ahead_y], 1) - pres_now
        grad_z = jnp.concatenate([pres_now[:, :, 1:], zero_z], 2) - pres_now
        vel_x = vel_now[0] - TIME_STEP * buoyancy * grad_x
        vel_y = vel_now[1] - TIME_STEP * buoyancy * grad_y
        vel_z = vel_now[2] - TIME_STEP * buoyancy * grad_z
        behind_x = passed_along(vel_x[-1:], "slab", 1)
        behind_y = passed_along(vel_y[:, -1:], "grp", 1)
        divergence = vel_x - jnp.concatenate([behind_x, vel_x[:-1]], 0)
        divergence = divergence + vel_y - jnp.concatenate([behind_y, vel_y[:, :-1]], 1)
        divergence = divergence + vel_z - jnp.concatenate([zero_z, vel_z[:, :, :-1]], 2)
        pres_next = pres_now - TIME_STEP * stiffness * divergence + TIME_STEP * source
        return (pres_next, jnp.stack([vel_x, vel_y, vel_z]))

    pres_end, vel_end = lax.fori_loop(0, STEPS, advance, (pressure, velocity))
    return (pres_end, vel_end)


def solution(mesh):
    in_specs = (
        P("slab", "grp", None),
        P(None, "slab", "grp", None),
        P("slab", "grp", None),
        P("slab", "grp", None),
        P(("slab", "grp"), None),
        P(("slab", "grp"), None, None),
        P(),
        P(),
    )
    out_specs = (P("slab", "grp", None), P(None, "slab", "grp", None))
    return jax.shard_map(local, mesh=mesh, in_specs=in_specs, out_specs=out_specs, check_vma=False)
```

profile of v0, /device:TPU:1, one launch (start us, length us, event | category | flops | bytes accessed | tf_op | source)
XLA Modules:
  0.0 431.8 jit_solution(10899775711630488973)
XLA Ops:
  7.2 3.9 copy.50
  13.4 5.2 %all-to-all-start = ((bf16[8,8,8]{2,1,0:T(8,128)(2,1)}), bf16[8,8,8]{2,1,0:T(8,128)(2,1)S(1)}, u32[]{:S(2)}, u32[]{:S(2)}) async-start(bf16[8,8,8]{2,1,0:T(8,128)(2,1)} %convolution_convert_fusion.2), calls=%async_computation | async-start | bytes 32768 | tf_op jit(solution)/shard_map/all_to_all | solution.py:67
  18.7 17.0 %while.16 = (s32[]{:T(128)}, s32[1024]{0:T(1024)}, s32[8,1]{0,1:T(1,128)S(1)}, s32[8,32]{1,0:T(8,128)S(1)}, s32[]{:T(128)}, /*index=5*/s32[]{:T(128)}) while((s32[]{:T(128)}, s32[1024]{0:T(1024)}, s32[8,1]{0,1:T(1,128)S(1)}, s32[8,32]{1,0:T(8,128)S(1)}, s32[]{:T(128)}, /*index=5*/s32[]{:T(128)}) %tuple.51), condition=%wide.while_cond.1, body=%wide.while_body.1.sunk | while | flops 2 | bytes 609 | solution.py:32
  35.7 16.0 %while.15 = (s32[]{:T(128)}, s32[1024,2]{0,1:T(2,128)}, s32[8,2]{0,1:T(2,128)S(1)}, s32[8,32,2]{1,2,0:T(2,128)S(1)}, s32[]{:T(128)}) while((s32[]{:T(128)}, s32[1024,2]{0,1:T(2,128)}, s32[8,2]{0,1:T(2,128)S(1)}, s32[8,32,2]{1,2,0:T(2,128)S(1)}, s32[]{:T(128)}) %tuple.54), condition=%wide.while_cond, body=%wide.while_body.sunk | while | flops 2 | bytes 1385 | solution.py:27
  52.9 4.2 all-to-all-start.1
  57.2 4.0 all-to-all-done.1
  62.7 26.6 %reduce-scatter.2.cloned.1.call-done = bf16[128,8,128]{2,0,1:T(8,128)(2,1)} async-done(((bf16[512,8,128]{2,0,1:T(8,128)(2,1)}), bf16[128,8,128]{2,0,1:T(8,128)(2,1)}) %reduce-scatter.2.cloned.1.call-update) | async-done | bytes 262160 | tf_op jit(solution)/shard_map/reduce_scatter | solution.py:77
  89.3 2.0 pad_convert_fusion
  91.3 332.7 %while.14 = (s32[]{:T(128)}, f32[8,128,256]{2,1,0:T(8,128)S(1)}, f32[3,8,128,256]{3,2,1,0:T(8,128)}, f32[8,128,256]{2,1,0:T(8,128)}, f32[8,128,256]{2,1,0:T(8,128)}, /*index=5*/f32[8,128,256]{2,1,0:T(8,128)}, s32[]{:T(128)}) while((s32[]{:T(128)}, f32[8,128,256]{2,1,0:T(8,128)S(1)}, f32[3,8,128,256]{3,2,1,0:T(8,128)}, ...), condition=%wide.region_7.8_spmd, body=%wide.region_6.7_spmd.sunk | while | flops 7864322 | bytes 46203172 | solution.py:106
  91.3 2.8 collective-permute-start
  98.6 3.3 fusion.38
  101.9 2.3 collective-permute-start.3
  104.2 3.5 collective-permute-start.2
  107.8 2.0 pad_maximum_fusion.2
  117.8 3.3 fusion.38
  121.1 3.4 collective-permute-start.3
  124.4 5.1 %collective-permute-start.2 = (f32[1,128,256]{2,1,0:T(8,128)S(1)}, f32[1,128,256]{2,1,0:T(8,128)S(1)}, u32[]{:S(2)}, u32[]{:S(2)}) collective-permute-start(f32[1,128,256]{2,1,0:T(8,128)S(1)} %slice.81), channel_id=1, source_target_pairs={{0,4},{4,8},{8,12},{12,16},{16,20},{20,24},{24,28},{1,5},{5,9},{9,... | collective-permute-start | bytes 393224 | tf_op jit(solution)/shard_map/while/body/eval_jaxpr/ppermute | solution.py:18
  129.6 2.0 pad_maximum_fusion.2
  132.8 1.9 collective-permute-start
  139.6 3.3 fusion.38
  142.9 2.0 collective-permute-start.3
  144.9 4.8 %collective-permute-start.2 = (f32[1,128,256]{2,1,0:T(8,128)S(1)}, f32[1,128,256]{2,1,0:T(8,128)S(1)}, u32[]{:S(2)}, u32[]{:S(2)}) collective-permute-start(f32[1,128,256]{2,1,0:T(8,128)S(1)} %slice.81), channel_id=1, source_target_pairs={{0,4},{4,8},{8,12},{12,16},{16,20},{20,24},{24,28},{1,5},{5,9},{9,... | collective-permute-start | bytes 393224 | tf_op jit(solution)/shard_map/while/body/eval_jaxpr/ppermute | solution.py:18
  149.7 2.0 pad_maximum_fusion.2
  159.7 3.3 fusion.38
  163.0 2.0 collective-permute-start.3
  165.0 4.8 %collective-permute-start.2 = (f32[1,128,256]{2,1,0:T(8,128)S(1)}, f32[1,128,256]{2,1,0:T(8,128)S(1)}, u32[]{:S(2)}, u32[]{:S(2)}) collective-permute-start(f32[1,128,256]{2,1,0:T(8,128)S(1)} %slice.81), channel_id=1, source_target_pairs={{0,4},{4,8},{8,12},{12,16},{16,20},{20,24},{24,28},{1,5},{5,9},{9,... | collective-permute-start | bytes 393224 | tf_op jit(solution)/shard_map/while/body/eval_jaxpr/ppermute | solution.py:18
  169.8 2.0 pad_maximum_fusion.2
  179.7 3.3 fusion.38
  183.0 2.0 collective-permute-start.3
  185.1 4.8 %collective-permute-start.2 = (f32[1,128,256]{2,1,0:T(8,128)S(1)}, f32[1,128,256]{2,1,0:T(8,128)S(1)}, u32[]{:S(2)}, u32[]{:S(2)}) collective-permute-start(f32[1,128,256]{2,1,0:T(8,128)S(1)} %slice.81), channel_id=1, source_target_pairs={{0,4},{4,8},{8,12},{12,16},{16,20},{20,24},{24,28},{1,5},{5,9},{9,... | collective-permute-start | bytes 393224 | tf_op jit(solution)/shard_map/while/body/eval_jaxpr/ppermute | solution.py:18
  189.9 2.0 pad_maximum_fusion.2
  200.5 3.3 fusion.38
  205.8 5.1 %collective-permute-start.2 = (f32[1,128,256]{2,1,0:T(8,128)S(1)}, f32[1,128,256]{2,1,0:T(8,128)S(1)}, u32[]{:S(2)}, u32[]{:S(2)}) collective-permute-start(f32[1,128,256]{2,1,0:T(8,128)S(1)} %slice.81), channel_id=1, source_target_pairs={{0,4},{4,8},{8,12},{12,16},{16,20},{20,24},{24,28},{1,5},{5,9},{9,... | collective-permute-start | bytes 393224 | tf_op jit(solution)/shard_map/while/body/eval_jaxpr/ppermute | solution.py:18
  210.9 2.0 pad_maximum_fusion.2
  221.5 3.3 fusion.38
  226.8 5.1 %collective-permute-start.2 = (f32[1,128,256]{2,1,0:T(8,128)S(1)}, f32[1,128,256]{2,1,0:T(8,128)S(1)}, u32[]{:S(2)}, u32[]{:S(2)}) collective-permute-start(f32[1,128,256]{2,1,0:T(8,128)S(1)} %slice.81), channel_id=1, source_target_pairs={{0,4},{4,8},{8,12},{12,16},{16,20},{20,24},{24,28},{1,5},{5,9},{9,... | collective-permute-start | bytes 393224 | tf_op jit(solution)/shard_map/while/body/eval_jaxpr/ppermute | solution.py:18
  231.9 2.0 pad_maximum_fusion.2
  242.5 3.3 fusion.38
  247.7 5.1 %collective-permute-start.2 = (f32[1,128,256]{2,1,0:T(8,128)S(1)}, f32[1,128,256]{2,1,0:T(8,128)S(1)}, u32[]{:S(2)}, u32[]{:S(2)}) collective-permute-start(f32[1,128,256]{2,1,0:T(8,128)S(1)} %slice.81), channel_id=1, source_target_pairs={{0,4},{4,8},{8,12},{12,16},{16,20},{20,24},{24,28},{1,5},{5,9},{9,... | collective-permute-start | bytes 393224 | tf_op jit(solution)/shard_map/while/body/eval_jaxpr/ppermute | solution.py:18
  252.9 2.0 pad_maximum_fusion.2
  263.5 3.3 fusion.38
  268.7 5.1 %collective-permute-start.2 = (f32[1,128,256]{2,1,0:T(8,128)S(1)}, f32[1,128,256]{2,1,0:T(8,128)S(1)}, u32[]{:S(2)}, u32[]{:S(2)}) collective-permute-start(f32[1,128,256]{2,1,0:T(8,128)S(1)} %slice.81), channel_id=1, source_target_pairs={{0,4},{4,8},{8,12},{12,16},{16,20},{20,24},{24,28},{1,5},{5,9},{9,... | collective-permute-start | bytes 393224 | tf_op jit(solution)/shard_map/while/body/eval_jaxpr/ppermute | solution.py:18
  273.9 2.0 pad_maximum_fusion.2
  284.5 3.3 fusion.38
  289.7 5.1 %collective-permute-start.2 = (f32[1,128,256]{2,1,0:T(8,128)S(1)}, f32[1,128,256]{2,1,0:T(8,128)S(1)}, u32[]{:S(2)}, u32[]{:S(2)}) collective-permute-start(f32[1,128,256]{2,1,0:T(8,128)S(1)} %slice.81), channel_id=1, source_target_pairs={{0,4},{4,8},{8,12},{12,16},{16,20},{20,24},{24,28},{1,5},{5,9},{9,... | collective-permute-start | bytes 393224 | tf_op jit(solution)/shard_map/while/body/eval_jaxpr/ppermute | solution.py:18
  294.9 2.0 pad_maximum_fusion.2
  305.4 3.3 fusion.38
  310.7 5.1 %collective-permute-start.2 = (f32[1,128,256]{2,1,0:T(8,128)S(1)}, f32[1,128,256]{2,1,0:T(8,128)S(1)}, u32[]{:S(2)}, u32[]{:S(2)}) collective-permute-start(f32[1,128,256]{2,1,0:T(8,128)S(1)} %slice.81), channel_id=1, source_target_pairs={{0,4},{4,8},{8,12},{12,16},{16,20},{20,24},{24,28},{1,5},{5,9},{9,... | collective-permute-start | bytes 393224 | tf_op jit(solution)/shard_map/while/body/eval_jaxpr/ppermute | solution.py:18
  315.9 2.0 pad_maximum_fusion.2
  326.4 3.3 fusion.38
  331.7 5.1 %collective-permute-start.2 = (f32[1,128,256]{2,1,0:T(8,128)S(1)}, f32[1,128,256]{2,1,0:T(8,128)S(1)}, u32[]{:S(2)}, u32[]{:S(2)}) collective-permute-start(f32[1,128,256]{2,1,0:T(8,128)S(1)} %slice.81), channel_id=1, source_target_pairs={{0,4},{4,8},{8,12},{12,16},{16,20},{20,24},{24,28},{1,5},{5,9},{9,... | collective-permute-start | bytes 393224 | tf_op jit(solution)/shard_map/while/body/eval_jaxpr/ppermute | solution.py:18
  336.8 2.0 pad_maximum_fusion.2
  347.4 3.3 fusion.38
  352.7 5.1 %collective-permute-start.2 = (f32[1,128,256]{2,1,0:T(8,128)S(1)}, f32[1,128,256]{2,1,0:T(8,128)S(1)}, u32[]{:S(2)}, u32[]{:S(2)}) collective-permute-start(f32[1,128,256]{2,1,0:T(8,128)S(1)} %slice.81), channel_id=1, source_target_pairs={{0,4},{4,8},{8,12},{12,16},{16,20},{20,24},{24,28},{1,5},{5,9},{9,... | collective-permute-start | bytes 393224 | tf_op jit(solution)/shard_map/while/body/eval_jaxpr/ppermute | solution.py:18
  357.8 2.0 pad_maximum_fusion.2
  368.4 3.3 fusion.38
  373.7 5.1 %collective-permute-start.2 = (f32[1,128,256]{2,1,0:T(8,128)S(1)}, f32[1,128,256]{2,1,0:T(8,128)S(1)}, u32[]{:S(2)}, u32[]{:S(2)}) collective-permute-start(f32[1,128,256]{2,1,0:T(8,128)S(1)} %slice.81), channel_id=1, source_target_pairs={{0,4},{4,8},{8,12},{12,16},{16,20},{20,24},{24,28},{1,5},{5,9},{9,... | collective-permute-start | bytes 393224 | tf_op jit(solution)/shard_map/while/body/eval_jaxpr/ppermute | solution.py:18
  378.8 2.0 pad_maximum_fusion.2
  389.4 3.3 fusion.38
  394.6 5.1 %collective-permute-start.2 = (f32[1,128,256]{2,1,0:T(8,128)S(1)}, f32[1,128,256]{2,1,0:T(8,128)S(1)}, u32[]{:S(2)}, u32[]{:S(2)}) collective-permute-start(f32[1,128,256]{2,1,0:T(8,128)S(1)} %slice.81), channel_id=1, source_target_pairs={{0,4},{4,8},{8,12},{12,16},{16,20},{20,24},{24,28},{1,5},{5,9},{9,... | collective-permute-start | bytes 393224 | tf_op jit(solution)/shard_map/while/body/eval_jaxpr/ppermute | solution.py:18
  399.8 2.0 pad_maximum_fusion.2
  410.4 3.3 fusion.38
  415.6 5.1 %collective-permute-start.2 = (f32[1,128,256]{2,1,0:T(8,128)S(1)}, f32[1,128,256]{2,1,0:T(8,128)S(1)}, u32[]{:S(2)}, u32[]{:S(2)}) collective-permute-start(f32[1,128,256]{2,1,0:T(8,128)S(1)} %slice.81), channel_id=1, source_target_pairs={{0,4},{4,8},{8,12},{12,16},{16,20},{20,24},{24,28},{1,5},{5,9},{9,... | collective-permute-start | bytes 393224 | tf_op jit(solution)/shard_map/while/body/eval_jaxpr/ppermute | solution.py:18
  420.8 2.0 pad_maximum_fusion.2
  (399 shorter events, 189.5 us)
Async XLA Ops:
  13.4 39.5 %all-to-all-start = ((bf16[8,8,8]{2,1,0:T(8,128)(2,1)}), bf16[8,8,8]{2,1,0:T(8,128)(2,1)S(1)}, u32[]{:S(2)}, u32[]{:S(2)}) async-start(bf16[8,8,8]{2,1,0:T(8,128)(2,1)} %convolution_convert_fusion.2), calls=%async_computation | async-start | bytes 32768 | tf_op jit(solution)/shard_map/all_to_all | solution.py:67
  52.9 8.2 %all-to-all-start.1 = ((bf16[8,8,128]{2,1,0:T(8,128)(2,1)}), bf16[8,8,128]{2,1,0:T(8,128)(2,1)S(1)}, u32[]{:S(2)}, u32[]{:S(2)}) async-start(bf16[8,8,128]{2,1,0:T(8,128)(2,1)} %convolution_convert_fusion.1), calls=%async_computation.1 | async-start | bytes 32768 | tf_op jit(solution)/shard_map/all_to_all | solution.py:66
  57.2 32.1 %reduce-scatter.2.cloned.1.call-start = ((), (), s32[]{:S(2)}) async-start(), calls=%async_computation.3 | async-start | bytes 1310720 | tf_op jit(solution)/shard_map/reduce_scatter | solution.py:77
  91.3 7.3 %collective-permute-start = (f32[1,128,256]{2,1,0:T(8,128)S(1)}, f32[1,128,256]{2,1,0:T(8,128)S(1)}, u32[]{:S(2)}, u32[]{:S(2)}) collective-permute-start(f32[1,128,256]{2,1,0:T(8,128)S(1)} %slice.75), channel_id=1, source_target_pairs={{4,0},{8,4},{12,8},{16,12},{20,16},{24,20},{28,24},{5,1},{9,5},{13... | collective-permute-start | bytes 393224 | tf_op jit(solution)/shard_map/while/body/eval_jaxpr/ppermute | solution.py:18
  94.1 4.5 %collective-permute-start.1 = (f32[8,1,256]{2,1,0:T(1,128)S(1)}, f32[8,1,256]{2,1,0:T(1,128)S(1)}, u32[]{:S(2)}, u32[]{:S(2)}) collective-permute-start(f32[8,1,256]{2,1,0:T(1,128)S(1)} %slice.78), channel_id=1, source_target_pairs={{1,0},{2,1},{3,2},{5,4},{6,5},{7,6},{9,8},{10,9},{11,10},{13,12},{... | collective-permute-start | bytes 24584 | tf_op jit(solution)/shard_map/while/body/eval_jaxpr/ppermute | solution.py:18
  101.9 7.9 %collective-permute-start.3 = (f32[8,1,256]{2,1,0:T(1,128)S(1)}, f32[8,1,256]{2,1,0:T(1,128)S(1)}, u32[]{:S(2)}, u32[]{:S(2)}) collective-permute-start(f32[8,1,256]{2,1,0:T(1,128)S(1)} %slice.82), channel_id=1, source_target_pairs={{0,1},{1,2},{2,3},{4,5},{5,6},{6,7},{8,9},{9,10},{10,11},{12,13},{... | collective-permute-start | bytes 24584 | tf_op jit(solution)/shard_map/while/body/eval_jaxpr/ppermute | solution.py:18
  104.2 5.7 %collective-permute-start.2 = (f32[1,128,256]{2,1,0:T(8,128)S(1)}, f32[1,128,256]{2,1,0:T(8,128)S(1)}, u32[]{:S(2)}, u32[]{:S(2)}) collective-permute-start(f32[1,128,256]{2,1,0:T(8,128)S(1)} %slice.81), channel_id=1, source_target_pairs={{0,4},{4,8},{8,12},{12,16},{16,20},{20,24},{24,28},{1,5},{5,9},{9,... | collective-permute-start | bytes 393224 | tf_op jit(solution)/shard_map/while/body/eval_jaxpr/ppermute | solution.py:18
  111.0 6.7 %collective-permute-start = (f32[1,128,256]{2,1,0:T(8,128)S(1)}, f32[1,128,256]{2,1,0:T(8,128)S(1)}, u32[]{:S(2)}, u32[]{:S(2)}) collective-permute-start(f32[1,128,256]{2,1,0:T(8,128)S(1)} %slice.75), channel_id=1, source_target_pairs={{4,0},{8,4},{12,8},{16,12},{20,16},{24,20},{28,24},{5,1},{9,5},{13... | collective-permute-start | bytes 393224 | tf_op jit(solution)/shard_map/while/body/eval_jaxpr/ppermute | solution.py:18
  113.0 4.4 %collective-permute-start.1 = (f32[8,1,256]{2,1,0:T(1,128)S(1)}, f32[8,1,256]{2,1,0:T(1,128)S(1)}, u32[]{:S(2)}, u32[]{:S(2)}) collective-permute-start(f32[8,1,256]{2,1,0:T(1,128)S(1)} %slice.78), channel_id=1, source_target_pairs={{1,0},{2,1},{3,2},{5,4},{6,5},{7,6},{9,8},{10,9},{11,10},{13,12},{... | collective-permute-start | bytes 24584 | tf_op jit(solution)/shard_map/while/body/eval_jaxpr/ppermute | solution.py:18
  121.1 10.6 %collective-permute-start.3 = (f32[8,1,256]{2,1,0:T(1,128)S(1)}, f32[8,1,256]{2,1,0:T(1,128)S(1)}, u32[]{:S(2)}, u32[]{:S(2)}) collective-permute-start(f32[8,1,256]{2,1,0:T(1,128)S(1)} %slice.82), channel_id=1, source_target_pairs={{0,1},{1,2},{2,3},{4,5},{5,6},{6,7},{8,9},{9,10},{10,11},{12,13},{... | collective-permute-start | bytes 24584 | tf_op jit(solution)/shard_map/while/body/eval_jaxpr/ppermute | solution.py:18
  124.4 7.2 %collective-permute-start.2 = (f32[1,128,256]{2,1,0:T(8,128)S(1)}, f32[1,128,256]{2,1,0:T(8,128)S(1)}, u32[]{:S(2)}, u32[]{:S(2)}) collective-permute-start(f32[1,128,256]{2,1,0:T(8,128)S(1)} %slice.81), channel_id=1, source_target_pairs={{0,4},{4,8},{8,12},{12,16},{16,20},{20,24},{24,28},{1,5},{5,9},{9,... | collective-permute-start | bytes 393224 | tf_op jit(solution)/shard_map/while/body/eval_jaxpr/ppermute | solution.py:18
  132.8 6.7 %collective-permute-start = (f32[1,128,256]{2,1,0:T(8,128)S(1)}, f32[1,128,256]{2,1,0:T(8,128)S(1)}, u32[]{:S(2)}, u32[]{:S(2)}) collective-permute-start(f32[1,128,256]{2,1,0:T(8,128)S(1)} %slice.75), channel_id=1, source_target_pairs={{4,0},{8,4},{12,8},{16,12},{20,16},{24,20},{28,24},{5,1},{9,5},{13... | collective-permute-start | bytes 393224 | tf_op jit(solution)/shard_map/while/body/eval_jaxpr/ppermute | solution.py:18
  134.8 4.4 %collective-permute-start.1 = (f32[8,1,256]{2,1,0:T(1,128)S(1)}, f32[8,1,256]{2,1,0:T(1,128)S(1)}, u32[]{:S(2)}, u32[]{:S(2)}) collective-permute-start(f32[8,1,256]{2,1,0:T(1,128)S(1)} %slice.78), channel_id=1, source_target_pairs={{1,0},{2,1},{3,2},{5,4},{6,5},{7,6},{9,8},{10,9},{11,10},{13,12},{... | collective-permute-start | bytes 24584 | tf_op jit(solution)/shard_map/while/body/eval_jaxpr/ppermute | solution.py:18
  142.9 8.9 %collective-permute-start.3 = (f32[8,1,256]{2,1,0:T(1,128)S(1)}, f32[8,1,256]{2,1,0:T(1,128)S(1)}, u32[]{:S(2)}, u32[]{:S(2)}) collective-permute-start(f32[8,1,256]{2,1,0:T(1,128)S(1)} %slice.82), channel_id=1, source_target_pairs={{0,1},{1,2},{2,3},{4,5},{5,6},{6,7},{8,9},{9,10},{10,11},{12,13},{... | collective-permute-start | bytes 24584 | tf_op jit(solution)/shard_map/while/body/eval_jaxpr/ppermute | solution.py:18
  144.9 6.9 %collective-permute-start.2 = (f32[1,128,256]{2,1,0:T(8,128)S(1)}, f32[1,128,256]{2,1,0:T(8,128)S(1)}, u32[]{:S(2)}, u32[]{:S(2)}) collective-permute-start(f32[1,128,256]{2,1,0:T(8,128)S(1)} %slice.81), channel_id=1, source_target_pairs={{0,4},{4,8},{8,12},{12,16},{16,20},{20,24},{24,28},{1,5},{5,9},{9,... | collective-permute-start | bytes 393224 | tf_op jit(solution)/shard_map/while/body/eval_jaxpr/ppermute | solution.py:18
  152.9 6.7 %collective-permute-start = (f32[1,128,256]{2,1,0:T(8,128)S(1)}, f32[1,128,256]{2,1,0:T(8,128)S(1)}, u32[]{:S(2)}, u32[]{:S(2)}) collective-permute-start(f32[1,128,256]{2,1,0:T(8,128)S(1)} %slice.75), channel_id=1, source_target_pairs={{4,0},{8,4},{12,8},{16,12},{20,16},{24,20},{28,24},{5,1},{9,5},{13... | collective-permute-start | bytes 393224 | tf_op jit(solution)/shard_map/while/body/eval_jaxpr/ppermute | solution.py:18
  154.9 4.4 %collective-permute-start.1 = (f32[8,1,256]{2,1,0:T(1,128)S(1)}, f32[8,1,256]{2,1,0:T(1,128)S(1)}, u32[]{:S(2)}, u32[]{:S(2)}) collective-permute-start(f32[8,1,256]{2,1,0:T(1,128)S(1)} %slice.78), channel_id=1, source_target_pairs={{1,0},{2,1},{3,2},{5,4},{6,5},{7,6},{9,8},{10,9},{11,10},{13,12},{... | collective-permute-start | bytes 24584 | tf_op jit(solution)/shard_map/while/body/eval_jaxpr/ppermute | solution.py:18
  163.0 8.9 %collective-permute-start.3 = (f32[8,1,256]{2,1,0:T(1,128)S(1)}, f32[8,1,256]{2,1,0:T(1,128)S(1)}, u32[]{:S(2)}, u32[]{:S(2)}) collective-permute-start(f32[8,1,256]{2,1,0:T(1,128)S(1)} %slice.82), channel_id=1, source_target_pairs={{0,1},{1,2},{2,3},{4,5},{5,6},{6,7},{8,9},{9,10},{10,11},{12,13},{... | collective-permute-start | bytes 24584 | tf_op jit(solution)/shard_map/while/body/eval_jaxpr/ppermute | solution.py:18
  165.0 6.9 %collective-permute-start.2 = (f32[1,128,256]{2,1,0:T(8,128)S(1)}, f32[1,128,256]{2,1,0:T(8,128)S(1)}, u32[]{:S(2)}, u32[]{:S(2)}) collective-permute-start(f32[1,128,256]{2,1,0:T(8,128)S(1)} %slice.81), channel_id=1, source_target_pairs={{0,4},{4,8},{8,12},{12,16},{16,20},{20,24},{24,28},{1,5},{5,9},{9,... | collective-permute-start | bytes 393224 | tf_op jit(solution)/shard_map/while/body/eval_jaxpr/ppermute | solution.py:18
  173.0 6.7 %collective-permute-start = (f32[1,128,256]{2,1,0:T(8,128)S(1)}, f32[1,128,256]{2,1,0:T(8,128)S(1)}, u32[]{:S(2)}, u32[]{:S(2)}) collective-permute-start(f32[1,128,256]{2,1,0:T(8,128)S(1)} %slice.75), channel_id=1, source_target_pairs={{4,0},{8,4},{12,8},{16,12},{20,16},{24,20},{28,24},{5,1},{9,5},{13... | collective-permute-start | bytes 393224 | tf_op jit(solution)/shard_map/while/body/eval_jaxpr/ppermute | solution.py:18
  175.0 4.4 %collective-permute-start.1 = (f32[8,1,256]{2,1,0:T(1,128)S(1)}, f32[8,1,256]{2,1,0:T(1,128)S(1)}, u32[]{:S(2)}, u32[]{:S(2)}) collective-permute-start(f32[8,1,256]{2,1,0:T(1,128)S(1)} %slice.78), channel_id=1, source_target_pairs={{1,0},{2,1},{3,2},{5,4},{6,5},{7,6},{9,8},{10,9},{11,10},{13,12},{... | collective-permute-start | bytes 24584 | tf_op jit(solution)/shard_map/while/body/eval_jaxpr/ppermute | solution.py:18
  183.0 9.0 %collective-permute-start.3 = (f32[8,1,256]{2,1,0:T(1,128)S(1)}, f32[8,1,256]{2,1,0:T(1,128)S(1)}, u32[]{:S(2)}, u32[]{:S(2)}) collective-permute-start(f32[8,1,256]{2,1,0:T(1,128)S(1)} %slice.82), channel_id=1, source_target_pairs={{0,1},{1,2},{2,3},{4,5},{5,6},{6,7},{8,9},{9,10},{10,11},{12,13},{... | collective-permute-start | bytes 24584 | tf_op jit(solution)/shard_map/while/body/eval_jaxpr/ppermute | solution.py:18
  185.1 7.0 %collective-permute-start.2 = (f32[1,128,256]{2,1,0:T(8,128)S(1)}, f32[1,128,256]{2,1,0:T(8,128)S(1)}, u32[]{:S(2)}, u32[]{:S(2)}) collective-permute-start(f32[1,128,256]{2,1,0:T(8,128)S(1)} %slice.81), channel_id=1, source_target_pairs={{0,4},{4,8},{8,12},{12,16},{16,20},{20,24},{24,28},{1,5},{5,9},{9,... | collective-permute-start | bytes 393224 | tf_op jit(solution)/shard_map/while/body/eval_jaxpr/ppermute | solution.py:18
  193.2 7.3 %collective-permute-start = (f32[1,128,256]{2,1,0:T(8,128)S(1)}, f32[1,128,256]{2,1,0:T(8,128)S(1)}, u32[]{:S(2)}, u32[]{:S(2)}) collective-permute-start(f32[1,128,256]{2,1,0:T(8,128)S(1)} %slice.75), channel_id=1, source_target_pairs={{4,0},{8,4},{12,8},{16,12},{20,16},{24,20},{28,24},{5,1},{9,5},{13... | collective-permute-start | bytes 393224 | tf_op jit(solution)/shard_map/while/body/eval_jaxpr/ppermute | solution.py:18
  195.1 4.4 %collective-permute-start.1 = (f32[8,1,256]{2,1,0:T(1,128)S(1)}, f32[8,1,256]{2,1,0:T(1,128)S(1)}, u32[]{:S(2)}, u32[]{:S(2)}) collective-permute-start(f32[8,1,256]{2,1,0:T(1,128)S(1)} %slice.78), channel_id=1, source_target_pairs={{1,0},{2,1},{3,2},{5,4},{6,5},{7,6},{9,8},{10,9},{11,10},{13,12},{... | collective-permute-start | bytes 24584 | tf_op jit(solution)/shard_map/while/body/eval_jaxpr/ppermute | solution.py:18
  203.8 9.2 %collective-permute-start.3 = (f32[8,1,256]{2,1,0:T(1,128)S(1)}, f32[8,1,256]{2,1,0:T(1,128)S(1)}, u32[]{:S(2)}, u32[]{:S(2)}) collective-permute-start(f32[8,1,256]{2,1,0:T(1,128)S(1)} %slice.82), channel_id=1, source_target_pairs={{0,1},{1,2},{2,3},{4,5},{5,6},{6,7},{8,9},{9,10},{10,11},{12,13},{... | collective-permute-start | bytes 24584 | tf_op jit(solution)/shard_map/while/body/eval_jaxpr/ppermute | solution.py:18
  205.8 7.2 %collective-permute-start.2 = (f32[1,128,256]{2,1,0:T(8,128)S(1)}, f32[1,128,256]{2,1,0:T(8,128)S(1)}, u32[]{:S(2)}, u32[]{:S(2)}) collective-permute-start(f32[1,128,256]{2,1,0:T(8,128)S(1)} %slice.81), channel_id=1, source_target_pairs={{0,4},{4,8},{8,12},{12,16},{16,20},{20,24},{24,28},{1,5},{5,9},{9,... | collective-permute-start | bytes 393224 | tf_op jit(solution)/shard_map/while/body/eval_jaxpr/ppermute | solution.py:18
  214.2 7.3 %collective-permute-start = (f32[1,128,256]{2,1,0:T(8,128)S(1)}, f32[1,128,256]{2,1,0:T(8,128)S(1)}, u32[]{:S(2)}, u32[]{:S(2)}) collective-permute-start(f32[1,128,256]{2,1,0:T(8,128)S(1)} %slice.75), channel_id=1, source_target_pairs={{4,0},{8,4},{12,8},{16,12},{20,16},{24,20},{28,24},{5,1},{9,5},{13... | collective-permute-start | bytes 393224 | tf_op jit(solution)/shard_map/while/body/eval_jaxpr/ppermute | solution.py:18
  216.1 4.4 %collective-permute-start.1 = (f32[8,1,256]{2,1,0:T(1,128)S(1)}, f32[8,1,256]{2,1,0:T(1,128)S(1)}, u32[]{:S(2)}, u32[]{:S(2)}) collective-permute-start(f32[8,1,256]{2,1,0:T(1,128)S(1)} %slice.78), channel_id=1, source_target_pairs={{1,0},{2,1},{3,2},{5,4},{6,5},{7,6},{9,8},{10,9},{11,10},{13,12},{... | collective-permute-start | bytes 24584 | tf_op jit(solution)/shard_map/while/body/eval_jaxpr/ppermute | solution.py:18
  224.8 9.2 %collective-permute-start.3 = (f32[8,1,256]{2,1,0:T(1,128)S(1)}, f32[8,1,256]{2,1,0:T(1,128)S(1)}, u32[]{:S(2)}, u32[]{:S(2)}) collective-permute-start(f32[8,1,256]{2,1,0:T(1,128)S(1)} %slice.82), channel_id=1, source_target_pairs={{0,1},{1,2},{2,3},{4,5},{5,6},{6,7},{8,9},{9,10},{10,11},{12,13},{... | collective-permute-start | bytes 24584 | tf_op jit(solution)/shard_map/while/body/eval_jaxpr/ppermute | solution.py:18
  226.8 7.2 %collective-permute-start.2 = (f32[1,128,256]{2,1,0:T(8,128)S(1)}, f32[1,128,256]{2,1,0:T(8,128)S(1)}, u32[]{:S(2)}, u32[]{:S(2)}) collective-permute-start(f32[1,128,256]{2,1,0:T(8,128)S(1)} %slice.81), channel_id=1, source_target_pairs={{0,4},{4,8},{8,12},{12,16},{16,20},{20,24},{24,28},{1,5},{5,9},{9,... | collective-permute-start | bytes 393224 | tf_op jit(solution)/shard_map/while/body/eval_jaxpr/ppermute | solution.py:18
  235.2 7.3 %collective-permute-start = (f32[1,128,256]{2,1,0:T(8,128)S(1)}, f32[1,128,256]{2,1,0:T(8,128)S(1)}, u32[]{:S(2)}, u32[]{:S(2)}) collective-permute-start(f32[1,128,256]{2,1,0:T(8,128)S(1)} %slice.75), channel_id=1, source_target_pairs={{4,0},{8,4},{12,8},{16,12},{20,16},{24,20},{28,24},{5,1},{9,5},{13... | collective-permute-start | bytes 393224 | tf_op jit(solution)/shard_map/while/body/eval_jaxpr/ppermute | solution.py:18
  237.1 4.4 %collective-permute-start.1 = (f32[8,1,256]{2,1,0:T(1,128)S(1)}, f32[8,1,256]{2,1,0:T(1,128)S(1)}, u32[]{:S(2)}, u32[]{:S(2)}) collective-permute-start(f32[8,1,256]{2,1,0:T(1,128)S(1)} %slice.78), channel_id=1, source_target_pairs={{1,0},{2,1},{3,2},{5,4},{6,5},{7,6},{9,8},{10,9},{11,10},{13,12},{... | collective-permute-start | bytes 24584 | tf_op jit(solution)/shard_map/while/body/eval_jaxpr/ppermute | solution.py:18
  245.8 9.2 %collective-permute-start.3 = (f32[8,1,256]{2,1,0:T(1,128)S(1)}, f32[8,1,256]{2,1,0:T(1,128)S(1)}, u32[]{:S(2)}, u32[]{:S(2)}) collective-permute-start(f32[8,1,256]{2,1,0:T(1,128)S(1)} %slice.82), channel_id=1, source_target_pairs={{0,1},{1,2},{2,3},{4,5},{5,6},{6,7},{8,9},{9,10},{10,11},{12,13},{... | collective-permute-start | bytes 24584 | tf_op jit(solution)/shard_map/while/body/eval_jaxpr/ppermute | solution.py:18
  247.7 7.2 %collective-permute-start.2 = (f32[1,128,256]{2,1,0:T(8,128)S(1)}, f32[1,128,256]{2,1,0:T(8,128)S(1)}, u32[]{:S(2)}, u32[]{:S(2)}) collective-permute-start(f32[1,128,256]{2,1,0:T(8,128)S(1)} %slice.81), channel_id=1, source_target_pairs={{0,4},{4,8},{8,12},{12,16},{16,20},{20,24},{24,28},{1,5},{5,9},{9,... | collective-permute-start | bytes 393224 | tf_op jit(solution)/shard_map/while/body/eval_jaxpr/ppermute | solution.py:18
  256.1 7.3 %collective-permute-start = (f32[1,128,256]{2,1,0:T(8,128)S(1)}, f32[1,128,256]{2,1,0:T(8,128)S(1)}, u32[]{:S(2)}, u32[]{:S(2)}) collective-permute-start(f32[1,128,256]{2,1,0:T(8,128)S(1)} %slice.75), channel_id=1, source_target_pairs={{4,0},{8,4},{12,8},{16,12},{20,16},{24,20},{28,24},{5,1},{9,5},{13... | collective-permute-start | bytes 393224 | tf_op jit(solution)/shard_map/while/body/eval_jaxpr/ppermute | solution.py:18
  258.1 4.4 %collective-permute-start.1 = (f32[8,1,256]{2,1,0:T(1,128)S(1)}, f32[8,1,256]{2,1,0:T(1,128)S(1)}, u32[]{:S(2)}, u32[]{:S(2)}) collective-permute-start(f32[8,1,256]{2,1,0:T(1,128)S(1)} %slice.78), channel_id=1, source_target_pairs={{1,0},{2,1},{3,2},{5,4},{6,5},{7,6},{9,8},{10,9},{11,10},{13,12},{... | collective-permute-start | bytes 24584 | tf_op jit(solution)/shard_map/while/body/eval_jaxpr/ppermute | solution.py:18
  266.8 9.2 %collective-permute-start.3 = (f32[8,1,256]{2,1,0:T(1,128)S(1)}, f32[8,1,256]{2,1,0:T(1,128)S(1)}, u32[]{:S(2)}, u32[]{:S(2)}) collective-permute-start(f32[8,1,256]{2,1,0:T(1,128)S(1)} %slice.82), channel_id=1, source_target_pairs={{0,1},{1,2},{2,3},{4,5},{5,6},{6,7},{8,9},{9,10},{10,11},{12,13},{... | collective-permute-start | bytes 24584 | tf_op jit(solution)/shard_map/while/body/eval_jaxpr/ppermute | solution.py:18
  268.7 7.2 %collective-permute-start.2 = (f32[1,128,256]{2,1,0:T(8,128)S(1)}, f32[1,128,256]{2,1,0:T(8,128)S(1)}, u32[]{:S(2)}, u32[]{:S(2)}) collective-permute-start(f32[1,128,256]{2,1,0:T(8,128)S(1)} %slice.81), channel_id=1, source_target_pairs={{0,4},{4,8},{8,12},{12,16},{16,20},{20,24},{24,28},{1,5},{5,9},{9,... | collective-permute-start | bytes 393224 | tf_op jit(solution)/shard_map/while/body/eval_jaxpr/ppermute | solution.py:18
  277.1 7.3 %collective-permute-start = (f32[1,128,256]{2,1,0:T(8,128)S(1)}, f32[1,128,256]{2,1,0:T(8,128)S(1)}, u32[]{:S(2)}, u32[]{:S(2)}) collective-permute-start(f32[1,128,256]{2,1,0:T(8,128)S(1)} %slice.75), channel_id=1, source_target_pairs={{4,0},{8,4},{12,8},{16,12},{20,16},{24,20},{28,24},{5,1},{9,5},{13... | collective-permute-start | bytes 393224 | tf_op jit(solution)/shard_map/while/body/eval_jaxpr/ppermute | solution.py:18
  279.1 4.4 %collective-permute-start.1 = (f32[8,1,256]{2,1,0:T(1,128)S(1)}, f32[8,1,256]{2,1,0:T(1,128)S(1)}, u32[]{:S(2)}, u32[]{:S(2)}) collective-permute-start(f32[8,1,256]{2,1,0:T(1,128)S(1)} %slice.78), channel_id=1, source_target_pairs={{1,0},{2,1},{3,2},{5,4},{6,5},{7,6},{9,8},{10,9},{11,10},{13,12},{... | collective-permute-start | bytes 24584 | tf_op jit(solution)/shard_map/while/body/eval_jaxpr/ppermute | solution.py:18
  287.8 9.2 %collective-permute-start.3 = (f32[8,1,256]{2,1,0:T(1,128)S(1)}, f32[8,1,256]{2,1,0:T(1,128)S(1)}, u32[]{:S(2)}, u32[]{:S(2)}) collective-permute-start(f32[8,1,256]{2,1,0:T(1,128)S(1)} %slice.82), channel_id=1, source_target_pairs={{0,1},{1,2},{2,3},{4,5},{5,6},{6,7},{8,9},{9,10},{10,11},{12,13},{... | collective-permute-start | bytes 24584 | tf_op jit(solution)/shard_map/while/body/eval_jaxpr/ppermute | solution.py:18
  289.7 7.2 %collective-permute-start.2 = (f32[1,128,256]{2,1,0:T(8,128)S(1)}, f32[1,128,256]{2,1,0:T(8,128)S(1)}, u32[]{:S(2)}, u32[]{:S(2)}) collective-permute-start(f32[1,128,256]{2,1,0:T(8,128)S(1)} %slice.81), channel_id=1, source_target_pairs={{0,4},{4,8},{8,12},{12,16},{16,20},{20,24},{24,28},{1,5},{5,9},{9,... | collective-permute-start | bytes 393224 | tf_op jit(solution)/shard_map/while/body/eval_jaxpr/ppermute | solution.py:18
  298.1 7.3 %collective-permute-start = (f32[1,128,256]{2,1,0:T(8,128)S(1)}, f32[1,128,256]{2,1,0:T(8,128)S(1)}, u32[]{:S(2)}, u32[]{:S(2)}) collective-permute-start(f32[1,128,256]{2,1,0:T(8,128)S(1)} %slice.75), channel_id=1, source_target_pairs={{4,0},{8,4},{12,8},{16,12},{20,16},{24,20},{28,24},{5,1},{9,5},{13... | collective-permute-start | bytes 393224 | tf_op jit(solution)/shard_map/while/body/eval_jaxpr/ppermute | solution.py:18
  300.1 4.4 %collective-permute-start.1 = (f32[8,1,256]{2,1,0:T(1,128)S(1)}, f32[8,1,256]{2,1,0:T(1,128)S(1)}, u32[]{:S(2)}, u32[]{:S(2)}) collective-permute-start(f32[8,1,256]{2,1,0:T(1,128)S(1)} %slice.78), channel_id=1, source_target_pairs={{1,0},{2,1},{3,2},{5,4},{6,5},{7,6},{9,8},{10,9},{11,10},{13,12},{... | collective-permute-start | bytes 24584 | tf_op jit(solution)/shard_map/while/body/eval_jaxpr/ppermute | solution.py:18
  308.8 9.2 %collective-permute-start.3 = (f32[8,1,256]{2,1,0:T(1,128)S(1)}, f32[8,1,256]{2,1,0:T(1,128)S(1)}, u32[]{:S(2)}, u32[]{:S(2)}) collective-permute-start(f32[8,1,256]{2,1,0:T(1,128)S(1)} %slice.82), channel_id=1, source_target_pairs={{0,1},{1,2},{2,3},{4,5},{5,6},{6,7},{8,9},{9,10},{10,11},{12,13},{... | collective-permute-start | bytes 24584 | tf_op jit(solution)/shard_map/while/body/eval_jaxpr/ppermute | solution.py:18
  310.7 7.2 %collective-permute-start.2 = (f32[1,128,256]{2,1,0:T(8,128)S(1)}, f32[1,128,256]{2,1,0:T(8,128)S(1)}, u32[]{:S(2)}, u32[]{:S(2)}) collective-permute-start(f32[1,128,256]{2,1,0:T(8,128)S(1)} %slice.81), channel_id=1, source_target_pairs={{0,4},{4,8},{8,12},{12,16},{16,20},{20,24},{24,28},{1,5},{5,9},{9,... | collective-permute-start | bytes 393224 | tf_op jit(solution)/shard_map/while/body/eval_jaxpr/ppermute | solution.py:18
  319.1 7.3 %collective-permute-start = (f32[1,128,256]{2,1,0:T(8,128)S(1)}, f32[1,128,256]{2,1,0:T(8,128)S(1)}, u32[]{:S(2)}, u32[]{:S(2)}) collective-permute-start(f32[1,128,256]{2,1,0:T(8,128)S(1)} %slice.75), channel_id=1, source_target_pairs={{4,0},{8,4},{12,8},{16,12},{20,16},{24,20},{28,24},{5,1},{9,5},{13... | collective-permute-start | bytes 393224 | tf_op jit(solution)/shard_map/while/body/eval_jaxpr/ppermute | solution.py:18
  321.0 4.4 %collective-permute-start.1 = (f32[8,1,256]{2,1,0:T(1,128)S(1)}, f32[8,1,256]{2,1,0:T(1,128)S(1)}, u32[]{:S(2)}, u32[]{:S(2)}) collective-permute-start(f32[8,1,256]{2,1,0:T(1,128)S(1)} %slice.78), channel_id=1, source_target_pairs={{1,0},{2,1},{3,2},{5,4},{6,5},{7,6},{9,8},{10,9},{11,10},{13,12},{... | collective-permute-start | bytes 24584 | tf_op jit(solution)/shard_map/while/body/eval_jaxpr/ppermute | solution.py:18
  329.7 9.2 %collective-permute-start.3 = (f32[8,1,256]{2,1,0:T(1,128)S(1)}, f32[8,1,256]{2,1,0:T(1,128)S(1)}, u32[]{:S(2)}, u32[]{:S(2)}) collective-permute-start(f32[8,1,256]{2,1,0:T(1,128)S(1)} %slice.82), channel_id=1, source_target_pairs={{0,1},{1,2},{2,3},{4,5},{5,6},{6,7},{8,9},{9,10},{10,11},{12,13},{... | collective-permute-start | bytes 24584 | tf_op jit(solution)/shard_map/while/body/eval_jaxpr/ppermute | solution.py:18
  331.7 7.2 %collective-permute-start.2 = (f32[1,128,256]{2,1,0:T(8,128)S(1)}, f32[1,128,256]{2,1,0:T(8,128)S(1)}, u32[]{:S(2)}, u32[]{:S(2)}) collective-permute-start(f32[1,128,256]{2,1,0:T(8,128)S(1)} %slice.81), channel_id=1, source_target_pairs={{0,4},{4,8},{8,12},{12,16},{16,20},{20,24},{24,28},{1,5},{5,9},{9,... | collective-permute-start | bytes 393224 | tf_op jit(solution)/shard_map/while/body/eval_jaxpr/ppermute | solution.py:18
  340.1 7.3 %collective-permute-start = (f32[1,128,256]{2,1,0:T(8,128)S(1)}, f32[1,128,256]{2,1,0:T(8,128)S(1)}, u32[]{:S(2)}, u32[]{:S(2)}) collective-permute-start(f32[1,128,256]{2,1,0:T(8,128)S(1)} %slice.75), channel_id=1, source_target_pairs={{4,0},{8,4},{12,8},{16,12},{20,16},{24,20},{28,24},{5,1},{9,5},{13... | collective-permute-start | bytes 393224 | tf_op jit(solution)/shard_map/while/body/eval_jaxpr/ppermute | solution.py:18
  342.0 4.4 %collective-permute-start.1 = (f32[8,1,256]{2,1,0:T(1,128)S(1)}, f32[8,1,256]{2,1,0:T(1,128)S(1)}, u32[]{:S(2)}, u32[]{:S(2)}) collective-permute-start(f32[8,1,256]{2,1,0:T(1,128)S(1)} %slice.78), channel_id=1, source_target_pairs={{1,0},{2,1},{3,2},{5,4},{6,5},{7,6},{9,8},{10,9},{11,10},{13,12},{... | collective-permute-start | bytes 24584 | tf_op jit(solution)/shard_map/while/body/eval_jaxpr/ppermute | solution.py:18
  350.7 9.2 %collective-permute-start.3 = (f32[8,1,256]{2,1,0:T(1,128)S(1)}, f32[8,1,256]{2,1,0:T(1,128)S(1)}, u32[]{:S(2)}, u32[]{:S(2)}) collective-permute-start(f32[8,1,256]{2,1,0:T(1,128)S(1)} %slice.82), channel_id=1, source_target_pairs={{0,1},{1,2},{2,3},{4,5},{5,6},{6,7},{8,9},{9,10},{10,11},{12,13},{... | collective-permute-start | bytes 24584 | tf_op jit(solution)/shard_map/while/body/eval_jaxpr/ppermute | solution.py:18
  352.7 7.2 %collective-permute-start.2 = (f32[1,128,256]{2,1,0:T(8,128)S(1)}, f32[1,128,256]{2,1,0:T(8,128)S(1)}, u32[]{:S(2)}, u32[]{:S(2)}) collective-permute-start(f32[1,128,256]{2,1,0:T(8,128)S(1)} %slice.81), channel_id=1, source_target_pairs={{0,4},{4,8},{8,12},{12,16},{16,20},{20,24},{24,28},{1,5},{5,9},{9,... | collective-permute-start | bytes 393224 | tf_op jit(solution)/shard_map/while/body/eval_jaxpr/ppermute | solution.py:18
  361.1 7.3 %collective-permute-start = (f32[1,128,256]{2,1,0:T(8,128)S(1)}, f32[1,128,256]{2,1,0:T(8,128)S(1)}, u32[]{:S(2)}, u32[]{:S(2)}) collective-permute-start(f32[1,128,256]{2,1,0:T(8,128)S(1)} %slice.75), channel_id=1, source_target_pairs={{4,0},{8,4},{12,8},{16,12},{20,16},{24,20},{28,24},{5,1},{9,5},{13... | collective-permute-start | bytes 393224 | tf_op jit(solution)/shard_map/while/body/eval_jaxpr/ppermute | solution.py:18
  371.7 9.2 %collective-permute-start.3 = (f32[8,1,256]{2,1,0:T(1,128)S(1)}, f32[8,1,256]{2,1,0:T(1,128)S(1)}, u32[]{:S(2)}, u32[]{:S(2)}) collective-permute-start(f32[8,1,256]{2,1,0:T(1,128)S(1)} %slice.82), channel_id=1, source_target_pairs={{0,1},{1,2},{2,3},{4,5},{5,6},{6,7},{8,9},{9,10},{10,11},{12,13},{... | collective-permute-start | bytes 24584 | tf_op jit(solution)/shard_map/while/body/eval_jaxpr/ppermute | solution.py:18
  373.7 7.2 %collective-permute-start.2 = (f32[1,128,256]{2,1,0:T(8,128)S(1)}, f32[1,128,256]{2,1,0:T(8,128)S(1)}, u32[]{:S(2)}, u32[]{:S(2)}) collective-permute-start(f32[1,128,256]{2,1,0:T(8,128)S(1)} %slice.81), channel_id=1, source_target_pairs={{0,4},{4,8},{8,12},{12,16},{16,20},{20,24},{24,28},{1,5},{5,9},{9,... | collective-permute-start | bytes 393224 | tf_op jit(solution)/shard_map/while/body/eval_jaxpr/ppermute | solution.py:18
  382.0 7.3 %collective-permute-start = (f32[1,128,256]{2,1,0:T(8,128)S(1)}, f32[1,128,256]{2,1,0:T(8,128)S(1)}, u32[]{:S(2)}, u32[]{:S(2)}) collective-permute-start(f32[1,128,256]{2,1,0:T(8,128)S(1)} %slice.75), channel_id=1, source_target_pairs={{4,0},{8,4},{12,8},{16,12},{20,16},{24,20},{28,24},{5,1},{9,5},{13... | collective-permute-start | bytes 393224 | tf_op jit(solution)/shard_map/while/body/eval_jaxpr/ppermute | solution.py:18
  392.7 9.2 %collective-permute-start.3 = (f32[8,1,256]{2,1,0:T(1,128)S(1)}, f32[8,1,256]{2,1,0:T(1,128)S(1)}, u32[]{:S(2)}, u32[]{:S(2)}) collective-permute-start(f32[8,1,256]{2,1,0:T(1,128)S(1)} %slice.82), channel_id=1, source_target_pairs={{0,1},{1,2},{2,3},{4,5},{5,6},{6,7},{8,9},{9,10},{10,11},{12,13},{... | collective-permute-start | bytes 24584 | tf_op jit(solution)/shard_map/while/body/eval_jaxpr/ppermute | solution.py:18
  394.6 7.2 %collective-permute-start.2 = (f32[1,128,256]{2,1,0:T(8,128)S(1)}, f32[1,128,256]{2,1,0:T(8,128)S(1)}, u32[]{:S(2)}, u32[]{:S(2)}) collective-permute-start(f32[1,128,256]{2,1,0:T(8,128)S(1)} %slice.81), channel_id=1, source_target_pairs={{0,4},{4,8},{8,12},{12,16},{16,20},{20,24},{24,28},{1,5},{5,9},{9,... | collective-permute-start | bytes 393224 | tf_op jit(solution)/shard_map/while/body/eval_jaxpr/ppermute | solution.py:18
  403.0 7.3 %collective-permute-start = (f32[1,128,256]{2,1,0:T(8,128)S(1)}, f32[1,128,256]{2,1,0:T(8,128)S(1)}, u32[]{:S(2)}, u32[]{:S(2)}) collective-permute-start(f32[1,128,256]{2,1,0:T(8,128)S(1)} %slice.75), channel_id=1, source_target_pairs={{4,0},{8,4},{12,8},{16,12},{20,16},{24,20},{28,24},{5,1},{9,5},{13... | collective-permute-start | bytes 393224 | tf_op jit(solution)/shard_map/while/body/eval_jaxpr/ppermute | solution.py:18
  413.7 9.2 %collective-permute-start.3 = (f32[8,1,256]{2,1,0:T(1,128)S(1)}, f32[8,1,256]{2,1,0:T(1,128)S(1)}, u32[]{:S(2)}, u32[]{:S(2)}) collective-permute-start(f32[8,1,256]{2,1,0:T(1,128)S(1)} %slice.82), channel_id=1, source_target_pairs={{0,1},{1,2},{2,3},{4,5},{5,6},{6,7},{8,9},{9,10},{10,11},{12,13},{... | collective-permute-start | bytes 24584 | tf_op jit(solution)/shard_map/while/body/eval_jaxpr/ppermute | solution.py:18
  415.6 7.2 %collective-permute-start.2 = (f32[1,128,256]{2,1,0:T(8,128)S(1)}, f32[1,128,256]{2,1,0:T(8,128)S(1)}, u32[]{:S(2)}, u32[]{:S(2)}) collective-permute-start(f32[1,128,256]{2,1,0:T(8,128)S(1)} %slice.81), channel_id=1, source_target_pairs={{0,4},{4,8},{8,12},{12,16},{16,20},{20,24},{24,28},{1,5},{5,9},{9,... | collective-permute-start | bytes 393224 | tf_op jit(solution)/shard_map/while/body/eval_jaxpr/ppermute | solution.py:18
  (39 other events, 213.2 us)
Sparse Core Ops, SparseCore 0:
  62.8 26.4 reduce-scatter.1
where the time goes:
time: 440 us; the launch traced here: 432 us
  starting transfers between devices  174 us (40%)
  other arithmetic  103 us (23%)
  waiting for transfers between devices  69.2 us (16%)
  local copies, waits for them, and re-layouts  65.9 us (15%)
  between operations  14.1 us (3%)
    ppermute x64, starting transfers between devices, passed_along(): lax.ppermute(value, axis, [(source, source + steps) for source in range(f...  164 us
    sub x16, other arithmetic, advance(): vel_x = vel_now[0] - TIME_STEP * buoyancy * grad_x  52.5 us
    ppermute x64, waiting for transfers between devices, passed_along(): lax.ppermute(value, axis, [(source, source + steps) for source in range(f...  38.7 us
    gather x48, local copies, waits for them, and re-layouts  32.9 us
    another operation x16, other arithmetic, advance(): return (pres_next, jnp.stack([vel_x, vel_y, vel_z]))  31.9 us
    reduce_scatter x1, waiting for transfers between devices, local(): lax.psum_scatter(jnp.einsum('ry,rxz->yxz', profile, outer_terms, preferre...  26.6 us
    slice x16, local copies, waits for them, and re-layouts, advance(): grad_x = jnp.concatenate([pres_now[1:], ahead_x], 0) - pres_now  16.5 us
    add x16, other arithmetic, advance(): pres_now - TIME_STEP * stiffness * divergence + TIME_STEP * source  16.3 us
  transfers between devices with their start and end apart: 67, of which 33 were waited for; matrix products, arithmetic and copies ran while one was open for 21% of the time, Pallas kernels for 0%

commit v1 on v0

v1 whole, which is shorter than its diff:
```python
import functools

import jax
import jax.numpy as jnp
from jax import lax
from jax.experimental import pallas as pl
from jax.experimental.pallas import tpu as pltpu
from jax.sharding import PartitionSpec as P

TIME_STEP = 0.3
STEPS = 16
HX = 4
HY = 16
BAND = 128.0
LANES = 128
SUB = 8
CHUNK = 32
BLOCK = 2
BF16 = jnp.bfloat16
F32 = jnp.float32
VM = pl.BlockSpec(memory_space=pltpu.VMEM)
SM = pl.BlockSpec(memory_space=pltpu.SMEM)


def passed_along(value, axis, steps):
    count = lax.axis_size(axis)
    first, last = (max(0, -steps), min(count, count - steps))
    return lax.ppermute(value, axis, [(source, source + steps) for source in range(first, last)])


def params(mib):
    return pltpu.CompilerParams(vmem_limit_bytes=mib << 20)


def pack_rows_kernel(p, v, k, b, s_e, c_e, k_e, b_e, vx_e, to_ahead, to_behind):
    planes, rows, depth = p.shape

    def one_plane(x, _):
        prev = jnp.maximum(x - 1, 0)
        for r in range(0, rows, CHUNK):
            sl = pl.ds(r, CHUNK)
            dst = pl.ds(HY + r, CHUNK)
            lane = lax.broadcasted_iota(jnp.int32, (CHUNK, depth), 1)
            row = lax.broadcasted_iota(jnp.int32, (CHUNK, depth), 0)
            vx, vy, vz = v[0, x, sl, :], v[1, x, sl, :], v[2, x, sl, :]
            vx_prev = jnp.where(x > 0, v[0, prev, sl, :], 0.0)
            above = jnp.zeros((1, depth), F32) if r == 0 else v[1, x, pl.ds(r - 1, 1), :]
            vy_prev = jnp.where(row == 0, above, pltpu.roll(vy, 1, 0))
            vz_prev = jnp.where(lane == 0, 0.0, pltpu.roll(vz, 1, 1))
            div = (vx - vx_prev) + (vy - vy_prev) + (vz - vz_prev)
            kk = k[x, sl, :]
            s_e[HX + x, dst, :] = p[x, sl, :]
            c_e[HX + x, dst, :] = -TIME_STEP * kk * div
            k_e[HX + x, dst, :] = kk
            b_e[HX + x, dst, :] = b[x, sl, :]
        for i, field in enumerate((s_e, c_e, k_e, b_e)):
            to_ahead[i * planes + x] = field[HX + x, pl.ds(rows, HY), :].astype(BF16)
            to_behind[i * planes + x] = field[HX + x, pl.ds(HY, HY), :].astype(BF16)
        return 0

    lax.fori_loop(0, planes, one_plane, 0)
    vx_e[pl.ds(HY, rows), :] = v[0, planes - 1]
    to_ahead[4 * planes] = v[0, planes - 1, pl.ds(rows - HY, HY), :].astype(BF16)
    to_behind[4 * planes] = v[0, planes - 1, pl.ds(0, HY), :].astype(BF16)
    last = v[1, :, rows - 1, :]
    to_ahead[4 * planes + 1] = jnp.concatenate([last, jnp.zeros((HY - planes, depth), F32)], 0).astype(BF16)


def pack_planes_kernel(
    behind, ahead, vy_last, s_i, c_i, k_i, b_i, vx_i, s_e, c_e, k_e, b_e, vx_e, to_ahead, to_behind
):
    del s_i, c_i, k_i, b_i, vx_i
    planes = vy_last.shape[0]
    rows = s_e.shape[1] - 2 * HY
    low, high = pl.ds(0, HY), pl.ds(HY + rows, HY)
    vy_behind = behind[4 * planes + 1].astype(F32)
    for x in range(planes):
        for i, field in enumerate((s_e, c_e, k_e, b_e)):
            field[HX + x, low, :] = behind[i * planes + x].astype(F32)
            field[HX + x, high, :] = ahead[i * planes + x].astype(F32)
        first = pl.ds(HY, 1)
        c_e[HX + x, first, :] += TIME_STEP * k_e[HX + x, first, :] * vy_behind[x : x + 1]
        beyond = pl.ds(HY + rows, 1)
        c_e[HX + x, beyond, :] += TIME_STEP * k_e[HX + x, beyond, :] * vy_last[x : x + 1, :]
    vx_e[low, :] = behind[4 * planes].astype(F32)
    vx_e[high, :] = ahead[4 * planes].astype(F32)
    at = 0
    for field, skip in ((s_e, 0), (c_e, 1), (k_e, 1), (b_e, 0)):
        for x in range(planes + skip, planes + HX):
            to_ahead[at] = field[x].astype(BF16)
            at += 1
    to_ahead[at] = vx_e[...].astype(BF16)
    at = 0
    for field, skip in ((s_e, 0), (c_e, 1), (k_e, 1), (b_e, 1)):
        for x in range(HX, 2 * HX - skip):
            to_behind[at] = field[x].astype(BF16)
            at += 1


def source_kernel(where_at, centre, routes, gathered, src):
    planes, rows, samples = src.shape
    sensors = gathered.shape[0]
    own_planes = planes - 2 * HX
    slab_at, row_from, row_count = where_at[0], where_at[1], where_at[2]
    row_at = row_from + lax.broadcasted_iota(jnp.int32, (rows, sensors), 0)
    distance = jnp.abs(row_at - centre[...]).astype(F32)
    band = jnp.maximum(0.0, 1.0 - distance / BAND)
    band = jnp.where((row_at >= 0) & (row_at < row_count), band, 0.0).astype(BF16)
    column = lax.broadcasted_iota(jnp.int32, (sensors, planes), 1)
    target = slab_at + jnp.where(column < HX, -1, jnp.where(column < HX + own_planes, 0, 1))
    weights = jnp.zeros((sensors, planes), F32)
    for i in range(routes.shape[1]):
        lat = gathered[:, samples + i * planes : samples + (i + 1) * planes].astype(F32)
        weights = weights + jnp.where(routes[:, i : i + 1] == target, lat, 0.0)
    trace = gathered[:, :samples].astype(F32)
    for x in range(planes):
        outer = (weights[:, x : x + 1] * trace).astype(BF16)
        src[x] = jnp.dot(band, outer, preferred_element_type=F32)


def tile(x, t, h):
    return (x, pl.ds(SUB * t, SUB), pl.ds(LANES * h, LANES))


def advance_planes(s, o, coef, x, count, t0, t1):
    c, a, ax, ay, az, d = coef
    row = lax.broadcasted_iota(jnp.int32, (SUB, LANES), 0)
    lane = lax.broadcasted_iota(jnp.int32, (SUB, LANES), 1)
    halves = range(s.shape[2] // LANES)

    def around(t):
        here = [[s[tile(x + i, t, h)] for h in halves] for i in range(count)]
        up = [[pltpu.roll(v, SUB - 1, 0) for v in q] for q in here]
        down = [[pltpu.roll(v, 1, 0) for v in q] for q in here]
        return here, up, down

    here, up, down = around(t0)
    down_prev = down
    for t in range(t0, t1):
        later, up_next, down_next = around(t + 1) if t + 1 < t1 else (here, up, down)
        before = [s[tile(x - 1, t, h)] for h in halves]
        for i in range(count):
            now = here[i]
            after = here[i + 1] if i + 1 < count else [s[tile(x + count, t, h)] for h in halves]
            right = [pltpu.roll(v, LANES - 1, 1) for v in now] + [jnp.zeros((SUB, LANES), F32)]
            left = [pltpu.roll(v, 1, 1) for v in now]
            for h in halves:
                at = tile(x + i, t, h)
                y_next = jnp.where(row == SUB - 1, up_next[i][h], up[i][h])
                y_prev = jnp.where(row == 0, down_prev[i][h], down[i][h])
                z_next = jnp.where(lane == LANES - 1, right[h + 1], right[h])
                z_prev = left[0] if h == 0 else jnp.where(lane == 0, left[h - 1], left[h])
                moved = a[at] * (after[h] + y_next + z_next) + ax[at] * before[h]
                moved = moved + ay[at] * y_prev + az[at] * z_prev + d[at] * now[h]
                o[at] = moved + (c[at] - o[at])
            before = now
        here, up, down, down_prev = later, up_next, down_next, down


def advance_round(s, o, coef, done):
    planes, rows, _ = s.shape
    fields = [s, o]
    for step in range(1, HX + 1):
        now, then = fields[(step - 1) % 2], fields[step % 2]
        skip = (done + step - 1) // SUB
        t0, t1 = skip, rows // SUB - skip

        def some_planes(i, _, now=now, then=then, step=step, t0=t0, t1=t1):
            advance_planes(now, then, coef, step + i * BLOCK, BLOCK, t0, t1)
            return 0

        lax.fori_loop(0, (planes - 2 * step) // BLOCK, some_planes, 0)


def pack_state(s, o, to_ahead, to_behind, skip):
    planes, rows, _ = s.shape
    own = planes - 2 * HX
    sl = pl.ds(skip, rows - 2 * skip)
    for i in range(HX):
        to_ahead[i] = s[own + i, sl, :].astype(BF16)
        to_behind[i] = s[HX + i, sl, :].astype(BF16)
    for i in range(1, HX):
        to_ahead[HX + i - 1] = (s[own + i, sl, :] - o[own + i, sl, :]).astype(BF16)
        to_behind[HX + i - 1] = (s[HX + i - 1, sl, :] - o[HX + i - 1, sl, :]).astype(BF16)


def first_round_kernel(
    behind, ahead, src, k_e, b_e, vx_e, s_i, c_i, s, o, c, a, ax, ay, az, d, to_ahead, to_behind
):
    del s_i, c_i
    planes, rows, depth = s.shape
    edge = planes - HX
    at = 0
    for field, skip in ((s, 0), (c, 1), (k_e, 1), (b_e, 0)):
        for x in range(skip, HX):
            field[x] = behind[at].astype(F32)
            at += 1
    vx_behind = behind[at]
    at = 0
    for field, skip in ((s, 0), (c, 1), (k_e, 1), (b_e, 1)):
        for x in range(edge, planes - skip):
            field[x] = ahead[at].astype(F32)
            at += 1
    c[HX] += TIME_STEP * k_e[HX] * vx_behind.astype(F32)
    c[edge] += TIME_STEP * k_e[edge] * vx_e[...]
    zeros = jnp.zeros((CHUNK, depth), F32)

    def one_plane(x, _):
        for r in range(0, rows, CHUNK):
            sl = pl.ds(r, CHUNK)
            row = lax.broadcasted_iota(jnp.int32, (CHUNK, depth), 0)
            lane = lax.broadcasted_iota(jnp.int32, (CHUNK, depth), 1)
            kk = TIME_STEP * TIME_STEP * k_e[x, sl, :]
            bb = b_e[x, sl, :]
            b_x = b_e[x - 1, sl, :]
            above = b_e[x, pl.ds(max(r - 1, 0), 1), :]
            b_y = jnp.where(row == 0, above, pltpu.roll(bb, 1, 0))
            b_z = jnp.where(lane == 0, 0.0, pltpu.roll(bb, 1, 1))
            a[x, sl, :] = kk * bb
            ax[x, sl, :] = kk * b_x
            ay[x, sl, :] = kk * b_y
            az[x, sl, :] = kk * b_z
            d[x, sl, :] = 2.0 - kk * (3.0 * bb + b_x + b_y + b_z)
            c[x, sl, pl.ds(depth - src.shape[2], src.shape[2])] += TIME_STEP * src[x, sl, :]
        return 0

    lax.fori_loop(1, planes - 1, one_plane, 0)

    def clear(x, _):
        for r in range(0, rows, CHUNK):
            o[x, pl.ds(r, CHUNK), :] = zeros
        return 0

    lax.fori_loop(0, planes, clear, 0)
    advance_round(s, o, (c, a, ax, ay, az, d), 0)
    pack_state(s, o, to_ahead, to_behind, 0)


def take_halo(behind, ahead, s, o, skip):
    planes, rows, _ = s.shape
    edge = planes - HX
    sl = pl.ds(skip, rows - 2 * skip)
    for i in range(HX):
        s[i, sl, :] = behind[i].astype(F32)
        s[edge + i, sl, :] = ahead[i].astype(F32)
    for i in range(1, HX):
        o[i, sl, :] = s[i, sl, :] - behind[HX + i - 1].astype(F32)
        o[edge + i - 1, sl, :] = s[edge + i - 1, sl, :] - ahead[HX + i - 1].astype(F32)


def middle_round_kernel(behind, ahead, c, a, ax, ay, az, d, s_i, o_i, s, o, to_ahead, to_behind, *, done, skips):
    del s_i, o_i
    take_halo(behind, ahead, s, o, skips[0])
    advance_round(s, o, (c, a, ax, ay, az, d), done)
    pack_state(s, o, to_ahead, to_behind, skips[1])


def last_round_kernel(
    behind, ahead, c, a, ax, ay, az, d, b_e, v, s_i, o_i, p_out, v_out, s, o, *, done, skip
):
    del s_i, o_i
    take_halo(behind, ahead, s, o, skip)
    advance_round(s, o, (c, a, ax, ay, az, d), done)
    planes, rows, depth = p_out.shape

    def one_plane(x, _):
        for r in range(0, rows, CHUNK):
            sl, src = pl.ds(r, CHUNK), pl.ds(HY + r, CHUNK)
            row = lax.broadcasted_iota(jnp.int32, (CHUNK, depth), 0)
            lane = lax.broadcasted_iota(jnp.int32, (CHUNK, depth), 1)
            total = o[HX + x, src, :]
            p_out[x, sl, :] = s[HX + x, src, :] - total
            below = o[HX + x, pl.ds(HY + r + CHUNK, 1), :]
            y_next = jnp.where(row == CHUNK - 1, below, pltpu.roll(total, CHUNK - 1, 0))
            z_next = jnp.where(lane == depth - 1, 0.0, pltpu.roll(total, depth - 1, 1))
            bb = TIME_STEP * b_e[HX + x, src, :]
            v_out[0, x, sl, :] = v[0, x, sl, :] - bb * (o[HX + x + 1, src, :] - total)
            v_out[1, x, sl, :] = v[1, x, sl, :] - bb * (y_next - total)
            v_out[2, x, sl, :] = v[2, x, sl, :] - bb * (z_next - total)
        return 0

    lax.fori_loop(0, planes, one_plane, 0)


def local(pressure, velocity, stiffness, buoyancy, traces, lateral, routes, ycenter):
    planes, rows, depth = pressure.shape
    samples = traces.shape[1]
    wide, tall = planes + 2 * HX, rows + 2 * HY
    block = pltpu.VMEM((wide, tall, depth), F32)
    line = pltpu.VMEM((tall, depth), F32)

    lat = jnp.concatenate([lateral[:, :, planes - HX :], lateral, lateral[:, :, :HX]], 2)
    rows_sent = jnp.concatenate([traces, lat.reshape(lat.shape[0], -1)], 1)
    gathered = lax.all_gather(rows_sent, "grp", tiled=True)
    gathered = lax.all_gather(gathered, "slab", tiled=True)

    units = 4 * planes
    s, c, k_e, b_e, vx_e, row_ahead, row_behind = pl.pallas_call(
        pack_rows_kernel,
        out_shape=(
            block, block, block, block, line,
            jax.ShapeDtypeStruct((units + 2, HY, depth), BF16),
            jax.ShapeDtypeStruct((units + 1, HY, depth), BF16),
        ),
        in_specs=[VM] * 4,
        out_specs=[VM] * 7,
        compiler_params=params(16),
    )(pressure, velocity, stiffness, buoyancy)
    from_behind = passed_along(row_ahead, "grp", 1)
    from_ahead = passed_along(row_behind, "grp", -1)

    n_ahead, n_behind = 4 * HX - 1, 4 * HX - 3
    s, c, k_e, b_e, vx_e, plane_ahead, plane_behind = pl.pallas_call(
        pack_planes_kernel,
        out_shape=(
            block, block, block, block, line,
            jax.ShapeDtypeStruct((n_ahead, tall, depth), BF16),
            jax.ShapeDtypeStruct((n_behind, tall, depth), BF16),
        ),
        in_specs=[VM] * 8,
        out_specs=[VM] * 7,
        input_output_aliases={3: 0, 4: 1, 5: 2, 6: 3, 7: 4},
        compiler_params=params(16),
    )(from_behind, from_ahead, velocity[1, :, rows - 1, :], s, c, k_e, b_e, vx_e)
    from_behind = passed_along(plane_ahead, "slab", 1)
    from_ahead = passed_along(plane_behind, "slab", -1)

    where_at = jnp.stack(
        [
            lax.axis_index("slab"),
            lax.axis_index("grp") * rows - HY,
            jnp.int32(rows * lax.axis_size("grp")),
        ]
    ).astype(jnp.int32)
    src = pl.pallas_call(
        source_kernel,
        out_shape=pltpu.VMEM((wide, tall, samples), F32),
        in_specs=[SM, VM, VM, VM],
        out_specs=VM,
        compiler_params=params(16),
    )(where_at, ycenter[None, :], routes, gathered)

    def sent(skip):
        return jax.ShapeDtypeStruct((2 * HX - 1, tall - 2 * skip, depth), BF16)

    s, o, c, a, ax, ay, az, d, plane_ahead, plane_behind = pl.pallas_call(
        first_round_kernel,
        out_shape=(block,) * 8 + (sent(0), sent(0)),
        in_specs=[VM] * 8,
        out_specs=[VM] * 10,
        input_output_aliases={6: 0, 7: 2},
        compiler_params=params(16),
    )(from_behind, from_ahead, src, k_e, b_e, vx_e, s, c)
    coef = (c, a, ax, ay, az, d)

    rounds = STEPS // HX
    skips = [SUB * (HX * r // SUB) for r in range(1, rounds)]
    for r in range(1, rounds - 1):
        from_behind = passed_along(plane_ahead, "slab", 1)
        from_ahead = passed_along(plane_behind, "slab", -1)
        s, o, plane_ahead, plane_behind = pl.pallas_call(
            functools.partial(middle_round_kernel, done=HX * r, skips=skips[r - 1 : r + 1]),
            out_shape=(block, block, sent(skips[r]), sent(skips[r])),
            in_specs=[VM] * 10,
            out_specs=[VM] * 4,
            input_output_aliases={8: 0, 9: 1},
            compiler_params=params(16),
        )(from_behind, from_ahead, *coef, s, o)
    from_behind = passed_along(plane_ahead, "slab", 1)
    from_ahead = passed_along(plane_behind, "slab", -1)
    return pl.pallas_call(
        functools.partial(last_round_kernel, done=HX * (rounds - 1), skip=skips[-1]),
        out_shape=(
            jax.ShapeDtypeStruct(pressure.shape, F32),
            jax.ShapeDtypeStruct(velocity.shape, F32),
            block,
            block,
        ),
        in_specs=[VM] * 12,
        out_specs=[VM] * 4,
        input_output_aliases={10: 2, 11: 3},
        compiler_params=params(16),
    )(from_behind, from_ahead, *coef, b_e, velocity, s, o)[:2]


def solution(mesh):
    in_specs = (
        P("slab", "grp", None),
        P(None, "slab", "grp", None),
        P("slab", "grp", None),
        P("slab", "grp", None),
        P(("slab", "grp"), None),
        P(("slab", "grp"), None, None),
        P(),
        P(),
    )
    out_specs = (P("slab", "grp", None), P(None, "slab", "grp", None))
    return jax.shard_map(local, mesh=mesh, in_specs=in_specs, out_specs=out_specs, check_vma=False)
```

time: 440 us -> 148 us (0.34); the launches traced: 432 us -> 147 us
  starting transfers between devices: 174 us -> 27.7 us
  other arithmetic: 103 us -> 0.09 us
  local copies, waits for them, and re-layouts: 65.9 us -> 13.9 us
  Pallas kernels: 0 us -> 37.4 us
  waiting for transfers between devices: 69.2 us -> 38.6 us
  blocking collectives: 0 us -> 28.4 us
  between operations: 14.1 us -> 0.89 us
    ppermute x64 -> x10, starting transfers between devices: 164 us -> 27.7 us  [passed_along(): lax.ppermute(value, axis, [(source, source + steps) for source in range(f...]
    sub x18 -> x0, other arithmetic: 52.5 us -> none  [the longest x16 52.5 us: advance(): vel_x = vel_now[0] - TIME_STEP * buoyancy * grad_x]
    pallas_call x0 -> x7, Pallas kernels: none -> 37.4 us  [the longest x2 12.3 us: local(): pl.pallas_call(functools.partial(middle_round_kernel, done=HX * r, skips=...]
    gather x48 -> x0, local copies, waits for them, and re-layouts: 32.9 us -> none
    another operation x18 -> x1, other arithmetic: 32.1 us -> 0.08 us  [local(): jnp.stack([lax.axis_index('slab'), lax.axis_index('grp') * rows - HY, jnp...]
    all_gather x0 -> x2, blocking collectives: none -> 28.4 us  [the longest x1 17.5 us: local(): gathered = lax.all_gather(gathered, 'slab', tiled=True)]
    reduce_scatter x1 -> x0, waiting for transfers between devices: 26.6 us -> none  [local(): lax.psum_scatter(jnp.einsum('ry,rxz->yxz', profile, outer_terms, preferre...]
    slice x128 -> x2, local copies, waits for them, and re-layouts: 25.3 us -> 0.02 us  [the longest x1 0.01 us: local(): velocity[1, :, rows - 1, :]]
  transfers between devices with their start and end apart: 67 -> 10, of which waited for: 33 -> 7; matrix products, arithmetic and copies ran while one was open for 21% -> 0% of each run, Pallas kernels for 0% -> 2%
where the time goes in v1:
time: 148 us; the launch traced here: 147 us
  waiting for transfers between devices  38.6 us (26%)
  Pallas kernels  37.4 us (25%)
  blocking collectives  28.4 us (19%)
  starting transfers between devices  27.7 us (19%)
  local copies, waits for them, and re-layouts  13.9 us (9%)
    ppermute x10, waiting for transfers between devices, passed_along(): lax.ppermute(value, axis, [(source, source + steps) for source in range(f...  38.6 us
    ppermute x10, starting transfers between devices, passed_along(): lax.ppermute(value, axis, [(source, source + steps) for source in range(f...  27.7 us
    all_gather x1, blocking collectives, local(): gathered = lax.all_gather(gathered, 'slab', tiled=True)  17.5 us
    unnamed x34, local copies, waits for them, and re-layouts  13.8 us
    pallas_call x2, Pallas kernels, local(): pl.pallas_call(functools.partial(middle_round_kernel, done=HX * r, skips=...  12.3 us
    all_gather x1, blocking collectives, local(): gathered = lax.all_gather(rows_sent, 'grp', tiled=True)  10.9 us
    pallas_call x1, Pallas kernels, local(): pl.pallas_call(first_round_kernel, out_shape=(block,) * 8 + (sent(0), sen...  10.4 us
    pallas_call x1, Pallas kernels, local(): pl.pallas_call(functools.partial(last_round_kernel, done=HX * (rounds - 1...  8.58 us
  transfers between devices with their start and end apart: 10, of which 7 were waited for; matrix products, arithmetic and copies ran while one was open for 0% of the time, Pallas kernels for 2%

profile of v1, /device:TPU:1, one launch (start us, length us, event | category | flops | bytes accessed | tf_op | source)
XLA Modules:
  0.0 147.0 jit_solution(12882691323112817602)
XLA Ops:
  0.6 0.0 copy-start.5
  0.6 1.9 %copy-done.5 = f32[3,8,128,256]{3,2,1,0:T(8,128)S(1)} copy-done((f32[3,8,128,256]{3,2,1,0:T(8,128)S(1)}, f32[3,8,128,256]{3,2,1,0:T(8,128)}, u32[]{:S(2)}) %copy-start.5) | copy-done | bytes 3145752
  2.5 0.0 copy-start.9
  2.5 1.2 copy-done.9
  3.7 0.0 copy-start.10
  3.8 1.2 copy-done.10
  5.0 0.0 copy-start.11
  5.0 1.2 copy-done.11
  6.2 0.9 shard_map.95
  7.1 4.0 %collective-permute-start = (bf16[34,16,256]{2,1,0:T(8,128)(2,1)S(1)}, bf16[34,16,256]{2,1,0:T(8,128)(2,1)S(1)}, u32[]{:S(2)}, u32[]{:S(2)}) collective-permute-start(bf16[34,16,256]{2,1,0:T(8,128)(2,1)S(1)} %get-tuple-element.36), channel_id=1, source_target_pairs={{0,1},{1,2},{2,3},{4,5},{5,6},{6,7},{8,9},{9,10},{10,11},{12,13},{... | collective-permute-start | bytes 835592 | tf_op jit(solution)/shard_map/ppermute | solution.py:28
  11.2 1.3 collective-permute-start.1
  12.5 7.6 %collective-permute-done.1.ahead = bf16[33,16,256]{2,1,0:T(8,128)(2,1)S(1)} collective-permute-done((bf16[33,16,256]{2,1,0:T(8,128)(2,1)S(1)}, bf16[33,16,256]{2,1,0:T(8,128)(2,1)S(1)}, u32[]{:S(2)}, u32[]{:S(2)}) %collective-permute-start.1) | collective-permute-done | bytes 270368 | tf_op jit(solution)/shard_map/ppermute | solution.py:28
  20.1 0.0 collective-permute-done.behind
  20.1 0.0 copy-start.13
  20.1 0.0 copy-start.14
  20.1 0.0 copy-start.15
  20.1 0.0 copy-start.12
  20.1 1.7 %shard_map.96 = (f32[16,160,256]{2,1,0:T(8,128)S(1)}, f32[16,160,256]{2,1,0:T(8,128)S(1)}, f32[16,160,256]{2,1,0:T(8,128)S(1)}, f32[16,160,256]{2,1,0:T(8,128)S(...) custom-call(bf16[34,16,256]{2,1,0:T(8,128)(2,1)S(1)} %collective-per, ...), custom_call_target="tpu_custom_call", output_to_operand_aliasing={{0}: (3, {}), {1}: (4, {}), {2}: (5, {}), {3}: (6, {}), {4}... | custom-call | tf_op jit(solution)/shard_map/pallas_call | solution.py:313
  21.9 0.0 copy-start
  21.9 1.5 %copy-done = f32[16,160,256]{2,1,0:T(8,128)} copy-done((f32[16,160,256]{2,1,0:T(8,128)}, f32[16,160,256]{2,1,0:T(8,128)S(1)}, u32[]{:S(2)}) %copy-start) | copy-done | bytes 2621464
  23.4 0.0 copy-start.2
  23.4 1.5 %copy-done.2 = f32[16,160,256]{2,1,0:T(8,128)} copy-done((f32[16,160,256]{2,1,0:T(8,128)}, f32[16,160,256]{2,1,0:T(8,128)S(1)}, u32[]{:S(2)}) %copy-start.2) | copy-done | bytes 2621464
  24.9 0.0 copy-start.7
  24.9 1.5 %copy-done.7 = f32[16,160,256]{2,1,0:T(8,128)} copy-done((f32[16,160,256]{2,1,0:T(8,128)}, f32[16,160,256]{2,1,0:T(8,128)S(1)}, u32[]{:S(2)}) %copy-start.7) | copy-done | bytes 2621464
  26.4 4.9 %collective-permute-start.2 = (bf16[15,160,256]{2,1,0:T(8,128)(2,1)}, bf16[15,160,256]{2,1,0:T(8,128)(2,1)}, u32[]{:S(2)}, u32[]{:S(2)}) collective-permute-start(bf16[15,160,256]{2,1,0:T(8,128)(2,1)} %get-tuple-element.43), channel_id=1, source_target_pairs={{0,4},{4,8},{8,12},{12,16},{16,20},{20,24},{24,28},{1,5},{5,9},{9,... | collective-permute-start | bytes 3686408 | tf_op jit(solution)/shard_map/ppermute | solution.py:28
  31.3 1.9 %collective-permute-start.3 = (bf16[13,160,256]{2,1,0:T(8,128)(2,1)}, bf16[13,160,256]{2,1,0:T(8,128)(2,1)}, u32[]{:S(2)}, u32[]{:S(2)}) collective-permute-start(bf16[13,160,256]{2,1,0:T(8,128)(2,1)} %get-tuple-element.44), channel_id=1, source_target_pairs={{4,0},{8,4},{12,8},{16,12},{20,16},{24,20},{28,24},{5,1},{9,5},{13... | collective-permute-start | bytes 3194888 | tf_op jit(solution)/shard_map/ppermute | solution.py:28
  33.2 0.0 copy-done.13
  33.3 0.1 copy.27
  33.3 0.0 copy-done.14
  33.3 0.2 copy.28.routes
  33.6 0.0 copy-done.15
  33.6 0.0 copy-start.1
  33.6 10.9 %all_gather.6 = bf16[128,160]{1,0:T(8,128)(2,1)S(1)} all-gather(bf16[32,160]{1,0:T(8,128)(2,1)S(1)} %pad_maximum_fusion), channel_id=1, replica_groups=mesh['slab'=8,'grp'=4] {'grp'}, dimensions={0}, use_global_device_ids=true | all-gather | bytes 51200 | tf_op jit(solution)/shard_map/all_gather | solution.py:294
  44.6 17.5 %all_gather.7.gathered = bf16[1024,160]{1,0:T(8,128)(2,1)S(1)} all-gather(bf16[128,160]{1,0:T(8,128)(2,1)S(1)} %all_gather.6), channel_id=1, replica_groups=mesh['slab'=8,'grp'=4] {'slab'}, dimensions={0}, use_global_device_ids=true | all-gather | bytes 368640 | tf_op jit(solution)/shard_map/all_gather | solution.py:295
  62.0 0.1 pad_add_fusion.where_at
  62.1 0.0 copy-done.12
  62.1 3.4 %shard_map.97.src = f32[16,160,128]{2,1,0:T(8,128)S(1)} custom-call(s32[3]{0:T(128)S(1)} %pad_add_fusion.where_at, s32[1,1024]{1,0:T(1,128)S(1)} %bitcast.8, s32[1024,2]{1,0:T(8,128)S(1)} %copy.28.routes, bf16[1024,160]{1,0:T(8,128)(2,1)S(1)} %all_gather.7.gathered), custom_call_target="tpu_custom_call" | custom-call | tf_op jit(solution)/shard_map/pallas_call | solution.py:335
  65.5 0.0 collective-permute-done.3.ahead
  65.5 0.0 collective-permute-done.2.behind
  65.6 0.0 copy-done.1
  65.6 0.0 copy-start.3
  65.6 1.7 %copy-done.3 = f32[16,160,256]{2,1,0:T(8,128)S(1)} copy-done((f32[16,160,256]{2,1,0:T(8,128)S(1)}, f32[16,160,256]{2,1,0:T(8,128)}, u32[]{:S(2)}) %copy-start.3) | copy-done | bytes 2621464
  67.3 0.0 copy-start.8
  67.3 1.7 %copy-done.8 = f32[16,160,256]{2,1,0:T(8,128)S(1)} copy-done((f32[16,160,256]{2,1,0:T(8,128)S(1)}, f32[16,160,256]{2,1,0:T(8,128)}, u32[]{:S(2)}) %copy-start.8) | copy-done | bytes 2621464
  69.0 10.4 %shard_map.98 = (f32[16,160,256]{2,1,0:T(8,128)S(1)}, f32[16,160,256]{2,1,0:T(8,128)S(1)}, f32[16,160,256]{2,1,0:T(8,128)S(1)}, f32[16,160,256]{2,1,0:T(8,128)S(...) custom-call(bf16[15,160,256]{2,1,0:T(8,128)(2,1)} %collective-permut, ...), custom_call_target="tpu_custom_call", output_to_operand_aliasing={{0}: (6, {}), {2}: (7, {})} | custom-call | tf_op jit(solution)/shard_map/pallas_call | solution.py:346
  79.5 5.0 %collective-permute-start.4 = (bf16[7,160,256]{2,1,0:T(8,128)(2,1)S(1)}, bf16[7,160,256]{2,1,0:T(8,128)(2,1)S(1)}, u32[]{:S(2)}, u32[]{:S(2)}) collective-permute-start(bf16[7,160,256]{2,1,0:T(8,128)(2,1)S(1)} %get-tuple-element.50), channel_id=1, source_target_pairs={{0,4},{4,8},{8,12},{12,16},{16,20},{20,24},{24,28},{1,5},{5,9},{9,... | collective-permute-start | bytes 1720328 | tf_op jit(solution)/shard_map/ppermute | solution.py:28
  84.4 1.9 %collective-permute-start.5 = (bf16[7,160,256]{2,1,0:T(8,128)(2,1)S(1)}, bf16[7,160,256]{2,1,0:T(8,128)(2,1)S(1)}, u32[]{:S(2)}, u32[]{:S(2)}) collective-permute-start(bf16[7,160,256]{2,1,0:T(8,128)(2,1)S(1)} %get-tuple-element.51), channel_id=1, source_target_pairs={{4,0},{8,4},{12,8},{16,12},{20,16},{24,20},{28,24},{5,1},{9,5},{13... | collective-permute-start | bytes 1720328 | tf_op jit(solution)/shard_map/ppermute | solution.py:28
  86.4 4.7 %collective-permute-done.4.behind = bf16[7,160,256]{2,1,0:T(8,128)(2,1)S(1)} collective-permute-done((bf16[7,160,256]{2,1,0:T(8,128)(2,1)S(1)}, bf16[7,160,256]{2,1,0:T(8,128)(2,1)S(1)}, u32[]{:S(2)}, u32[]{:S(2)}) %collective-permute-start.4) | collective-permute-done | bytes 573472 | tf_op jit(solution)/shard_map/ppermute | solution.py:28
  91.1 7.8 %collective-permute-done.5.ahead = bf16[7,160,256]{2,1,0:T(8,128)(2,1)S(1)} collective-permute-done((bf16[7,160,256]{2,1,0:T(8,128)(2,1)S(1)}, bf16[7,160,256]{2,1,0:T(8,128)(2,1)S(1)}, u32[]{:S(2)}, u32[]{:S(2)}) %collective-permute-start.5) | collective-permute-done | bytes 573472 | tf_op jit(solution)/shard_map/ppermute | solution.py:28
  98.8 6.4 %shard_map.99 = (f32[16,160,256]{2,1,0:T(8,128)S(1)}, f32[16,160,256]{2,1,0:T(8,128)S(1)}, bf16[7,144,256]{2,1,0:T(8,128)(2,1)S(1)}, bf16[7,144,256]{2,1,0:T(8,128)(2,1)S(1)}) custom-call(bf16[7,160,256]{2,1,0:T(8,128)(2,1)S(1)} %collective-permute-done.4.behind, ...), custom_call_target="tpu_custom_call", output_to_operand_aliasing={{0}: (8, {}), {1}: (9, {})} | custom-call | tf_op jit(solution)/shard_map/pallas_call | solution.py:361
  105.2 1.9 %collective-permute-start.6 = (bf16[7,144,256]{2,1,0:T(8,128)(2,1)S(1)}, bf16[7,144,256]{2,1,0:T(8,128)(2,1)S(1)}, u32[]{:S(2)}, u32[]{:S(2)}) collective-permute-start(bf16[7,144,256]{2,1,0:T(8,128)(2,1)S(1)} %get-tuple-element.60), channel_id=1, source_target_pairs={{0,4},{4,8},{8,12},{12,16},{16,20},{20,24},{24,28},{1,5},{5,9},{9,... | collective-permute-start | bytes 1548296 | tf_op jit(solution)/shard_map/ppermute | solution.py:28
  107.2 2.4 %collective-permute-start.7 = (bf16[7,144,256]{2,1,0:T(8,128)(2,1)S(1)}, bf16[7,144,256]{2,1,0:T(8,128)(2,1)S(1)}, u32[]{:S(2)}, u32[]{:S(2)}) collective-permute-start(bf16[7,144,256]{2,1,0:T(8,128)(2,1)S(1)} %get-tuple-element.61), channel_id=1, source_target_pairs={{4,0},{8,4},{12,8},{16,12},{20,16},{24,20},{28,24},{5,1},{9,5},{13... | collective-permute-start | bytes 1548296 | tf_op jit(solution)/shard_map/ppermute | solution.py:28
  109.6 3.6 %collective-permute-done.6.behind = bf16[7,144,256]{2,1,0:T(8,128)(2,1)S(1)} collective-permute-done((bf16[7,144,256]{2,1,0:T(8,128)(2,1)S(1)}, bf16[7,144,256]{2,1,0:T(8,128)(2,1)S(1)}, u32[]{:S(2)}, u32[]{:S(2)}) %collective-permute-start.6) | collective-permute-done | bytes 516128 | tf_op jit(solution)/shard_map/ppermute | solution.py:28
  113.2 6.1 %collective-permute-done.7.ahead = bf16[7,144,256]{2,1,0:T(8,128)(2,1)S(1)} collective-permute-done((bf16[7,144,256]{2,1,0:T(8,128)(2,1)S(1)}, bf16[7,144,256]{2,1,0:T(8,128)(2,1)S(1)}, u32[]{:S(2)}, u32[]{:S(2)}) %collective-permute-start.7) | collective-permute-done | bytes 516128 | tf_op jit(solution)/shard_map/ppermute | solution.py:28
  119.2 0.0 copy-start.4
  119.3 0.0 copy-start.6
  119.3 5.9 %shard_map.100 = (f32[16,160,256]{2,1,0:T(8,128)S(1)}, f32[16,160,256]{2,1,0:T(8,128)S(1)}, bf16[7,144,256]{2,1,0:T(8,128)(2,1)S(1)}, bf16[7,144,256]{2,1,0:T(8,128)(2,1)S(1)}) custom-call(bf16[7,144,256]{2,1,0:T(8,128)(2,1)S(1)} %collective-permute-done.6.behind, ...), custom_call_target="tpu_custom_call", output_to_operand_aliasing={{0}: (8, {}), {1}: (9, {})} | custom-call | tf_op jit(solution)/shard_map/pallas_call | solution.py:361
  125.1 1.9 %collective-permute-start.8 = (bf16[7,144,256]{2,1,0:T(8,128)(2,1)S(1)}, bf16[7,144,256]{2,1,0:T(8,128)(2,1)S(1)}, u32[]{:S(2)}, u32[]{:S(2)}) collective-permute-start(bf16[7,144,256]{2,1,0:T(8,128)(2,1)S(1)} %get-tuple-element.64), channel_id=1, source_target_pairs={{0,4},{4,8},{8,12},{12,16},{16,20},{20,24},{24,28},{1,5},{5,9},{9,... | collective-permute-start | bytes 1548296 | tf_op jit(solution)/shard_map/ppermute | solution.py:28
  127.1 2.4 %collective-permute-start.9 = (bf16[7,144,256]{2,1,0:T(8,128)(2,1)S(1)}, bf16[7,144,256]{2,1,0:T(8,128)(2,1)S(1)}, u32[]{:S(2)}, u32[]{:S(2)}) collective-permute-start(bf16[7,144,256]{2,1,0:T(8,128)(2,1)S(1)} %get-tuple-element.65), channel_id=1, source_target_pairs={{4,0},{8,4},{12,8},{16,12},{20,16},{24,20},{28,24},{5,1},{9,5},{13... | collective-permute-start | bytes 1548296 | tf_op jit(solution)/shard_map/ppermute | solution.py:28
  129.5 3.6 %collective-permute-done.8.behind = bf16[7,144,256]{2,1,0:T(8,128)(2,1)S(1)} collective-permute-done((bf16[7,144,256]{2,1,0:T(8,128)(2,1)S(1)}, bf16[7,144,256]{2,1,0:T(8,128)(2,1)S(1)}, u32[]{:S(2)}, u32[]{:S(2)}) %collective-permute-start.8) | collective-permute-done | bytes 516128 | tf_op jit(solution)/shard_map/ppermute | solution.py:28
  133.1 5.3 %collective-permute-done.9.ahead = bf16[7,144,256]{2,1,0:T(8,128)(2,1)S(1)} collective-permute-done((bf16[7,144,256]{2,1,0:T(8,128)(2,1)S(1)}, bf16[7,144,256]{2,1,0:T(8,128)(2,1)S(1)}, u32[]{:S(2)}, u32[]{:S(2)}) %collective-permute-start.9) | collective-permute-done | bytes 516128 | tf_op jit(solution)/shard_map/ppermute | solution.py:28
  138.4 0.0 copy-done.4
  138.4 0.0 copy-done.6
  138.4 8.6 %shard_map.101 = (f32[8,128,256]{2,1,0:T(8,128)}, f32[3,8,128,256]{3,2,1,0:T(8,128)}, f32[16,160,256]{2,1,0:T(8,128)S(1)}, f32[16,160,256]{2,1,0:T(8,128)S(1)}) custom-call(bf16[7,144,256]{2,1,0:T(8,128)(2,1)S(1)} %collective-permute-done.8.behind, ...), custom_call_target="tpu_custom_call", output_to_operand_aliasing={{2}: (10, {}), {3}: (11, {})} | custom-call | tf_op jit(solution)/shard_map/pallas_call | solution.py:371
  (5 shorter events, 0.0 us)
Async XLA Ops:
  0.6 1.9 %copy-start.5 = (f32[3,8,128,256]{3,2,1,0:T(8,128)S(1)}, f32[3,8,128,256]{3,2,1,0:T(8,128)}, u32[]{:S(2)}) copy-start(f32[3,8,128,256]{3,2,1,0:T(8,128)} %v.3) | copy-start | bytes 9437188
  2.5 1.2 copy-start.9
  3.7 1.2 copy-start.10
  5.0 1.2 copy-start.11
  7.1 13.0 %collective-permute-start = (bf16[34,16,256]{2,1,0:T(8,128)(2,1)S(1)}, bf16[34,16,256]{2,1,0:T(8,128)(2,1)S(1)}, u32[]{:S(2)}, u32[]{:S(2)}) collective-permute-start(bf16[34,16,256]{2,1,0:T(8,128)(2,1)S(1)} %get-tuple-element.36), channel_id=1, source_target_pairs={{0,1},{1,2},{2,3},{4,5},{5,6},{6,7},{8,9},{9,10},{10,11},{12,13},{... | collective-permute-start | bytes 835592 | tf_op jit(solution)/shard_map/ppermute | solution.py:28
  11.2 8.9 %collective-permute-start.1 = (bf16[33,16,256]{2,1,0:T(8,128)(2,1)S(1)}, bf16[33,16,256]{2,1,0:T(8,128)(2,1)S(1)}, u32[]{:S(2)}, u32[]{:S(2)}) collective-permute-start(bf16[33,16,256]{2,1,0:T(8,128)(2,1)S(1)} %get-tuple-element.37), channel_id=1, source_target_pairs={{1,0},{2,1},{3,2},{5,4},{6,5},{7,6},{9,8},{10,9},{11,10},{13,12},{... | collective-permute-start | bytes 811016 | tf_op jit(solution)/shard_map/ppermute | solution.py:28
  20.1 13.1 %copy-start.13 = (bf16[32,2,8]{0,2,1:T(8,128)(2,1)S(1)}, bf16[32,2,8]{0,2,1:T(8,128)(2,1)}, u32[]{:S(2)}) copy-start(bf16[32,2,8]{0,2,1:T(8,128)(2,1)} %param.13) | copy-start | bytes 3076
  20.1 13.2 %copy-start.14 = (s32[1024,2]{0,1:T(2,128)S(1)}, s32[1024,2]{0,1:T(2,128)}, u32[]{:S(2)}) copy-start(s32[1024,2]{0,1:T(2,128)} %param.14) | copy-start | bytes 24580
  20.1 13.5 %copy-start.15 = (bf16[32,128]{1,0:T(8,128)(2,1)S(1)}, bf16[32,128]{1,0:T(8,128)(2,1)}, u32[]{:S(2)}) copy-start(bf16[32,128]{1,0:T(8,128)(2,1)} %param.12) | copy-start | bytes 24580
  20.1 42.0 %copy-start.12 = (s32[1024]{0:T(1024)S(1)}, s32[1024]{0:T(1024)}, u32[]{:S(2)}) copy-start(s32[1024]{0:T(1024)} %param.15) | copy-start | bytes 12292
  21.9 1.5 %copy-start = (f32[16,160,256]{2,1,0:T(8,128)}, f32[16,160,256]{2,1,0:T(8,128)S(1)}, u32[]{:S(2)}) copy-start(f32[16,160,256]{2,1,0:T(8,128)S(1)} %get-tuple-element.49.c_i) | copy-start | bytes 7864324
  23.4 1.5 %copy-start.2 = (f32[16,160,256]{2,1,0:T(8,128)}, f32[16,160,256]{2,1,0:T(8,128)S(1)}, u32[]{:S(2)}) copy-start(f32[16,160,256]{2,1,0:T(8,128)S(1)} %get-tuple-element.46.b_e) | copy-start | bytes 7864324
  24.9 1.5 %copy-start.7 = (f32[16,160,256]{2,1,0:T(8,128)}, f32[16,160,256]{2,1,0:T(8,128)S(1)}, u32[]{:S(2)}) copy-start(f32[16,160,256]{2,1,0:T(8,128)S(1)} %get-tuple-element.45.k_e) | copy-start | bytes 7864324
  26.4 39.1 %collective-permute-start.2 = (bf16[15,160,256]{2,1,0:T(8,128)(2,1)}, bf16[15,160,256]{2,1,0:T(8,128)(2,1)}, u32[]{:S(2)}, u32[]{:S(2)}) collective-permute-start(bf16[15,160,256]{2,1,0:T(8,128)(2,1)} %get-tuple-element.43), channel_id=1, source_target_pairs={{0,4},{4,8},{8,12},{12,16},{16,20},{20,24},{24,28},{1,5},{5,9},{9,... | collective-permute-start | bytes 3686408 | tf_op jit(solution)/shard_map/ppermute | solution.py:28
  31.3 34.3 %collective-permute-start.3 = (bf16[13,160,256]{2,1,0:T(8,128)(2,1)}, bf16[13,160,256]{2,1,0:T(8,128)(2,1)}, u32[]{:S(2)}, u32[]{:S(2)}) collective-permute-start(bf16[13,160,256]{2,1,0:T(8,128)(2,1)} %get-tuple-element.44), channel_id=1, source_target_pairs={{4,0},{8,4},{12,8},{16,12},{20,16},{24,20},{28,24},{5,1},{9,5},{13... | collective-permute-start | bytes 3194888 | tf_op jit(solution)/shard_map/ppermute | solution.py:28
  33.6 32.0 %copy-start.1 = (f32[16,160,256]{2,1,0:T(8,128)S(1)}, f32[16,160,256]{2,1,0:T(8,128)}, u32[]{:S(2)}) copy-start(f32[16,160,256]{2,1,0:T(8,128)} %copy-done) | copy-start | bytes 7864324
  65.6 1.7 %copy-start.3 = (f32[16,160,256]{2,1,0:T(8,128)S(1)}, f32[16,160,256]{2,1,0:T(8,128)}, u32[]{:S(2)}) copy-start(f32[16,160,256]{2,1,0:T(8,128)} %copy-done.2) | copy-start | bytes 7864324
  67.3 1.7 %copy-start.8 = (f32[16,160,256]{2,1,0:T(8,128)S(1)}, f32[16,160,256]{2,1,0:T(8,128)}, u32[]{:S(2)}) copy-start(f32[16,160,256]{2,1,0:T(8,128)} %copy-done.7) | copy-start | bytes 7864324
  79.5 11.6 %collective-permute-start.4 = (bf16[7,160,256]{2,1,0:T(8,128)(2,1)S(1)}, bf16[7,160,256]{2,1,0:T(8,128)(2,1)S(1)}, u32[]{:S(2)}, u32[]{:S(2)}) collective-permute-start(bf16[7,160,256]{2,1,0:T(8,128)(2,1)S(1)} %get-tuple-element.50), channel_id=1, source_target_pairs={{0,4},{4,8},{8,12},{12,16},{16,20},{20,24},{24,28},{1,5},{5,9},{9,... | collective-permute-start | bytes 1720328 | tf_op jit(solution)/shard_map/ppermute | solution.py:28
  84.4 14.4 %collective-permute-start.5 = (bf16[7,160,256]{2,1,0:T(8,128)(2,1)S(1)}, bf16[7,160,256]{2,1,0:T(8,128)(2,1)S(1)}, u32[]{:S(2)}, u32[]{:S(2)}) collective-permute-start(bf16[7,160,256]{2,1,0:T(8,128)(2,1)S(1)} %get-tuple-element.51), channel_id=1, source_target_pairs={{4,0},{8,4},{12,8},{16,12},{20,16},{24,20},{28,24},{5,1},{9,5},{13... | collective-permute-start | bytes 1720328 | tf_op jit(solution)/shard_map/ppermute | solution.py:28
  105.2 7.9 %collective-permute-start.6 = (bf16[7,144,256]{2,1,0:T(8,128)(2,1)S(1)}, bf16[7,144,256]{2,1,0:T(8,128)(2,1)S(1)}, u32[]{:S(2)}, u32[]{:S(2)}) collective-permute-start(bf16[7,144,256]{2,1,0:T(8,128)(2,1)S(1)} %get-tuple-element.60), channel_id=1, source_target_pairs={{0,4},{4,8},{8,12},{12,16},{16,20},{20,24},{24,28},{1,5},{5,9},{9,... | collective-permute-start | bytes 1548296 | tf_op jit(solution)/shard_map/ppermute | solution.py:28
  107.2 12.1 %collective-permute-start.7 = (bf16[7,144,256]{2,1,0:T(8,128)(2,1)S(1)}, bf16[7,144,256]{2,1,0:T(8,128)(2,1)S(1)}, u32[]{:S(2)}, u32[]{:S(2)}) collective-permute-start(bf16[7,144,256]{2,1,0:T(8,128)(2,1)S(1)} %get-tuple-element.61), channel_id=1, source_target_pairs={{4,0},{8,4},{12,8},{16,12},{20,16},{24,20},{28,24},{5,1},{9,5},{13... | collective-permute-start | bytes 1548296 | tf_op jit(solution)/shard_map/ppermute | solution.py:28
  119.2 19.1 %copy-start.4 = (f32[16,160,256]{2,1,0:T(8,128)S(1)}, f32[16,160,256]{2,1,0:T(8,128)}, u32[]{:S(2)}) copy-start(f32[16,160,256]{2,1,0:T(8,128)} %copy-done.2) | copy-start | bytes 7864324
  119.3 19.1 %copy-start.6 = (f32[3,8,128,256]{3,2,1,0:T(8,128)S(1)}, f32[3,8,128,256]{3,2,1,0:T(8,128)}, u32[]{:S(2)}) copy-start(f32[3,8,128,256]{3,2,1,0:T(8,128)} %v.3) | copy-start | bytes 9437188
  125.1 7.9 %collective-permute-start.8 = (bf16[7,144,256]{2,1,0:T(8,128)(2,1)S(1)}, bf16[7,144,256]{2,1,0:T(8,128)(2,1)S(1)}, u32[]{:S(2)}, u32[]{:S(2)}) collective-permute-start(bf16[7,144,256]{2,1,0:T(8,128)(2,1)S(1)} %get-tuple-element.64), channel_id=1, source_target_pairs={{0,4},{4,8},{8,12},{12,16},{16,20},{20,24},{24,28},{1,5},{5,9},{9,... | collective-permute-start | bytes 1548296 | tf_op jit(solution)/shard_map/ppermute | solution.py:28
  127.1 11.3 %collective-permute-start.9 = (bf16[7,144,256]{2,1,0:T(8,128)(2,1)S(1)}, bf16[7,144,256]{2,1,0:T(8,128)(2,1)S(1)}, u32[]{:S(2)}, u32[]{:S(2)}) collective-permute-start(bf16[7,144,256]{2,1,0:T(8,128)(2,1)S(1)} %get-tuple-element.65), channel_id=1, source_target_pairs={{4,0},{8,4},{12,8},{16,12},{20,16},{24,20},{28,24},{5,1},{9,5},{13... | collective-permute-start | bytes 1548296 | tf_op jit(solution)/shard_map/ppermute | solution.py:28

commit v2 on v1

v2 whole, which is shorter than its diff:
```python
import functools

import jax
import jax.numpy as jnp
from jax import lax
from jax.experimental import pallas as pl
from jax.experimental.pallas import tpu as pltpu
from jax.sharding import PartitionSpec as P

TIME_STEP = 0.3
STEPS = 16
HX = 4
HY = 16
BAND = 128.0
LANES = 128
SUB = 8
CHUNK = 32
BLOCK = 2
S, C, K, B, O, A, AX, AY, AZ, D = range(10)
FIELDS = 10
BF16 = jnp.bfloat16
F32 = jnp.float32
VM = pl.BlockSpec(memory_space=pltpu.VMEM)
HBM = pl.BlockSpec(memory_space=pltpu.HBM)


def passed_along(value, axis, steps):
    count = lax.axis_size(axis)
    first, last = (max(0, -steps), min(count, count - steps))
    return lax.ppermute(value, axis, [(source, source + steps) for source in range(first, last)])


def params(mib):
    return pltpu.CompilerParams(vmem_limit_bytes=mib << 20)


def main_planes(planes):
    ahead = [(f, planes + skip, HX - skip) for f, skip in enumerate((0, 1, 1, 0))]
    behind = [(f, HX, HX - skip) for f, skip in enumerate((0, 1, 1, 1))]
    return ahead, behind


def unit_list(spans):
    return [(f, x) for f, first, count in spans for x in range(first, first + count)]


def pack_kernel(p, v, k, b, c, row_ahead, row_behind, plane_ahead, plane_behind, held, sems):
    planes, rows, depth = p.shape
    p_e, k_e, b_e = (held.at[i] for i in range(3, 6))

    def copies(x):
        pairs = [(v.at[i, x], held.at[i, x]) for i in range(3)]
        pairs = pairs + [(src.at[x], dst.at[x]) for src, dst in ((k, k_e), (p, p_e), (b, b_e))]
        return [pltpu.make_async_copy(src, dst, sems.at[i, x]) for i, (src, dst) in enumerate(pairs)]

    def start(x, _):
        for copy in copies(x):
            copy.start()
        return 0

    lax.fori_loop(0, planes, start, 0)
    fields = (p_e, c, k_e, b_e)

    def one_plane(x, _):
        for copy in copies(x):
            copy.wait()
        prev = jnp.maximum(x - 1, 0)
        for r in range(0, rows, CHUNK):
            sl = pl.ds(r, CHUNK)
            lane = lax.broadcasted_iota(jnp.int32, (CHUNK, depth), 1)
            row = lax.broadcasted_iota(jnp.int32, (CHUNK, depth), 0)
            vx, vy, vz = held[0, x, sl, :], held[1, x, sl, :], held[2, x, sl, :]
            vx_prev = jnp.where(x > 0, held[0, prev, sl, :], 0.0)
            above = jnp.zeros((1, depth), F32) if r == 0 else held[1, x, pl.ds(r - 1, 1), :]
            vy_prev = jnp.where(row == 0, above, pltpu.roll(vy, 1, 0))
            vz_prev = jnp.where(lane == 0, 0.0, pltpu.roll(vz, 1, 1))
            div = (vx - vx_prev) + (vy - vy_prev) + (vz - vz_prev)
            c[x, sl, :] = -TIME_STEP * k_e[x, sl, :] * div
        for f, field in enumerate(fields):
            row_ahead[f * planes + x] = field[x, pl.ds(rows - HY, HY), :].astype(BF16)
            row_behind[f * planes + x] = field[x, pl.ds(0, HY), :].astype(BF16)
        return 0

    lax.fori_loop(0, planes, one_plane, 0)
    ahead, behind = main_planes(planes)
    for out, spans in ((plane_ahead, ahead), (plane_behind, behind)):
        for i, (f, x) in enumerate(unit_list(spans)):
            out[i] = fields[f][x - HX].astype(BF16)
    plane_ahead[len(unit_list(ahead))] = held[0, planes - 1].astype(BF16)
    row_ahead[4 * planes] = held[0, planes - 1, pl.ds(rows - HY, HY), :].astype(BF16)
    row_behind[4 * planes] = held[0, planes - 1, pl.ds(0, HY), :].astype(BF16)
    edge = held[1, :, rows - 1, :]
    row_ahead[4 * planes + 1] = jnp.concatenate([edge, jnp.zeros((HY - planes, depth), F32)], 0).astype(BF16)


def corner_kernel(behind, ahead, own_ahead, own_behind, to_ahead, to_behind):
    planes = (behind.shape[0] - 2) // 4
    depth = behind.shape[2]
    row = lax.broadcasted_iota(jnp.int32, (HY, depth), 0)
    vy_behind = behind[4 * planes + 1].astype(F32)
    vy_last = own_ahead[4 * planes + 1].astype(F32)
    for out, spans in zip((to_ahead, to_behind), main_planes(planes)):
        units = unit_list(spans)
        deltas = []
        for i, (f, x) in enumerate(units):
            x = x - HX
            out[2 * i] = behind[f * planes + x]
            got = ahead[f * planes + x]
            if f == C:
                got = got.astype(F32)
                fix = TIME_STEP * ahead[K * planes + x].astype(F32) * vy_last[x : x + 1]
                got = jnp.where(row == 0, got + fix, got).astype(BF16)
                near = own_behind[K * planes + x].astype(F32)[:1]
                deltas.append(TIME_STEP * near * vy_behind[x : x + 1])
            out[2 * i + 1] = got
        deltas = jnp.concatenate(deltas + [jnp.zeros((HY - len(deltas), depth), F32)], 0)
        out[2 * len(units)] = deltas.astype(BF16)
    at = len(unit_list(main_planes(planes)[0]))
    to_ahead[2 * at + 1] = behind[4 * planes]
    to_ahead[2 * at + 2] = ahead[4 * planes]


def repeat_kernel(got, copies):
    for i in range(copies.shape[0]):
        copies[i] = got[...].reshape(copies.shape[1:])


def source_kernel(centre, routes, gathered, src, *, held):
    planes, rows, samples = src.shape
    groups, sensors, _ = gathered.shape
    slabs = sensors // held
    sensors = sensors * groups
    own_rows = rows - 2 * HY
    row_at = lax.axis_index("grp") * own_rows - HY + lax.broadcasted_iota(jnp.int32, (rows, sensors), 0)
    distance = jnp.abs(row_at - centre[...]).astype(F32)
    band = jnp.maximum(0.0, 1.0 - distance / BAND)
    band = jnp.where((row_at >= 0) & (row_at < own_rows * groups), band, 0.0).astype(BF16)
    parts = [gathered[g, pl.ds(held * t, held), :] for t in range(slabs) for g in range(groups)]
    ordered = jnp.concatenate(parts, 0)
    column = lax.broadcasted_iota(jnp.int32, (sensors, planes), 1)
    target = jnp.where(column < HX, -1, jnp.where(column < planes - HX, 0, 1)) + lax.axis_index("slab")
    weights = jnp.zeros((sensors, planes), F32)
    for i in range(routes.shape[1]):
        lat = ordered[:, samples + i * planes : samples + (i + 1) * planes].astype(F32)
        weights = weights + jnp.where(routes[:, i : i + 1] == target, lat, 0.0)
    trace = ordered[:, :samples].astype(F32)
    for x in range(1, planes - 1):
        outer = (weights[:, x : x + 1] * trace).astype(BF16)
        src[x] = TIME_STEP * jnp.dot(band, outer, preferred_element_type=F32)


def tile(x, t, h):
    return (x, pl.ds(SUB * t, SUB), pl.ds(LANES * h, LANES))


def advance_planes(s, o, coef, x, count, t0, t1):
    c, a, ax, ay, az, d = coef
    row = lax.broadcasted_iota(jnp.int32, (SUB, LANES), 0)
    lane = lax.broadcasted_iota(jnp.int32, (SUB, LANES), 1)
    halves = range(s.shape[2] // LANES)

    def around(t):
        here = [[s[tile(x + i, t, h)] for h in halves] for i in range(count)]
        up = [[pltpu.roll(v, SUB - 1, 0) for v in q] for q in here]
        down = [[pltpu.roll(v, 1, 0) for v in q] for q in here]
        return here, up, down

    here, up, down = around(t0)
    down_prev = down
    for t in range(t0, t1):
        later, up_next, down_next = around(t + 1) if t + 1 < t1 else (here, up, down)
        before = [s[tile(x - 1, t, h)] for h in halves]
        for i in range(count):
            now = here[i]
            after = here[i + 1] if i + 1 < count else [s[tile(x + count, t, h)] for h in halves]
            right = [pltpu.roll(v, LANES - 1, 1) for v in now] + [jnp.zeros((SUB, LANES), F32)]
            left = [pltpu.roll(v, 1, 1) for v in now]
            for h in halves:
                at = tile(x + i, t, h)
                y_next = jnp.where(row == SUB - 1, up_next[i][h], up[i][h])
                y_prev = jnp.where(row == 0, down_prev[i][h], down[i][h])
                z_next = jnp.where(lane == LANES - 1, right[h + 1], right[h])
                z_prev = left[0] if h == 0 else jnp.where(lane == 0, left[h - 1], left[h])
                moved = a[at] * (after[h] + y_next + z_next) + ax[at] * before[h]
                moved = moved + ay[at] * y_prev + az[at] * z_prev + d[at] * now[h]
                o[at] = moved + (c[at] - o[at])
            before = now
        here, up, down, down_prev = later, up_next, down_next, down


def advance_round(store, done):
    planes, rows = store.shape[1:3]
    fields = [store.at[S], store.at[O]]
    coef = [store.at[f] for f in (C, A, AX, AY, AZ, D)]
    for step in range(1, HX + 1):
        now, then = fields[(step - 1) % 2], fields[step % 2]
        skip = (done + step - 1) // SUB
        t0, t1 = skip, rows // SUB - skip

        def some_planes(i, _, now=now, then=then, step=step, t0=t0, t1=t1):
            advance_planes(now, then, coef, step + i * BLOCK, BLOCK, t0, t1)
            return 0

        lax.fori_loop(0, (planes - 2 * step) // BLOCK, some_planes, 0)


def pack_state(store, to_ahead, to_behind, skip):
    planes, rows = store.shape[1:3]
    own = planes - 2 * HX
    sl = pl.ds(skip, rows - 2 * skip)
    for i in range(HX):
        to_ahead[i] = store[S, own + i, sl, :].astype(BF16)
        to_behind[i] = store[S, HX + i, sl, :].astype(BF16)
    for i in range(1, HX):
        for out, x in ((to_ahead, own + i), (to_behind, HX + i - 1)):
            out[HX + i - 1] = (store[S, x, sl, :] - store[O, x, sl, :]).astype(BF16)


def first_round_kernel(*refs):
    given, (p, v, k, b, c, store, to_ahead, to_behind) = refs[:8], refs[8:16]
    taken, (line, sems) = refs[16:24], refs[24:]
    behind, ahead, corner_behind, corner_ahead, row_behind, row_ahead, own_ahead, src = taken
    takes = [pltpu.make_async_copy(given[i], taken[i], sems.at[5 + i]) for i in range(8)]
    planes, rows, depth = store.shape[1:]
    edge = planes - HX
    own_rows = rows - 2 * HY
    own = planes - 2 * HX
    low, middle, high = pl.ds(0, HY), pl.ds(HY, own_rows), pl.ds(HY + own_rows, HY)
    inner = pl.ds(HX, own)
    copies = [
        pltpu.make_async_copy(part, store.at[f, inner, middle, :], sems.at[f])
        for f, part in ((S, p), (C, c), (K, k), (B, b))
    ]
    copies.append(pltpu.make_async_copy(v.at[0, own - 1], line.at[middle, :], sems.at[4]))
    for copy in takes + copies:
        copy.start()
    for copy in takes:
        copy.wait()
    sent_ahead, sent_behind = main_planes(own)
    moves = ((behind, corner_behind, sent_ahead, -own), (ahead, corner_ahead, sent_behind, own))
    for main, corner, spans, shift in moves:
        units = unit_list(spans)
        for i, (f, x) in enumerate(units):
            store[f, x + shift, low, :] = corner[2 * i].astype(F32)
            store[f, x + shift, middle, :] = main[i].astype(F32)
            store[f, x + shift, high, :] = corner[2 * i + 1].astype(F32)
        _, x, count = spans[1]
        fixed = corner[2 * len(units)].astype(F32)
        for i in range(count):
            store[C, x + shift + i, pl.ds(HY, 1), :] += fixed[i : i + 1]
    for x in range(own):
        for f in (S, C, K, B):
            store[f, HX + x, low, :] = row_behind[f * own + x].astype(F32)
            store[f, HX + x, high, :] = row_ahead[f * own + x].astype(F32)
    line[low, :] = row_behind[4 * own].astype(F32)
    line[high, :] = row_ahead[4 * own].astype(F32)
    vy_behind = row_behind[4 * own + 1].astype(F32)
    vy_last = own_ahead[4 * own + 1].astype(F32)
    for copy in copies:
        copy.wait()
    for x in range(own):
        for at, vy in ((HY, vy_behind), (HY + own_rows, vy_last)):
            sl = pl.ds(at, 1)
            store[C, HX + x, sl, :] += TIME_STEP * store[K, HX + x, sl, :] * vy[x : x + 1]
    at = len(unit_list(sent_ahead))
    vx_parts = ((low, corner_behind[2 * at + 1]), (middle, behind[at]), (high, corner_behind[2 * at + 2]))
    for sl, part in vx_parts:
        store[C, HX, sl, :] += TIME_STEP * store[K, HX, sl, :] * part.astype(F32)
        store[C, edge, sl, :] += TIME_STEP * store[K, edge, sl, :] * line[sl, :]
    later = pl.ds(depth - src.shape[2], src.shape[2])

    def one_plane(x, _):
        for r in range(0, rows, CHUNK):
            sl = pl.ds(r, CHUNK)
            row = lax.broadcasted_iota(jnp.int32, (CHUNK, depth), 0)
            lane = lax.broadcasted_iota(jnp.int32, (CHUNK, depth), 1)
            kk = TIME_STEP * TIME_STEP * store[K, x, sl, :]
            bb = store[B, x, sl, :]
            b_x = store[B, x - 1, sl, :]
            above = store[B, x, pl.ds(max(r - 1, 0), 1), :]
            b_y = jnp.where(row == 0, above, pltpu.roll(bb, 1, 0))
            b_z = jnp.where(lane == 0, 0.0, pltpu.roll(bb, 1, 1))
            store[A, x, sl, :] = kk * bb
            store[AX, x, sl, :] = kk * b_x
            store[AY, x, sl, :] = kk * b_y
            store[AZ, x, sl, :] = kk * b_z
            store[D, x, sl, :] = 2.0 - kk * (3.0 * bb + b_x + b_y + b_z)
            store[O, x, sl, :] = jnp.zeros((CHUNK, depth), F32)
            store[C, x, sl, later] += src[x, sl, :]
        return 0

    lax.fori_loop(1, planes - 1, one_plane, 0)
    advance_round(store, 0)
    pack_state(store, to_ahead, to_behind, 0)


def take_halo(behind, ahead, store, skip):
    planes, rows = store.shape[1:3]
    edge = planes - HX
    sl = pl.ds(skip, rows - 2 * skip)
    for i in range(HX):
        store[S, i, sl, :] = behind[i].astype(F32)
        store[S, edge + i, sl, :] = ahead[i].astype(F32)
    for i in range(1, HX):
        for x, got in ((i, behind), (edge + i - 1, ahead)):
            store[O, x, sl, :] = store[S, x, sl, :] - got[HX + i - 1].astype(F32)


def middle_round_kernel(behind, ahead, store_i, store, to_ahead, to_behind, *, done, skips):
    del store_i
    take_halo(behind, ahead, store, skips[0])
    advance_round(store, done)
    pack_state(store, to_ahead, to_behind, skips[1])


def last_round_kernel(behind, ahead, v, store_i, p_out, v_out, store, held, in_sems, out_sems, *, done, skip):
    del store_i
    planes, rows, depth = p_out.shape
    own = pl.ds(HY, rows)

    def reads(x):
        return [pltpu.make_async_copy(v.at[i, x], held.at[i, x], in_sems.at[i, x]) for i in range(3)]

    def writes(x):
        pairs = [(f, v_out.at[i, x]) for i, f in enumerate((A, AX, AY))] + [(AZ, p_out.at[x])]
        return [
            pltpu.make_async_copy(store.at[f, HX + x, own, :], dst, out_sems.at[i, x])
            for i, (f, dst) in enumerate(pairs)
        ]

    def start(x, _):
        for copy in reads(x):
            copy.start()
        return 0

    lax.fori_loop(0, planes, start, 0)
    take_halo(behind, ahead, store, skip)
    advance_round(store, done)

    def one_plane(x, _):
        for copy in reads(x):
            copy.wait()
        for r in range(0, rows, CHUNK):
            sl, at = pl.ds(r, CHUNK), pl.ds(HY + r, CHUNK)
            row = lax.broadcasted_iota(jnp.int32, (CHUNK, depth), 0)
            lane = lax.broadcasted_iota(jnp.int32, (CHUNK, depth), 1)
            total = store[O, HX + x, at, :]
            below = store[O, HX + x, pl.ds(HY + r + CHUNK, 1), :]
            y_next = jnp.where(row == CHUNK - 1, below, pltpu.roll(total, CHUNK - 1, 0))
            z_next = jnp.where(lane == depth - 1, 0.0, pltpu.roll(total, depth - 1, 1))
            bb = TIME_STEP * store[B, HX + x, at, :]
            store[A, HX + x, at, :] = held[0, x, sl, :] - bb * (store[O, HX + x + 1, at, :] - total)
            store[AX, HX + x, at, :] = held[1, x, sl, :] - bb * (y_next - total)
            store[AY, HX + x, at, :] = held[2, x, sl, :] - bb * (z_next - total)
            store[AZ, HX + x, at, :] = store[S, HX + x, at, :] - total
        for copy in writes(x):
            copy.start()
        return 0

    lax.fori_loop(0, planes, one_plane, 0)

    def finish(x, _):
        for copy in writes(x):
            copy.wait()
        return 0

    lax.fori_loop(0, planes, finish, 0)


def local(pressure, velocity, stiffness, buoyancy, traces, lateral, routes, ycenter):
    planes, rows, depth = pressure.shape
    wide, tall = planes + 2 * HX, rows + 2 * HY
    store_shape = pltpu.VMEM((FIELDS, wide, tall, depth), F32)
    slabs, groups = lax.axis_size("slab"), lax.axis_size("grp")

    def sent(count, height):
        return jax.ShapeDtypeStruct((count, height, depth), BF16)

    def everyones(copies, axis):
        return lax.all_to_all(copies, axis, split_axis=0, concat_axis=0, tiled=True)

    lat = jnp.concatenate([lateral[:, :, planes - HX :], lateral, lateral[:, :, :HX]], 2)
    sensor_rows = jnp.concatenate([traces, lat.reshape(lat.shape[0], -1)], 1)
    copies = jnp.broadcast_to(sensor_rows[None], (slabs,) + sensor_rows.shape)
    copies, centre, routes, pressure = lax.optimization_barrier((copies, ycenter[None, :], routes, pressure))
    got = everyones(copies, "slab")

    n_rows = 4 * planes
    n_ahead, n_behind = [len(unit_list(spans)) for spans in main_planes(planes)]
    inputs = [pltpu.with_memory_space_constraint(x, pltpu.HBM) for x in (pressure, velocity, stiffness, buoyancy)]
    c, row_ahead, row_behind, plane_ahead, plane_behind = pl.pallas_call(
        pack_kernel,
        out_shape=(
            jax.ShapeDtypeStruct(pressure.shape, F32), sent(n_rows + 2, HY), sent(n_rows + 1, HY),
            sent(n_ahead + 1, rows), sent(n_behind, rows),
        ),
        in_specs=[HBM] * 4,
        out_specs=[VM] * 5,
        scratch_shapes=[pltpu.VMEM((6,) + pressure.shape, F32), pltpu.SemaphoreType.DMA((6, planes))],
        compiler_params=params(24),
    )(*inputs)
    main_behind = passed_along(plane_ahead, "slab", 1)
    main_ahead = passed_along(plane_behind, "slab", -1)
    from_behind = passed_along(row_ahead, "grp", 1)
    from_ahead = passed_along(row_behind, "grp", -1)

    copies = pl.pallas_call(
        repeat_kernel,
        out_shape=jax.ShapeDtypeStruct((groups, slabs * sensor_rows.shape[0], sensor_rows.shape[1]), BF16),
        in_specs=[VM],
        out_specs=VM,
        compiler_params=params(4),
    )(got)
    gathered = everyones(copies, "grp")

    corner_ahead, corner_behind = pl.pallas_call(
        corner_kernel,
        out_shape=(sent(2 * n_ahead + 3, HY), sent(2 * n_behind + 1, HY)),
        in_specs=[VM] * 4,
        out_specs=[VM] * 2,
        compiler_params=params(8),
    )(from_behind, from_ahead, row_ahead, row_behind)
    corner_from_behind = passed_along(corner_ahead, "slab", 1)
    corner_from_ahead = passed_along(corner_behind, "slab", -1)

    src = pl.pallas_call(
        functools.partial(source_kernel, held=traces.shape[0]),
        out_shape=jax.ShapeDtypeStruct((wide, tall, traces.shape[1]), F32),
        in_specs=[VM] * 3,
        out_specs=VM,
        compiler_params=params(16),
    )(centre, routes, gathered)

    given = (main_behind, main_ahead, corner_from_behind, corner_from_ahead, from_behind, from_ahead, row_ahead, src)
    store, plane_ahead, plane_behind = pl.pallas_call(
        first_round_kernel,
        out_shape=(store_shape, sent(2 * HX - 1, tall), sent(2 * HX - 1, tall)),
        in_specs=[HBM] * 13,
        out_specs=[VM] * 3,
        scratch_shapes=[pltpu.VMEM(x.shape, x.dtype) for x in given]
        + [pltpu.VMEM((tall, depth), F32), pltpu.SemaphoreType.DMA((5 + len(given),))],
        compiler_params=params(14),
    )(*[pltpu.with_memory_space_constraint(x, pltpu.HBM) for x in given + (*inputs, c)])

    rounds = STEPS // HX
    skips = [SUB * (HX * r // SUB) for r in range(1, rounds)]
    for r in range(1, rounds - 1):
        from_behind = passed_along(plane_ahead, "slab", 1)
        from_ahead = passed_along(plane_behind, "slab", -1)
        height = tall - 2 * skips[r]
        store, plane_ahead, plane_behind = pl.pallas_call(
            functools.partial(middle_round_kernel, done=HX * r, skips=skips[r - 1 : r + 1]),
            out_shape=(store_shape, sent(2 * HX - 1, height), sent(2 * HX - 1, height)),
            in_specs=[VM] * 3,
            out_specs=[VM] * 3,
            input_output_aliases={2: 0},
            compiler_params=params(14),
        )(from_behind, from_ahead, store)
    from_behind = passed_along(plane_ahead, "slab", 1)
    from_ahead = passed_along(plane_behind, "slab", -1)
    p_out, v_out, _ = pl.pallas_call(
        functools.partial(last_round_kernel, done=HX * (rounds - 1), skip=skips[-1]),
        out_shape=(
            jax.ShapeDtypeStruct(pressure.shape, F32),
            jax.ShapeDtypeStruct(velocity.shape, F32),
            store_shape,
        ),
        in_specs=[VM, VM, HBM, VM],
        out_specs=[HBM, HBM, VM],
        input_output_aliases={3: 2},
        scratch_shapes=[
            pltpu.VMEM(velocity.shape, F32),
            pltpu.SemaphoreType.DMA((3, planes)),
            pltpu.SemaphoreType.DMA((4, planes)),
        ],
        compiler_params=params(14),
    )(from_behind, from_ahead, inputs[1], store)
    return p_out, v_out


def solution(mesh):
    in_specs = (
        P("slab", "grp", None),
        P(None, "slab", "grp", None),
        P("slab", "grp", None),
        P("slab", "grp", None),
        P(("slab", "grp"), None),
        P(("slab", "grp"), None, None),
        P(),
        P(),
    )
    out_specs = (P("slab", "grp", None), P(None, "slab", "grp", None))
    return jax.shard_map(local, mesh=mesh, in_specs=in_specs, out_specs=out_specs, check_vma=False)
```

time: 148 us -> 138 us (0.932)
  blocking collectives: 28.4 us -> 0 us
  starting transfers between devices: 27.7 us -> 42.4 us
  waiting for transfers between devices: 38.6 us -> 44.7 us
  local copies, waits for them, and re-layouts: 13.9 us -> 7.9 us
  Pallas kernels: 37.4 us -> 40.2 us
    all_gather x2 -> x0, blocking collectives: 28.4 us -> none  [the longest x1 17.5 us: local(): gathered = lax.all_gather(gathered, 'slab', tiled=True)]
    all_to_all x0 -> x2, waiting for transfers between devices: none -> 13.3 us  [everyones(): return lax.all_to_all(copies, axis, split_axis=0, concat_axis=0, tiled=True)]
    unnamed x34 -> x14, local copies, waits for them, and re-layouts: 13.8 us -> 3.36 us
    all_to_all x0 -> x2, starting transfers between devices: none -> 8.96 us  [everyones(): return lax.all_to_all(copies, axis, split_axis=0, concat_axis=0, tiled=True)]
    ppermute x10 -> x12, waiting for transfers between devices: 38.6 us -> 31.4 us  [passed_along(): lax.ppermute(value, axis, [(source, source + steps) for source in range(f...]
    ppermute x10 -> x12, starting transfers between devices: 27.7 us -> 33.4 us  [passed_along(): lax.ppermute(value, axis, [(source, source + steps) for source in range(f...]
    pallas_call x4 -> x5, Pallas kernels: 16.5 us -> 19.6 us  [the longest x1 12.5 us: local(): pl.pallas_call(first_round_kernel, out_shape=(store_shape, sent(2 * HX -...]
  transfers between devices with their start and end apart: 10 -> 14, of which waited for: 7 -> 8; matrix products, arithmetic and copies ran while one was open for 0% -> 2% of each run, Pallas kernels for 2% -> 2%
where the time goes in v2:
time: 138 us; the launch traced here: 137 us
  waiting for transfers between devices  44.7 us (32%)
  starting transfers between devices  42.4 us (31%)
  Pallas kernels  40.2 us (29%)
  local copies, waits for them, and re-layouts  7.9 us (6%)
  other arithmetic  1.41 us (1%)
    ppermute x12, starting transfers between devices, passed_along(): lax.ppermute(value, axis, [(source, source + steps) for source in range(f...  33.4 us
    ppermute x12, waiting for transfers between devices, passed_along(): lax.ppermute(value, axis, [(source, source + steps) for source in range(f...  31.4 us
    all_to_all x2, waiting for transfers between devices, everyones(): return lax.all_to_all(copies, axis, split_axis=0, concat_axis=0, tiled=True)  13.3 us
    pallas_call x1, Pallas kernels, local(): pl.pallas_call(first_round_kernel, out_shape=(store_shape, sent(2 * HX -...  12.5 us
    pallas_call x2, Pallas kernels, local(): pl.pallas_call(functools.partial(middle_round_kernel, done=HX * r, skips=...  12.3 us
    all_to_all x2, starting transfers between devices, everyones(): return lax.all_to_all(copies, axis, split_axis=0, concat_axis=0, tiled=True)  8.96 us
    pallas_call x1, Pallas kernels, local(): pl.pallas_call(functools.partial(last_round_kernel, done=HX * (rounds - 1...  8.41 us
    pallas_call x1, Pallas kernels, local(): pl.pallas_call(pack_kernel, out_shape=(jax.ShapeDtypeStruct(pressure.shap...  4.41 us
  transfers between devices with their start and end apart: 14, of which 8 were waited for; matrix products, arithmetic and copies ran while one was open for 2% of the time, Pallas kernels for 2%

profile of v2, /device:TPU:1, one launch (start us, length us, event | category | flops | bytes accessed | tf_op | source)
XLA Modules:
  0.0 137.5 jit_solution(2174634878561476613)
XLA Ops:
  0.6 0.8 fusion
  1.4 0.7 pad_maximum_fusion.1
  2.1 0.1 copy.15
  2.2 0.7 pad_maximum_fusion
  2.9 0.7 broadcast_in_dim.4
  3.6 4.4 %shard_map.95 = (f32[8,128,256]{2,1,0:T(8,128)S(1)}, bf16[34,16,256]{2,1,0:T(8,128)(2,1)S(1)}, bf16[33,16,256]{2,1,0:T(8,128)(2,1)S(1)}, bf16[15,128,256]{2,1,0:T(8,128)(2,1)S(1)}, bf16[13,128,256]{2,1,0:T(8,128)(2,1)}) custom-call(f32[8,128,256]{2,1,0:T(8,128)} %refs_8_, f32[3,8,128,256]{3,2,1,0:T(8,128)} %v.3, f32[8,128,256]{2,1,0:T(8,128)} %refs_10_.1, ...), custom_call_target="tpu_custom_call" | custom-call | tf_op jit(solution)/shard_map/pallas_call | solution.py:391
  8.0 0.0 copy-start.4
  8.0 1.0 copy-done.4
  8.9 0.0 copy-start.1
  9.0 4.5 %collective-permute-start = (bf16[15,128,256]{2,1,0:T(8,128)(2,1)S(1)}, bf16[15,128,256]{2,1,0:T(8,128)(2,1)}, u32[]{:S(2)}, u32[]{:S(2)}) collective-permute-start(bf16[15,128,256]{2,1,0:T(8,128)(2,1)S(1)} %get-tuple-element.25), channel_id=1, source_target_pairs={{0,4},{4,8},{8,12},{12,16},{16,20},{20,24},{24,28},{1,5},{5,9},{9,... | collective-permute-start | bytes 2949128 | tf_op jit(solution)/shard_map/ppermute | solution.py:30
  13.5 1.9 %collective-permute-start.1 = (bf16[13,128,256]{2,1,0:T(8,128)(2,1)}, bf16[13,128,256]{2,1,0:T(8,128)(2,1)}, u32[]{:S(2)}, u32[]{:S(2)}) collective-permute-start(bf16[13,128,256]{2,1,0:T(8,128)(2,1)} %get-tuple-element.26), channel_id=1, source_target_pairs={{4,0},{8,4},{12,8},{16,12},{20,16},{24,20},{28,24},{5,1},{9,5},{13... | collective-permute-start | bytes 2555912 | tf_op jit(solution)/shard_map/ppermute | solution.py:30
  15.4 4.4 %all-to-all-start = ((bf16[8,32,160]{2,1,0:T(8,128)(2,1)}), bf16[8,32,160]{2,1,0:T(8,128)(2,1)S(1)}, u32[]{:S(2)}, u32[]{:S(2)}) async-start(bf16[8,32,160]{2,1,0:T(8,128)(2,1)} %broadcast_in_dim.4), calls=%async_computation | async-start | bytes 262144 | tf_op jit(solution)/shard_map/all_to_all | solution.py:380
  19.8 3.2 %collective-permute-start.2 = (bf16[34,16,256]{2,1,0:T(8,128)(2,1)S(1)}, bf16[34,16,256]{2,1,0:T(8,128)(2,1)S(1)}, u32[]{:S(2)}, u32[]{:S(2)}) collective-permute-start(bf16[34,16,256]{2,1,0:T(8,128)(2,1)S(1)} %get-tuple-element.27.own_ahead.refs_6_), channel_id=1, source_target_pairs={{0,1},{1,2},{2,3},{4,5},{5,6},{6,7},{8,9},{9,10},{10,11},{12,13},{... | collective-permute-start | bytes 835592 | tf_op jit(solution)/shard_map/ppermute | solution.py:30
  23.0 1.3 collective-permute-start.3
  24.3 11.9 %all-to-all-done.got = bf16[8,32,160]{2,1,0:T(8,128)(2,1)S(1)} async-done(((bf16[8,32,160]{2,1,0:T(8,128)(2,1)}), bf16[8,32,160]{2,1,0:T(8,128)(2,1)S(1)}, u32[]{:S(2)}, u32[]{:S(2)}) %all-to-all-start) | async-done | bytes 81952 | tf_op jit(solution)/shard_map/all_to_all | solution.py:380
  36.2 0.9 copy.16
  37.1 4.6 %all-to-all-start.1 = ((bf16[4,256,160]{1,2,0:T(8,128)(2,1)}), bf16[4,256,160]{1,2,0:T(8,128)(2,1)}, u32[]{:S(2)}, u32[]{:S(2)}) async-start(bf16[4,256,160]{1,2,0:T(8,128)(2,1)} %copy.16), calls=%async_computation.1 | async-start | bytes 655360 | tf_op jit(solution)/shard_map/all_to_all | solution.py:380
  41.7 0.0 collective-permute-done.3.ahead.refs_5_
  41.7 0.0 copy-start.3
  41.7 0.0 collective-permute-done.2.behind.refs_4_
  41.7 0.0 copy-start.2
  41.8 4.3 %collective-permute-start.4 = (bf16[31,16,256]{2,1,0:T(8,128)(2,1)S(1)}, bf16[31,16,256]{2,1,0:T(8,128)(2,1)}, u32[]{:S(2)}, u32[]{:S(2)}) collective-permute-start(bf16[31,16,256]{2,1,0:T(8,128)(2,1)S(1)} %get-tuple-element.29), channel_id=1, source_target_pairs={{0,4},{4,8},{8,12},{12,16},{16,20},{20,24},{24,28},{1,5},{5,9},{9,... | collective-permute-start | bytes 761864 | tf_op jit(solution)/shard_map/ppermute | solution.py:30
  46.1 1.9 %collective-permute-start.5 = (bf16[27,16,256]{2,1,0:T(8,128)(2,1)S(1)}, bf16[27,16,256]{2,1,0:T(8,128)(2,1)S(1)}, u32[]{:S(2)}, u32[]{:S(2)}) collective-permute-start(bf16[27,16,256]{2,1,0:T(8,128)(2,1)S(1)} %get-tuple-element.30), channel_id=1, source_target_pairs={{4,0},{8,4},{12,8},{16,12},{20,16},{24,20},{28,24},{5,1},{9,5},{13... | collective-permute-start | bytes 663560 | tf_op jit(solution)/shard_map/ppermute | solution.py:30
  48.0 0.9 copy.17.routes
  49.0 1.5 %all-to-all-done.1 = bf16[4,256,160]{1,2,0:T(8,128)(2,1)} async-done(((bf16[4,256,160]{1,2,0:T(8,128)(2,1)}), bf16[4,256,160]{1,2,0:T(8,128)(2,1)}, u32[]{:S(2)}, u32[]{:S(2)}) %all-to-all-start.1) | async-done | bytes 327712 | tf_op jit(solution)/shard_map/all_to_all | solution.py:380
  50.4 1.2 copy.18.gathered
  51.6 0.0 copy-start.5
  51.6 0.7 copy-done.5
  52.3 2.6 %shard_map.98.refs_7_ = f32[16,160,128]{2,1,0:T(8,128)S(1)} custom-call(s32[1,1024]{1,0:T(1,128)S(1)} %bitcast.2, s32[1024,2]{1,0:T(8,128)S(1)} %copy.17.routes, bf16[4,256,160]{2,1,0:T(8,128)(2,1)S(1)} %copy.18.gathered), custom_call_target="tpu_custom_call" | custom-call | tf_op jit(solution)/shard_map/pallas_call | solution.py:426
  54.9 0.0 copy-start
  54.9 1.1 copy-done
  55.9 0.0 collective-permute-done.5.refs_3_
  55.9 0.0 copy-start.6
  55.9 0.0 collective-permute-done.4.refs_2_
  55.9 0.0 collective-permute-done.1.refs_1_
  55.9 0.0 collective-permute-done.refs_0_
  55.9 0.0 copy-done.1
  56.0 0.0 copy-done.3
  56.0 0.0 copy-done.2
  56.0 0.6 copy-done.6
  56.6 12.5 %shard_map.99 = (f32[10,16,160,256]{3,2,1,0:T(8,128)S(1)}, bf16[7,160,256]{2,1,0:T(8,128)(2,1)S(1)}, bf16[7,160,256]{2,1,0:T(8,128)(2,1)S(1)}) custom-call(bf16[15,128,256]{2,1,0:T(8,128)(2,1)} %collective-permute-done.refs_0_, bf16[13,128,256]{2,1,0:T(8,128)(2,1)} %collective-permute-done.1.refs_1_, bf16[31,16,256]{2,1,0:T(8,128)(2,1)} %collective-permute-done.4.refs_2_, ...), custom_call_target="tpu_custom_call" | custom-call | tf_op jit(solution)/shard_map/pallas_call | solution.py:435
  69.1 5.6 %collective-permute-start.6 = (bf16[7,160,256]{2,1,0:T(8,128)(2,1)S(1)}, bf16[7,160,256]{2,1,0:T(8,128)(2,1)S(1)}, u32[]{:S(2)}, u32[]{:S(2)}) collective-permute-start(bf16[7,160,256]{2,1,0:T(8,128)(2,1)S(1)} %get-tuple-element.35), channel_id=1, source_target_pairs={{0,4},{4,8},{8,12},{12,16},{16,20},{20,24},{24,28},{1,5},{5,9},{9,... | collective-permute-start | bytes 1720328 | tf_op jit(solution)/shard_map/ppermute | solution.py:30
  74.8 1.9 %collective-permute-start.7 = (bf16[7,160,256]{2,1,0:T(8,128)(2,1)S(1)}, bf16[7,160,256]{2,1,0:T(8,128)(2,1)S(1)}, u32[]{:S(2)}, u32[]{:S(2)}) collective-permute-start(bf16[7,160,256]{2,1,0:T(8,128)(2,1)S(1)} %get-tuple-element.36), channel_id=1, source_target_pairs={{4,0},{8,4},{12,8},{16,12},{20,16},{24,20},{28,24},{5,1},{9,5},{13... | collective-permute-start | bytes 1720328 | tf_op jit(solution)/shard_map/ppermute | solution.py:30
  76.7 4.7 %collective-permute-done.6.behind = bf16[7,160,256]{2,1,0:T(8,128)(2,1)S(1)} collective-permute-done((bf16[7,160,256]{2,1,0:T(8,128)(2,1)S(1)}, bf16[7,160,256]{2,1,0:T(8,128)(2,1)S(1)}, u32[]{:S(2)}, u32[]{:S(2)}) %collective-permute-start.6) | collective-permute-done | bytes 573472 | tf_op jit(solution)/shard_map/ppermute | solution.py:30
  81.4 7.9 %collective-permute-done.7.ahead = bf16[7,160,256]{2,1,0:T(8,128)(2,1)S(1)} collective-permute-done((bf16[7,160,256]{2,1,0:T(8,128)(2,1)S(1)}, bf16[7,160,256]{2,1,0:T(8,128)(2,1)S(1)}, u32[]{:S(2)}, u32[]{:S(2)}) %collective-permute-start.7) | collective-permute-done | bytes 573472 | tf_op jit(solution)/shard_map/ppermute | solution.py:30
  89.3 6.4 %shard_map.100 = (f32[10,16,160,256]{3,2,1,0:T(8,128)S(1)}, bf16[7,144,256]{2,1,0:T(8,128)(2,1)S(1)}, bf16[7,144,256]{2,1,0:T(8,128)(2,1)S(1)}) custom-call(bf16[7,160,256]{2,1,0:T(8,128)(2,1)S(1)} %collective-permute-done.6.behind, bf16[7,160,256]{2,1,0:T(8,128)(2,1)S(1)} %collective-permute-done.7.ahead, ...), custom_call_target="tpu_custom_call", output_to_operand_aliasing={{0}: (2, {})} | custom-call | tf_op jit(solution)/shard_map/pallas_call | solution.py:451
  95.7 1.9 %collective-permute-start.8 = (bf16[7,144,256]{2,1,0:T(8,128)(2,1)S(1)}, bf16[7,144,256]{2,1,0:T(8,128)(2,1)S(1)}, u32[]{:S(2)}, u32[]{:S(2)}) collective-permute-start(bf16[7,144,256]{2,1,0:T(8,128)(2,1)S(1)} %get-tuple-element.38), channel_id=1, source_target_pairs={{0,4},{4,8},{8,12},{12,16},{16,20},{20,24},{24,28},{1,5},{5,9},{9,... | collective-permute-start | bytes 1548296 | tf_op jit(solution)/shard_map/ppermute | solution.py:30
  97.7 2.4 %collective-permute-start.9 = (bf16[7,144,256]{2,1,0:T(8,128)(2,1)S(1)}, bf16[7,144,256]{2,1,0:T(8,128)(2,1)S(1)}, u32[]{:S(2)}, u32[]{:S(2)}) collective-permute-start(bf16[7,144,256]{2,1,0:T(8,128)(2,1)S(1)} %get-tuple-element.39), channel_id=1, source_target_pairs={{4,0},{8,4},{12,8},{16,12},{20,16},{24,20},{28,24},{5,1},{9,5},{13... | collective-permute-start | bytes 1548296 | tf_op jit(solution)/shard_map/ppermute | solution.py:30
  100.1 3.6 %collective-permute-done.8.behind = bf16[7,144,256]{2,1,0:T(8,128)(2,1)S(1)} collective-permute-done((bf16[7,144,256]{2,1,0:T(8,128)(2,1)S(1)}, bf16[7,144,256]{2,1,0:T(8,128)(2,1)S(1)}, u32[]{:S(2)}, u32[]{:S(2)}) %collective-permute-start.8) | collective-permute-done | bytes 516128 | tf_op jit(solution)/shard_map/ppermute | solution.py:30
  103.7 6.3 %collective-permute-done.9.ahead = bf16[7,144,256]{2,1,0:T(8,128)(2,1)S(1)} collective-permute-done((bf16[7,144,256]{2,1,0:T(8,128)(2,1)S(1)}, bf16[7,144,256]{2,1,0:T(8,128)(2,1)S(1)}, u32[]{:S(2)}, u32[]{:S(2)}) %collective-permute-start.9) | collective-permute-done | bytes 516128 | tf_op jit(solution)/shard_map/ppermute | solution.py:30
  110.0 5.9 %shard_map.101 = (f32[10,16,160,256]{3,2,1,0:T(8,128)S(1)}, bf16[7,144,256]{2,1,0:T(8,128)(2,1)S(1)}, bf16[7,144,256]{2,1,0:T(8,128)(2,1)S(1)}) custom-call(bf16[7,144,256]{2,1,0:T(8,128)(2,1)S(1)} %collective-permute-done.8.behind, bf16[7,144,256]{2,1,0:T(8,128)(2,1)S(1)} %collective-permute-done.9.ahead, ...), custom_call_target="tpu_custom_call", output_to_operand_aliasing={{0}: (2, {})} | custom-call | tf_op jit(solution)/shard_map/pallas_call | solution.py:451
  115.8 1.9 %collective-permute-start.10 = (bf16[7,144,256]{2,1,0:T(8,128)(2,1)S(1)}, bf16[7,144,256]{2,1,0:T(8,128)(2,1)S(1)}, u32[]{:S(2)}, u32[]{:S(2)}) collective-permute-start(bf16[7,144,256]{2,1,0:T(8,128)(2,1)S(1)} %get-tuple-element.41), channel_id=1, source_target_pairs={{0,4},{4,8},{8,12},{12,16},{16,20},{20,24},{24,28},{1,5},{5,9},{9,... | collective-permute-start | bytes 1548296 | tf_op jit(solution)/shard_map/ppermute | solution.py:30
  117.8 2.4 %collective-permute-start.11 = (bf16[7,144,256]{2,1,0:T(8,128)(2,1)S(1)}, bf16[7,144,256]{2,1,0:T(8,128)(2,1)S(1)}, u32[]{:S(2)}, u32[]{:S(2)}) collective-permute-start(bf16[7,144,256]{2,1,0:T(8,128)(2,1)S(1)} %get-tuple-element.42), channel_id=1, source_target_pairs={{4,0},{8,4},{12,8},{16,12},{20,16},{24,20},{28,24},{5,1},{9,5},{13... | collective-permute-start | bytes 1548296 | tf_op jit(solution)/shard_map/ppermute | solution.py:30
  120.2 3.6 %collective-permute-done.10.behind = bf16[7,144,256]{2,1,0:T(8,128)(2,1)S(1)} collective-permute-done((bf16[7,144,256]{2,1,0:T(8,128)(2,1)S(1)}, bf16[7,144,256]{2,1,0:T(8,128)(2,1)S(1)}, u32[]{:S(2)}, u32[]{:S(2)}) %collective-permute-start.10) | collective-permute-done | bytes 516128 | tf_op jit(solution)/shard_map/ppermute | solution.py:30
  123.8 5.3 %collective-permute-done.11.ahead = bf16[7,144,256]{2,1,0:T(8,128)(2,1)S(1)} collective-permute-done((bf16[7,144,256]{2,1,0:T(8,128)(2,1)S(1)}, bf16[7,144,256]{2,1,0:T(8,128)(2,1)S(1)}, u32[]{:S(2)}, u32[]{:S(2)}) %collective-permute-start.11) | collective-permute-done | bytes 516128 | tf_op jit(solution)/shard_map/ppermute | solution.py:30
  129.1 8.4 %shard_map.102 = (f32[8,128,256]{2,1,0:T(8,128)}, f32[3,8,128,256]{3,2,1,0:T(8,128)}, f32[10,16,160,256]{3,2,1,0:T(8,128)S(1)}) custom-call(bf16[7,144,256]{2,1,0:T(8,128)(2,1)S(1)} %collective-permute-done.10.behind, bf16[7,144,256]{2,1,0:T(8,128)(2,1)S(1)} %collective-permute-done.11.ahead, f32[3,8,128,256]{3,2,1,0:T(8,128)} %v.3, ...), custom_call_target="tpu_custom_call", output_to_operand_aliasing={{2}: (3, {})} | custom-call | tf_op jit(solution)/shard_map/pallas_call | solution.py:461
  (2 shorter events, 0.1 us)
Async XLA Ops:
  8.0 1.0 copy-start.4
  8.9 47.0 %copy-start.1 = (bf16[34,16,256]{2,1,0:T(8,128)(2,1)}, bf16[34,16,256]{2,1,0:T(8,128)(2,1)S(1)}, u32[]{:S(2)}) copy-start(bf16[34,16,256]{2,1,0:T(8,128)(2,1)S(1)} %get-tuple-element.27.own_ahead.refs_6_) | copy-start | bytes 835588
  9.0 47.0 %collective-permute-start = (bf16[15,128,256]{2,1,0:T(8,128)(2,1)S(1)}, bf16[15,128,256]{2,1,0:T(8,128)(2,1)}, u32[]{:S(2)}, u32[]{:S(2)}) collective-permute-start(bf16[15,128,256]{2,1,0:T(8,128)(2,1)S(1)} %get-tuple-element.25), channel_id=1, source_target_pairs={{0,4},{4,8},{8,12},{12,16},{16,20},{20,24},{24,28},{1,5},{5,9},{9,... | collective-permute-start | bytes 2949128 | tf_op jit(solution)/shard_map/ppermute | solution.py:30
  13.5 42.5 %collective-permute-start.1 = (bf16[13,128,256]{2,1,0:T(8,128)(2,1)}, bf16[13,128,256]{2,1,0:T(8,128)(2,1)}, u32[]{:S(2)}, u32[]{:S(2)}) collective-permute-start(bf16[13,128,256]{2,1,0:T(8,128)(2,1)} %get-tuple-element.26), channel_id=1, source_target_pairs={{4,0},{8,4},{12,8},{16,12},{20,16},{24,20},{28,24},{5,1},{9,5},{13... | collective-permute-start | bytes 2555912 | tf_op jit(solution)/shard_map/ppermute | solution.py:30
  15.4 20.7 %all-to-all-start = ((bf16[8,32,160]{2,1,0:T(8,128)(2,1)}), bf16[8,32,160]{2,1,0:T(8,128)(2,1)S(1)}, u32[]{:S(2)}, u32[]{:S(2)}) async-start(bf16[8,32,160]{2,1,0:T(8,128)(2,1)} %broadcast_in_dim.4), calls=%async_computation | async-start | bytes 262144 | tf_op jit(solution)/shard_map/all_to_all | solution.py:380
  19.8 21.9 %collective-permute-start.2 = (bf16[34,16,256]{2,1,0:T(8,128)(2,1)S(1)}, bf16[34,16,256]{2,1,0:T(8,128)(2,1)S(1)}, u32[]{:S(2)}, u32[]{:S(2)}) collective-permute-start(bf16[34,16,256]{2,1,0:T(8,128)(2,1)S(1)} %get-tuple-element.27.own_ahead.refs_6_), channel_id=1, source_target_pairs={{0,1},{1,2},{2,3},{4,5},{5,6},{6,7},{8,9},{9,10},{10,11},{12,13},{... | collective-permute-start | bytes 835592 | tf_op jit(solution)/shard_map/ppermute | solution.py:30
  23.0 18.7 %collective-permute-start.3 = (bf16[33,16,256]{2,1,0:T(8,128)(2,1)S(1)}, bf16[33,16,256]{2,1,0:T(8,128)(2,1)S(1)}, u32[]{:S(2)}, u32[]{:S(2)}) collective-permute-start(bf16[33,16,256]{2,1,0:T(8,128)(2,1)S(1)} %get-tuple-element.28.own_behind), channel_id=1, source_target_pairs={{1,0},{2,1},{3,2},{5,4},{6,5},{7,6},{9,8},{10,9},{11,10},{13,12},{... | collective-permute-start | bytes 811016 | tf_op jit(solution)/shard_map/ppermute | solution.py:30
  37.1 13.3 %all-to-all-start.1 = ((bf16[4,256,160]{1,2,0:T(8,128)(2,1)}), bf16[4,256,160]{1,2,0:T(8,128)(2,1)}, u32[]{:S(2)}, u32[]{:S(2)}) async-start(bf16[4,256,160]{1,2,0:T(8,128)(2,1)} %copy.16), calls=%async_computation.1 | async-start | bytes 655360 | tf_op jit(solution)/shard_map/all_to_all | solution.py:380
  41.7 14.3 %copy-start.3 = (bf16[33,16,256]{2,1,0:T(8,128)(2,1)}, bf16[33,16,256]{2,1,0:T(8,128)(2,1)S(1)}, u32[]{:S(2)}) copy-start(bf16[33,16,256]{2,1,0:T(8,128)(2,1)S(1)} %collective-permute-done.3.ahead.refs_5_) | copy-start | bytes 811012
  41.7 14.3 %copy-start.2 = (bf16[34,16,256]{2,1,0:T(8,128)(2,1)}, bf16[34,16,256]{2,1,0:T(8,128)(2,1)S(1)}, u32[]{:S(2)}) copy-start(bf16[34,16,256]{2,1,0:T(8,128)(2,1)S(1)} %collective-permute-done.2.behind.refs_4_) | copy-start | bytes 835588
  41.8 14.2 %collective-permute-start.4 = (bf16[31,16,256]{2,1,0:T(8,128)(2,1)S(1)}, bf16[31,16,256]{2,1,0:T(8,128)(2,1)}, u32[]{:S(2)}, u32[]{:S(2)}) collective-permute-start(bf16[31,16,256]{2,1,0:T(8,128)(2,1)S(1)} %get-tuple-element.29), channel_id=1, source_target_pairs={{0,4},{4,8},{8,12},{12,16},{16,20},{20,24},{24,28},{1,5},{5,9},{9,... | collective-permute-start | bytes 761864 | tf_op jit(solution)/shard_map/ppermute | solution.py:30
  46.1 9.8 %collective-permute-start.5 = (bf16[27,16,256]{2,1,0:T(8,128)(2,1)S(1)}, bf16[27,16,256]{2,1,0:T(8,128)(2,1)S(1)}, u32[]{:S(2)}, u32[]{:S(2)}) collective-permute-start(bf16[27,16,256]{2,1,0:T(8,128)(2,1)S(1)} %get-tuple-element.30), channel_id=1, source_target_pairs={{4,0},{8,4},{12,8},{16,12},{20,16},{24,20},{28,24},{5,1},{9,5},{13... | collective-permute-start | bytes 663560 | tf_op jit(solution)/shard_map/ppermute | solution.py:30
  51.6 0.7 copy-start.5
  54.9 1.1 copy-start
  55.9 0.7 copy-start.6
  69.1 12.3 %collective-permute-start.6 = (bf16[7,160,256]{2,1,0:T(8,128)(2,1)S(1)}, bf16[7,160,256]{2,1,0:T(8,128)(2,1)S(1)}, u32[]{:S(2)}, u32[]{:S(2)}) collective-permute-start(bf16[7,160,256]{2,1,0:T(8,128)(2,1)S(1)} %get-tuple-element.35), channel_id=1, source_target_pairs={{0,4},{4,8},{8,12},{12,16},{16,20},{20,24},{24,28},{1,5},{5,9},{9,... | collective-permute-start | bytes 1720328 | tf_op jit(solution)/shard_map/ppermute | solution.py:30
  74.8 14.5 %collective-permute-start.7 = (bf16[7,160,256]{2,1,0:T(8,128)(2,1)S(1)}, bf16[7,160,256]{2,1,0:T(8,128)(2,1)S(1)}, u32[]{:S(2)}, u32[]{:S(2)}) collective-permute-start(bf16[7,160,256]{2,1,0:T(8,128)(2,1)S(1)} %get-tuple-element.36), channel_id=1, source_target_pairs={{4,0},{8,4},{12,8},{16,12},{20,16},{24,20},{28,24},{5,1},{9,5},{13... | collective-permute-start | bytes 1720328 | tf_op jit(solution)/shard_map/ppermute | solution.py:30
  95.7 7.9 %collective-permute-start.8 = (bf16[7,144,256]{2,1,0:T(8,128)(2,1)S(1)}, bf16[7,144,256]{2,1,0:T(8,128)(2,1)S(1)}, u32[]{:S(2)}, u32[]{:S(2)}) collective-permute-start(bf16[7,144,256]{2,1,0:T(8,128)(2,1)S(1)} %get-tuple-element.38), channel_id=1, source_target_pairs={{0,4},{4,8},{8,12},{12,16},{16,20},{20,24},{24,28},{1,5},{5,9},{9,... | collective-permute-start | bytes 1548296 | tf_op jit(solution)/shard_map/ppermute | solution.py:30
  97.7 12.3 %collective-permute-start.9 = (bf16[7,144,256]{2,1,0:T(8,128)(2,1)S(1)}, bf16[7,144,256]{2,1,0:T(8,128)(2,1)S(1)}, u32[]{:S(2)}, u32[]{:S(2)}) collective-permute-start(bf16[7,144,256]{2,1,0:T(8,128)(2,1)S(1)} %get-tuple-element.39), channel_id=1, source_target_pairs={{4,0},{8,4},{12,8},{16,12},{20,16},{24,20},{28,24},{5,1},{9,5},{13... | collective-permute-start | bytes 1548296 | tf_op jit(solution)/shard_map/ppermute | solution.py:30
  115.8 7.9 %collective-permute-start.10 = (bf16[7,144,256]{2,1,0:T(8,128)(2,1)S(1)}, bf16[7,144,256]{2,1,0:T(8,128)(2,1)S(1)}, u32[]{:S(2)}, u32[]{:S(2)}) collective-permute-start(bf16[7,144,256]{2,1,0:T(8,128)(2,1)S(1)} %get-tuple-element.41), channel_id=1, source_target_pairs={{0,4},{4,8},{8,12},{12,16},{16,20},{20,24},{24,28},{1,5},{5,9},{9,... | collective-permute-start | bytes 1548296 | tf_op jit(solution)/shard_map/ppermute | solution.py:30
  117.8 11.3 %collective-permute-start.11 = (bf16[7,144,256]{2,1,0:T(8,128)(2,1)S(1)}, bf16[7,144,256]{2,1,0:T(8,128)(2,1)S(1)}, u32[]{:S(2)}, u32[]{:S(2)}) collective-permute-start(bf16[7,144,256]{2,1,0:T(8,128)(2,1)S(1)} %get-tuple-element.42), channel_id=1, source_target_pairs={{4,0},{8,4},{12,8},{16,12},{20,16},{24,20},{28,24},{5,1},{9,5},{13... | collective-permute-start | bytes 1548296 | tf_op jit(solution)/shard_map/ppermute | solution.py:30

commit v3 on v2

--- a/solution.py
+++ b/solution.py
@@ -120,33 +120,30 @@
     to_ahead[2 * at + 2] = ahead[4 * planes]
 
 
-def repeat_kernel(got, copies):
+def sensors_kernel(traces, lateral, copies):
+    own = traces.shape[0]
     for i in range(copies.shape[0]):
-        copies[i] = got[...].reshape(copies.shape[1:])
-
-
-def source_kernel(centre, routes, gathered, src, *, held):
-    planes, rows, samples = src.shape
-    groups, sensors, _ = gathered.shape
-    slabs = sensors // held
-    sensors = sensors * groups
-    own_rows = rows - 2 * HY
-    row_at = lax.axis_index("grp") * own_rows - HY + lax.broadcasted_iota(jnp.int32, (rows, sensors), 0)
-    distance = jnp.abs(row_at - centre[...]).astype(F32)
-    band = jnp.maximum(0.0, 1.0 - distance / BAND)
-    band = jnp.where((row_at >= 0) & (row_at < own_rows * groups), band, 0.0).astype(BF16)
-    parts = [gathered[g, pl.ds(held * t, held), :] for t in range(slabs) for g in range(groups)]
-    ordered = jnp.concatenate(parts, 0)
-    column = lax.broadcasted_iota(jnp.int32, (sensors, planes), 1)
-    target = jnp.where(column < HX, -1, jnp.where(column < planes - HX, 0, 1)) + lax.axis_index("slab")
-    weights = jnp.zeros((sensors, planes), F32)
-    for i in range(routes.shape[1]):
-        lat = ordered[:, samples + i * planes : samples + (i + 1) * planes].astype(F32)
-        weights = weights + jnp.where(routes[:, i : i + 1] == target, lat, 0.0)
-    trace = ordered[:, :samples].astype(F32)
-    for x in range(1, planes - 1):
-        outer = (weights[:, x : x + 1] * trace).astype(BF16)
-        src[x] = TIME_STEP * jnp.dot(band, outer, preferred_element_type=F32)
+        copies[i, pl.ds(0, own), :] = traces[...]
+        copies[i, pl.ds(own, lateral.shape[0]), :] = jnp.zeros((lateral.shape[0], copies.shape[2]), BF16)
+        copies[i, pl.ds(own, lateral.shape[0]), pl.ds(0, own)] = lateral[...]
+
+
+def repeat_kernel(got, copies, *, own):
+    slabs, height, samples = got.shape
+    rows = got[:, :own, :].astype(F32).reshape(slabs * own, samples)
+    traces = jnp.transpose(rows).astype(BF16)
+    per = LANES // own
+    weights = []
+    for first in range(0, slabs, per):
+        part = jnp.zeros((height - own, samples), F32)
+        for i in range(per):
+            piece = got[first + i, pl.ds(own, height - own), :].astype(F32)
+            part = part + (pltpu.roll(piece, own * i, 1) if i else piece)
+        weights.append(part)
+    weights = jnp.concatenate(weights, 1).astype(BF16)
+    for g in range(copies.shape[0]):
+        copies[g, pl.ds(0, samples), :] = traces
+        copies[g, pl.ds(samples, height - own), :] = weights
 
 
 def tile(x, t, h):
@@ -188,20 +185,26 @@
         here, up, down, down_prev = later, up_next, down_next, down
 
 
-def advance_round(store, done):
+def advance_some(store, done, inner):
     planes, rows = store.shape[1:3]
     fields = [store.at[S], store.at[O]]
     coef = [store.at[f] for f in (C, A, AX, AY, AZ, D)]
+    edge = planes - HX
     for step in range(1, HX + 1):
         now, then = fields[(step - 1) % 2], fields[step % 2]
         skip = (done + step - 1) // SUB
         t0, t1 = skip, rows // SUB - skip
-
-        def some_planes(i, _, now=now, then=then, step=step, t0=t0, t1=t1):
-            advance_planes(now, then, coef, step + i * BLOCK, BLOCK, t0, t1)
+        if inner:
+            first, count, stride, block = HX + step, (planes - 2 * HX - 2 * step) // 2, 2, 2
+        else:
+            first, count, stride, block = step, 2, edge - 2 * step, HX
+
+        def some_planes(i, _, now=now, then=then, first=first, stride=stride, block=block, t0=t0, t1=t1):
+            advance_planes(now, then, coef, first + i * stride, block, t0, t1)
             return 0
 
-        lax.fori_loop(0, (planes - 2 * step) // BLOCK, some_planes, 0)
+        if count > 0:
+            lax.fori_loop(0, count, some_planes, 0)
 
 
 def pack_state(store, to_ahead, to_behind, skip):
@@ -216,82 +219,143 @@
             out[HX + i - 1] = (store[S, x, sl, :] - store[O, x, sl, :]).astype(BF16)
 
 
+def set_coefficients(store, x):
+    rows, depth = store.shape[2:]
+    for r in range(0, rows, CHUNK):
+        sl = pl.ds(r, CHUNK)
+        row = lax.broadcasted_iota(jnp.int32, (CHUNK, depth), 0)
+        lane = lax.broadcasted_iota(jnp.int32, (CHUNK, depth), 1)
+        kk = TIME_STEP * TIME_STEP * store[K, x, sl, :]
+        bb = store[B, x, sl, :]
+        b_x = store[B, x - 1, sl, :]
+        above = store[B, x, pl.ds(max(r - 1, 0), 1), :]
+        b_y = jnp.where(row == 0, above, pltpu.roll(bb, 1, 0))
+        b_z = jnp.where(lane == 0, 0.0, pltpu.roll(bb, 1, 1))
+        store[A, x, sl, :] = kk * bb
+        store[AX, x, sl, :] = kk * b_x
+        store[AY, x, sl, :] = kk * b_y
+        store[AZ, x, sl, :] = kk * b_z
+        store[D, x, sl, :] = 2.0 - kk * (3.0 * bb + b_x + b_y + b_z)
+        store[O, x, sl, :] = jnp.zeros((CHUNK, depth), F32)
+
+
+def add_source(tables, gathered, store):
+    planes, rows, depth = store.shape[1:]
+    own, own_rows = planes - 2 * HX, rows - 2 * HY
+    groups = gathered.shape[0]
+    top = tables.shape[0] - 1
+    samples = gathered.shape[1] - top * own
+    trace = jnp.concatenate([gathered[g, pl.ds(0, samples), :] for g in range(groups)], 1).astype(F32)
+    sensors = trace.shape[1]
+    row_at = lax.axis_index("grp") * own_rows - HY + lax.broadcasted_iota(jnp.int32, (rows, sensors), 0)
+    distance = jnp.abs(row_at - tables[pl.ds(top, 1), :]).astype(F32)
+    band = jnp.maximum(0.0, 1.0 - distance / BAND)
+    band = jnp.where((row_at >= 0) & (row_at < own_rows * groups), band, 0.0).astype(BF16)
+    slab_at = lax.axis_index("slab")
+    weights = [jnp.zeros((own, sensors), F32) for _ in range(3)]
+    for i in range(top):
+        lat = [gathered[g, pl.ds(samples + i * own, own), :] for g in range(groups)]
+        lat = jnp.concatenate(lat, 1).astype(F32)
+        for j in range(3):
+            weights[j] = weights[j] + jnp.where(tables[pl.ds(i, 1), :] == slab_at + (j - 1), lat, 0.0)
+    for x in range(1, planes - 1):
+        side, at = divmod(x + own - HX, own)
+        outer = (trace * weights[side][at : at + 1]).astype(BF16)
+        src = TIME_STEP * lax.dot_general(band, outer, (((1,), (1,)), ((), ())), preferred_element_type=F32)
+        later = pl.ds(depth - samples, samples)
+        if side == 1:
+            store[C, x, :, later] += src
+        else:
+            store[C, x, :, pl.ds(0, depth - samples)] = jnp.zeros((rows, depth - samples), F32)
+            store[C, x, :, later] = src
+
+
+def taken(given, held, sems):
+    copies = [pltpu.make_async_copy(src, dst, sems.at[i]) for i, (src, dst) in enumerate(zip(given, held))]
+    for copy in copies:
+        copy.start()
+    return copies
+
+
+def own_kernel(*refs):
+    given, (p, k, b, c), store = refs[:5], refs[5:9], refs[9]
+    held, sems = refs[10:15], refs[15]
+    row_behind, row_ahead, own_ahead, tables, gathered = held
+    planes, rows, _ = store.shape[1:]
+    own, own_rows = planes - 2 * HX, rows - 2 * HY
+    low, middle, high = pl.ds(0, HY), pl.ds(HY, own_rows), pl.ds(HY + own_rows, HY)
+    here = [store.at[f, pl.ds(HX, own), middle, :] for f in (S, K, B, C)]
+    copies = taken(given + (p, k, b, c), held + tuple(here), sems)
+    for copy in copies[:3]:
+        copy.wait()
+    for x in range(own):
+        for f in (S, C, K, B):
+            store[f, HX + x, low, :] = row_behind[f * own + x].astype(F32)
+            store[f, HX + x, high, :] = row_ahead[f * own + x].astype(F32)
+    for copy in copies[3:]:
+        copy.wait()
+    vy_behind = row_behind[4 * own + 1].astype(F32)
+    vy_last = own_ahead[4 * own + 1].astype(F32)
+    for x in range(own):
+        for at, vy in ((HY, vy_behind), (HY + own_rows, vy_last)):
+            sl = pl.ds(at, 1)
+            store[C, HX + x, sl, :] += TIME_STEP * store[K, HX + x, sl, :] * vy[x : x + 1]
+    add_source(tables, gathered, store)
+
+    def one_plane(x, _):
+        set_coefficients(store, x)
+        return 0
+
+    lax.fori_loop(HX + 1, HX + own, one_plane, 0)
+    advance_some(store, 0, True)
+
+
 def first_round_kernel(*refs):
-    given, (p, v, k, b, c, store, to_ahead, to_behind) = refs[:8], refs[8:16]
-    taken, (line, sems) = refs[16:24], refs[24:]
-    behind, ahead, corner_behind, corner_ahead, row_behind, row_ahead, own_ahead, src = taken
-    takes = [pltpu.make_async_copy(given[i], taken[i], sems.at[5 + i]) for i in range(8)]
-    planes, rows, depth = store.shape[1:]
+    given, v, store, to_ahead, to_behind = refs[:6], refs[6], refs[8], refs[9], refs[10]
+    held, line, sems = refs[11:17], refs[17], refs[18]
+    behind, ahead, corner_behind, corner_ahead, row_behind, row_ahead = held
+    planes, rows, _ = store.shape[1:]
     edge = planes - HX
-    own_rows = rows - 2 * HY
-    own = planes - 2 * HX
+    own, own_rows = planes - 2 * HX, rows - 2 * HY
     low, middle, high = pl.ds(0, HY), pl.ds(HY, own_rows), pl.ds(HY + own_rows, HY)
-    inner = pl.ds(HX, own)
-    copies = [
-        pltpu.make_async_copy(part, store.at[f, inner, middle, :], sems.at[f])
-        for f, part in ((S, p), (C, c), (K, k), (B, b))
-    ]
-    copies.append(pltpu.make_async_copy(v.at[0, own - 1], line.at[middle, :], sems.at[4]))
-    for copy in takes + copies:
-        copy.start()
-    for copy in takes:
-        copy.wait()
+    copies = taken(given + (v.at[0, own - 1],), held + (line.at[middle, :],), sems)
     sent_ahead, sent_behind = main_planes(own)
     moves = ((behind, corner_behind, sent_ahead, -own), (ahead, corner_ahead, sent_behind, own))
+    for copy in copies:
+        copy.wait()
     for main, corner, spans, shift in moves:
         units = unit_list(spans)
         for i, (f, x) in enumerate(units):
-            store[f, x + shift, low, :] = corner[2 * i].astype(F32)
-            store[f, x + shift, middle, :] = main[i].astype(F32)
-            store[f, x + shift, high, :] = corner[2 * i + 1].astype(F32)
+            parts = ((low, corner[2 * i]), (middle, main[i]), (high, corner[2 * i + 1]))
+            for sl, part in parts:
+                part = part.astype(F32)
+                if f == C:
+                    part = part + store[C, x + shift, sl, :]
+                store[f, x + shift, sl, :] = part
         _, x, count = spans[1]
         fixed = corner[2 * len(units)].astype(F32)
         for i in range(count):
             store[C, x + shift + i, pl.ds(HY, 1), :] += fixed[i : i + 1]
-    for x in range(own):
-        for f in (S, C, K, B):
-            store[f, HX + x, low, :] = row_behind[f * own + x].astype(F32)
-            store[f, HX + x, high, :] = row_ahead[f * own + x].astype(F32)
     line[low, :] = row_behind[4 * own].astype(F32)
     line[high, :] = row_ahead[4 * own].astype(F32)
-    vy_behind = row_behind[4 * own + 1].astype(F32)
-    vy_last = own_ahead[4 * own + 1].astype(F32)
-    for copy in copies:
-        copy.wait()
-    for x in range(own):
-        for at, vy in ((HY, vy_behind), (HY + own_rows, vy_last)):
-            sl = pl.ds(at, 1)
-            store[C, HX + x, sl, :] += TIME_STEP * store[K, HX + x, sl, :] * vy[x : x + 1]
     at = len(unit_list(sent_ahead))
     vx_parts = ((low, corner_behind[2 * at + 1]), (middle, behind[at]), (high, corner_behind[2 * at + 2]))
     for sl, part in vx_parts:
         store[C, HX, sl, :] += TIME_STEP * store[K, HX, sl, :] * part.astype(F32)
         store[C, edge, sl, :] += TIME_STEP * store[K, edge, sl, :] * line[sl, :]
-    later = pl.ds(depth - src.shape[2], src.shape[2])
-
-    def one_plane(x, _):
-        for r in range(0, rows, CHUNK):
-            sl = pl.ds(r, CHUNK)
-            row = lax.broadcasted_iota(jnp.int32, (CHUNK, depth), 0)
-            lane = lax.broadcasted_iota(jnp.int32, (CHUNK, depth), 1)
-            kk = TIME_STEP * TIME_STEP * store[K, x, sl, :]
-            bb = store[B, x, sl, :]
-            b_x = store[B, x - 1, sl, :]
-            above = store[B, x, pl.ds(max(r - 1, 0), 1), :]
-            b_y = jnp.where(row == 0, above, pltpu.roll(bb, 1, 0))
-            b_z = jnp.where(lane == 0, 0.0, pltpu.roll(bb, 1, 1))
-            store[A, x, sl, :] = kk * bb
-            store[AX, x, sl, :] = kk * b_x
-            store[AY, x, sl, :] = kk * b_y
-            store[AZ, x, sl, :] = kk * b_z
-            store[D, x, sl, :] = 2.0 - kk * (3.0 * bb + b_x + b_y + b_z)
-            store[O, x, sl, :] = jnp.zeros((CHUNK, depth), F32)
-            store[C, x, sl, later] += src[x, sl, :]
-        return 0
-
-    lax.fori_loop(1, planes - 1, one_plane, 0)
-    advance_round(store, 0)
+
+    def one_plane(i, _):
+        set_coefficients(store, jnp.where(i < HX, i + 1, i + edge - HX))
+        return 0
+
+    lax.fori_loop(0, 2 * HX - 1, one_plane, 0)
+    advance_some(store, 0, False)
     pack_state(store, to_ahead, to_behind, 0)
+
+
+def inner_kernel(store_i, store, *, done):
+    del store_i
+    advance_some(store, done, True)
 
 
 def take_halo(behind, ahead, store, skip):
@@ -309,7 +373,7 @@
 def middle_round_kernel(behind, ahead, store_i, store, to_ahead, to_behind, *, done, skips):
     del store_i
     take_halo(behind, ahead, store, skips[0])
-    advance_round(store, done)
+    advance_some(store, done, False)
     pack_state(store, to_ahead, to_behind, skips[1])
 
 
@@ -335,7 +399,7 @@
 
     lax.fori_loop(0, planes, start, 0)
     take_halo(behind, ahead, store, skip)
-    advance_round(store, done)
+    advance_some(store, done, False)
 
     def one_plane(x, _):
         for copy in reads(x):
@@ -379,11 +443,19 @@
     def everyones(copies, axis):
         return lax.all_to_all(copies, axis, split_axis=0, concat_axis=0, tiled=True)
 
-    lat = jnp.concatenate([lateral[:, :, planes - HX :], lateral, lateral[:, :, :HX]], 2)
-    sensor_rows = jnp.concatenate([traces, lat.reshape(lat.shape[0], -1)], 1)
-    copies = jnp.broadcast_to(sensor_rows[None], (slabs,) + sensor_rows.shape)
-    copies, centre, routes, pressure = lax.optimization_barrier((copies, ycenter[None, :], routes, pressure))
+    held, samples = traces.shape
+    top = routes.shape[1]
+    weights = jnp.transpose(lateral, (1, 2, 0)).reshape(top * planes, held)
+    copies = pl.pallas_call(
+        sensors_kernel,
+        out_shape=jax.ShapeDtypeStruct((slabs, held + top * planes, samples), BF16),
+        in_specs=[VM] * 2,
+        out_specs=VM,
+        compiler_params=params(4),
+    )(traces, weights)
     got = everyones(copies, "slab")
+    tables = jnp.concatenate([routes.T, ycenter[None]], 0)
+    tables = jnp.swapaxes(tables.reshape(top + 1, slabs, groups, held), 1, 2).reshape(top + 1, -1)
 
     n_rows = 4 * planes
     n_ahead, n_behind = [len(unit_list(spans)) for spans in main_planes(planes)]
@@ -399,17 +471,18 @@
         scratch_shapes=[pltpu.VMEM((6,) + pressure.shape, F32), pltpu.SemaphoreType.DMA((6, planes))],
         compiler_params=params(24),
     )(*inputs)
+    from_behind = passed_along(row_ahead, "grp", 1)
+    from_ahead = passed_along(row_behind, "grp", -1)
+    got, plane_ahead, plane_behind = lax.optimization_barrier((got, plane_ahead, plane_behind))
     main_behind = passed_along(plane_ahead, "slab", 1)
     main_ahead = passed_along(plane_behind, "slab", -1)
-    from_behind = passed_along(row_ahead, "grp", 1)
-    from_ahead = passed_along(row_behind, "grp", -1)
 
     copies = pl.pallas_call(
-        repeat_kernel,
-        out_shape=jax.ShapeDtypeStruct((groups, slabs * sensor_rows.shape[0], sensor_rows.shape[1]), BF16),
+        functools.partial(repeat_kernel, own=held),
+        out_shape=jax.ShapeDtypeStruct((groups, samples + top * planes, slabs * held), BF16),
         in_specs=[VM],
         out_specs=VM,
-        compiler_params=params(4),
+        compiler_params=params(8),
     )(got)
     gathered = everyones(copies, "grp")
 
@@ -423,30 +496,49 @@
     corner_from_behind = passed_along(corner_ahead, "slab", 1)
     corner_from_ahead = passed_along(corner_behind, "slab", -1)
 
-    src = pl.pallas_call(
-        functools.partial(source_kernel, held=traces.shape[0]),
-        out_shape=jax.ShapeDtypeStruct((wide, tall, traces.shape[1]), F32),
-        in_specs=[VM] * 3,
+    def in_hbm(*values):
+        return [pltpu.with_memory_space_constraint(x, pltpu.HBM) for x in values]
+
+    def copied(given, extra):
+        return [pltpu.VMEM(x.shape, x.dtype) for x in given] + [pltpu.SemaphoreType.DMA((len(given) + extra,))]
+
+    given = (from_behind, from_ahead, row_ahead, tables, gathered)
+    store = pl.pallas_call(
+        own_kernel,
+        out_shape=store_shape,
+        in_specs=[HBM] * 9,
         out_specs=VM,
-        compiler_params=params(16),
-    )(centre, routes, gathered)
-
-    given = (main_behind, main_ahead, corner_from_behind, corner_from_ahead, from_behind, from_ahead, row_ahead, src)
+        scratch_shapes=copied(given, 4),
+        compiler_params=params(14),
+    )(*in_hbm(*given), inputs[0], inputs[2], inputs[3], *in_hbm(c))
+    given = (main_behind, main_ahead, corner_from_behind, corner_from_ahead, from_behind, from_ahead)
+    scratch = copied(given, 1)
     store, plane_ahead, plane_behind = pl.pallas_call(
         first_round_kernel,
         out_shape=(store_shape, sent(2 * HX - 1, tall), sent(2 * HX - 1, tall)),
-        in_specs=[HBM] * 13,
+        in_specs=[HBM] * 7 + [VM],
         out_specs=[VM] * 3,
-        scratch_shapes=[pltpu.VMEM(x.shape, x.dtype) for x in given]
-        + [pltpu.VMEM((tall, depth), F32), pltpu.SemaphoreType.DMA((5 + len(given),))],
+        input_output_aliases={7: 0},
+        scratch_shapes=scratch[:-1] + [pltpu.VMEM((tall, depth), F32), scratch[-1]],
         compiler_params=params(14),
-    )(*[pltpu.with_memory_space_constraint(x, pltpu.HBM) for x in given + (*inputs, c)])
+    )(*in_hbm(*given), inputs[1], store)
+
+    def inner(store, done):
+        return pl.pallas_call(
+            functools.partial(inner_kernel, done=done),
+            out_shape=store_shape,
+            in_specs=[VM],
+            out_specs=VM,
+            input_output_aliases={0: 0},
+            compiler_params=params(14),
+        )(store)
 
     rounds = STEPS // HX
     skips = [SUB * (HX * r // SUB) for r in range(1, rounds)]
     for r in range(1, rounds - 1):
         from_behind = passed_along(plane_ahead, "slab", 1)
         from_ahead = passed_along(plane_behind, "slab", -1)
+        store = inner(store, HX * r)
         height = tall - 2 * skips[r]
         store, plane_ahead, plane_behind = pl.pallas_call(
             functools.partial(middle_round_kernel, done=HX * r, skips=skips[r - 1 : r + 1]),
@@ -458,6 +550,7 @@
         )(from_behind, from_ahead, store)
     from_behind = passed_along(plane_ahead, "slab", 1)
     from_ahead = passed_along(plane_behind, "slab", -1)
+    store = inner(store, HX * (rounds - 1))
     p_out, v_out, _ = pl.pallas_call(
         functools.partial(last_round_kernel, done=HX * (rounds - 1), skip=skips[-1]),
         out_shape=(

time: 138 us -> 119 us (0.86)
  waiting for transfers between devices: 44.7 us -> 31.2 us
  local copies, waits for them, and re-layouts: 7.9 us -> 5.27 us
  starting transfers between devices: 42.4 us -> 40.4 us
  other arithmetic: 1.41 us -> 0.01 us
    all_to_all x2, waiting for transfers between devices: 13.3 us -> 0.01 us  [everyones(): return lax.all_to_all(copies, axis, split_axis=0, concat_axis=0, tiled=True)]
    pallas_call x2 -> x6, Pallas kernels: 2.61 us -> 13.2 us  [the longest x1 6.99 us: local(): pl.pallas_call(own_kernel, out_shape=store_shape, in_specs=[HBM] * 9, out...]
    pallas_call x1, Pallas kernels: 12.5 us -> 7.61 us  [local(): pl.pallas_call(first_round_kernel, out_shape=(store_shape, sent(2 * HX -...]
    pallas_call x2, Pallas kernels: 12.3 us -> 8.44 us  [local(): pl.pallas_call(functools.partial(middle_round_kernel, done=HX * r, skips=...]
    ppermute x12, starting transfers between devices: 33.4 us -> 29.8 us  [passed_along(): lax.ppermute(value, axis, [(source, source + steps) for source in range(f...]
    pallas_call x1, Pallas kernels: 8.41 us -> 6.53 us  [local(): pl.pallas_call(functools.partial(last_round_kernel, done=HX * (rounds - 1...]
    all_to_all x2, starting transfers between devices: 8.96 us -> 10.6 us  [everyones(): return lax.all_to_all(copies, axis, split_axis=0, concat_axis=0, tiled=True)]
    concatenate x0 -> x4, local copies, waits for them, and re-layouts: none -> 1.57 us  [local(): tables = jnp.concatenate([routes.T, ycenter[None]], 0)]
  transfers between devices with their start and end apart: 14 -> 14, of which waited for: 8 -> 7; matrix products, arithmetic and copies ran while one was open for 2% -> 2% of each run, Pallas kernels for 2% -> 14%
where the time goes in v3:
time: 119 us; the launch traced here: 117 us
  starting transfers between devices  40.4 us (34%)
  Pallas kernels  39.4 us (33%)
  waiting for transfers between devices  31.2 us (26%)
  local copies, waits for them, and re-layouts  5.27 us (4%)
    ppermute x12, waiting for transfers between devices, passed_along(): lax.ppermute(value, axis, [(source, source + steps) for source in range(f...  31.2 us
    ppermute x12, starting transfers between devices, passed_along(): lax.ppermute(value, axis, [(source, source + steps) for source in range(f...  29.8 us
    all_to_all x2, starting transfers between devices, everyones(): return lax.all_to_all(copies, axis, split_axis=0, concat_axis=0, tiled=True)  10.6 us
    pallas_call x2, Pallas kernels, local(): pl.pallas_call(functools.partial(middle_round_kernel, done=HX * r, skips=...  8.44 us
    pallas_call x1, Pallas kernels, local(): pl.pallas_call(first_round_kernel, out_shape=(store_shape, sent(2 * HX -...  7.61 us
    pallas_call x1, Pallas kernels, local(): pl.pallas_call(own_kernel, out_shape=store_shape, in_specs=[HBM] * 9, out...  6.99 us
    pallas_call x1, Pallas kernels, local(): pl.pallas_call(functools.partial(last_round_kernel, done=HX * (rounds - 1...  6.53 us
    pallas_call x3, Pallas kernels, inner(): pl.pallas_call(functools.partial(inner_kernel, done=done), out_shape=stor...  4.76 us
  transfers between devices with their start and end apart: 14, of which 7 were waited for; matrix products, arithmetic and copies ran while one was open for 2% of the time, Pallas kernels for 14%

profile of v3, /device:TPU:1, one launch (start us, length us, event | category | flops | bytes accessed | tf_op | source)
XLA Modules:
  0.0 117.3 jit_solution(7888516359877913630)
XLA Ops:
  0.6 0.0 copy-start.4
  0.6 0.7 copy-done.4
  1.3 0.0 copy-start.5
  1.3 0.7 copy-done.5
  2.0 0.7 shard_map.95
  2.7 5.2 %all-to-all-start = ((bf16[8,48,128]{2,1,0:T(8,128)(2,1)}), bf16[8,48,128]{2,1,0:T(8,128)(2,1)S(1)}, u32[]{:S(2)}, u32[]{:S(2)}) async-start(bf16[8,48,128]{2,1,0:T(8,128)(2,1)} %shard_map.95), calls=%async_computation | async-start | bytes 196608 | tf_op jit(solution)/shard_map/all_to_all | solution.py:444
  7.9 3.6 %shard_map.96 = (f32[8,128,256]{2,1,0:T(8,128)S(1)}, bf16[34,16,256]{2,1,0:T(8,128)(2,1)S(1)}, bf16[33,16,256]{2,1,0:T(8,128)(2,1)S(1)}, bf16[15,128,256]{2,1,0:T(8,128)(2,1)S(1)}, bf16[13,128,256]{2,1,0:T(8,128)(2,1)S(1)}) custom-call(f32[8,128,256]{2,1,0:T(8,128)} %refs_5_.1, f32[3,8,128,256]{3,2,1,0:T(8,128)} %v.3, f32[8,128,256]{2,1,0:T(8,128)} %refs_6_.2, ...), custom_call_target="tpu_custom_call" | custom-call | tf_op jit(solution)/shard_map/pallas_call | solution.py:463
  11.5 0.0 copy-start.3
  11.5 1.0 copy-done.3
  12.5 0.0 copy-start.2
  12.5 0.0 all-to-all-done.got
  12.5 3.5 %collective-permute-start = (bf16[15,128,256]{2,1,0:T(8,128)(2,1)S(1)}, bf16[15,128,256]{2,1,0:T(8,128)(2,1)}, u32[]{:S(2)}, u32[]{:S(2)}) collective-permute-start(bf16[15,128,256]{2,1,0:T(8,128)(2,1)S(1)} %get-tuple-element.25), channel_id=1, source_target_pairs={{0,4},{4,8},{8,12},{12,16},{16,20},{20,24},{24,28},{1,5},{5,9},{9,... | collective-permute-start | bytes 2949128 | tf_op jit(solution)/shard_map/ppermute | solution.py:30
  16.0 1.9 %collective-permute-start.1 = (bf16[13,128,256]{2,1,0:T(8,128)(2,1)S(1)}, bf16[13,128,256]{2,1,0:T(8,128)(2,1)}, u32[]{:S(2)}, u32[]{:S(2)}) collective-permute-start(bf16[13,128,256]{2,1,0:T(8,128)(2,1)S(1)} %get-tuple-element.26), channel_id=1, source_target_pairs={{4,0},{8,4},{12,8},{16,12},{20,16},{24,20},{28,24},{5,1},{9,5},{13... | collective-permute-start | bytes 2555912 | tf_op jit(solution)/shard_map/ppermute | solution.py:30
  17.9 3.2 %collective-permute-start.2 = (bf16[34,16,256]{2,1,0:T(8,128)(2,1)S(1)}, bf16[34,16,256]{2,1,0:T(8,128)(2,1)S(1)}, u32[]{:S(2)}, u32[]{:S(2)}) collective-permute-start(bf16[34,16,256]{2,1,0:T(8,128)(2,1)S(1)} %get-tuple-element.27.own_ahead.refs_2_), channel_id=1, source_target_pairs={{0,1},{1,2},{2,3},{4,5},{5,6},{6,7},{8,9},{9,10},{10,11},{12,13},{... | collective-permute-start | bytes 835592 | tf_op jit(solution)/shard_map/ppermute | solution.py:30
  21.1 1.3 %collective-permute-start.3 = (bf16[33,16,256]{2,1,0:T(8,128)(2,1)S(1)}, bf16[33,16,256]{2,1,0:T(8,128)(2,1)S(1)}, u32[]{:S(2)}, u32[]{:S(2)}) collective-permute-start(bf16[33,16,256]{2,1,0:T(8,128)(2,1)S(1)} %get-tuple-element.28.own_behind), channel_id=1, source_target_pairs={{1,0},{2,1},{3,2},{5,4},{6,5},{7,6},{9,8},{10,9},{11,10},{13,12},{... | collective-permute-start | bytes 811016 | tf_op jit(solution)/shard_map/ppermute | solution.py:30
  22.4 0.8 shard_map.98
  23.3 5.4 %all-to-all-start.1 = ((bf16[4,144,256]{2,1,0:T(8,128)(2,1)}), bf16[4,144,256]{2,1,0:T(8,128)(2,1)}, u32[]{:S(2)}, u32[]{:S(2)}) async-start(bf16[4,144,256]{2,1,0:T(8,128)(2,1)} %shard_map.98), calls=%async_computation.1 | async-start | bytes 589824 | tf_op jit(solution)/shard_map/all_to_all | solution.py:444
  28.6 2.8 %collective-permute-done.3.ahead.refs_1_.refs_5_ = bf16[33,16,256]{2,1,0:T(8,128)(2,1)S(1)} collective-permute-done((bf16[33,16,256]{2,1,0:T(8,128)(2,1)S(1)}, bf16[33,16,256]{2,1,0:T(8,128)(2,1)S(1)}, u32[]{:S(2)}, u32[]{:S(2)}) %collective-permute-start.3) | collective-permute-done | bytes 270368 | tf_op jit(solution)/shard_map/ppermute | solution.py:30
  31.4 0.0 copy-start.1
  31.4 0.0 collective-permute-done.2.behind.refs_0_.refs_4_
  31.4 0.0 copy-start
  31.5 3.5 %collective-permute-start.4 = (bf16[31,16,256]{2,1,0:T(8,128)(2,1)S(1)}, bf16[31,16,256]{2,1,0:T(8,128)(2,1)S(1)}, u32[]{:S(2)}, u32[]{:S(2)}) collective-permute-start(bf16[31,16,256]{2,1,0:T(8,128)(2,1)S(1)} %get-tuple-element.29), channel_id=1, source_target_pairs={{0,4},{4,8},{8,12},{12,16},{16,20},{20,24},{24,28},{1,5},{5,9},{9,... | collective-permute-start | bytes 761864 | tf_op jit(solution)/shard_map/ppermute | solution.py:30
  35.0 1.9 %collective-permute-start.5 = (bf16[27,16,256]{2,1,0:T(8,128)(2,1)S(1)}, bf16[27,16,256]{2,1,0:T(8,128)(2,1)}, u32[]{:S(2)}, u32[]{:S(2)}) collective-permute-start(bf16[27,16,256]{2,1,0:T(8,128)(2,1)S(1)} %get-tuple-element.30), channel_id=1, source_target_pairs={{4,0},{8,4},{12,8},{16,12},{20,16},{24,20},{28,24},{5,1},{9,5},{13... | collective-permute-start | bytes 663560 | tf_op jit(solution)/shard_map/ppermute | solution.py:30
  36.9 0.8 concatenate.9
  37.7 0.8 concatenate.8
  38.5 0.7 reshape.15.refs_3_
  39.2 0.0 all-to-all-done.1.refs_4_
  39.2 0.0 copy-done.2
  39.2 0.0 copy-done.1
  39.2 0.0 copy-done
  39.2 7.0 %shard_map.99.refs_7_ = f32[10,16,160,256]{3,2,1,0:T(8,128)S(1)} custom-call(bf16[34,16,256]{2,1,0:T(8,128)(2,1)} %copy-done, bf16[33,16,256]{2,1,0:T(8,128)(2,1)} %copy-done.1, bf16[34,16,256]{2,1,0:T(8,128)(2,1)} %copy-done.2, s32[3,1024]{1,0:T(4,128)} %reshape.15.refs_3_, bf16[4,144,256]{2,1,0:T(8,128)(2,1)} %all-to-all-done.1.refs_4_, ...), custom_call_target="tpu_custom_call" | custom-call | tf_op jit(solution)/shard_map/pallas_call | solution.py:506
  46.2 0.0 collective-permute-done.5.refs_3_
  46.2 0.0 collective-permute-done.4.refs_2_
  46.2 0.0 copy-start.6
  46.2 0.0 collective-permute-done.1.refs_1_
  46.2 0.0 collective-permute-done.refs_0_
  46.3 0.7 copy-done.6
  46.9 7.6 %shard_map.100 = (f32[10,16,160,256]{3,2,1,0:T(8,128)S(1)}, bf16[7,160,256]{2,1,0:T(8,128)(2,1)S(1)}, bf16[7,160,256]{2,1,0:T(8,128)(2,1)S(1)}) custom-call(bf16[15,128,256]{2,1,0:T(8,128)(2,1)} %collective-permute-done.refs_0_, bf16[13,128,256]{2,1,0:T(8,128)(2,1)} %collective-permute-done.1.refs_1_, ...), custom_call_target="tpu_custom_call", output_to_operand_aliasing={{0}: (7, {})} | custom-call | tf_op jit(solution)/shard_map/pallas_call | solution.py:516
  54.5 3.6 %collective-permute-start.6 = (bf16[7,160,256]{2,1,0:T(8,128)(2,1)S(1)}, bf16[7,160,256]{2,1,0:T(8,128)(2,1)S(1)}, u32[]{:S(2)}, u32[]{:S(2)}) collective-permute-start(bf16[7,160,256]{2,1,0:T(8,128)(2,1)S(1)} %get-tuple-element.33), channel_id=1, source_target_pairs={{0,4},{4,8},{8,12},{12,16},{16,20},{20,24},{24,28},{1,5},{5,9},{9,... | collective-permute-start | bytes 1720328 | tf_op jit(solution)/shard_map/ppermute | solution.py:30
  58.2 1.9 %collective-permute-start.7 = (bf16[7,160,256]{2,1,0:T(8,128)(2,1)S(1)}, bf16[7,160,256]{2,1,0:T(8,128)(2,1)S(1)}, u32[]{:S(2)}, u32[]{:S(2)}) collective-permute-start(bf16[7,160,256]{2,1,0:T(8,128)(2,1)S(1)} %get-tuple-element.34), channel_id=1, source_target_pairs={{4,0},{8,4},{12,8},{16,12},{20,16},{24,20},{28,24},{5,1},{9,5},{13... | collective-permute-start | bytes 1720328 | tf_op jit(solution)/shard_map/ppermute | solution.py:30
  60.1 1.7 %shard_map.101.store_i = f32[10,16,160,256]{3,2,1,0:T(8,128)S(1)} custom-call(f32[10,16,160,256]{3,2,1,0:T(8,128)S(1)} %get-tuple-element.35.store_i), custom_call_target="tpu_custom_call", output_to_operand_aliasing={{}: (0, {})} | custom-call | tf_op jit(solution)/shard_map/pallas_call | solution.py:527
  61.8 3.0 %collective-permute-done.6.behind = bf16[7,160,256]{2,1,0:T(8,128)(2,1)S(1)} collective-permute-done((bf16[7,160,256]{2,1,0:T(8,128)(2,1)S(1)}, bf16[7,160,256]{2,1,0:T(8,128)(2,1)S(1)}, u32[]{:S(2)}, u32[]{:S(2)}) %collective-permute-start.6) | collective-permute-done | bytes 573472 | tf_op jit(solution)/shard_map/ppermute | solution.py:30
  64.8 8.7 %collective-permute-done.7.ahead = bf16[7,160,256]{2,1,0:T(8,128)(2,1)S(1)} collective-permute-done((bf16[7,160,256]{2,1,0:T(8,128)(2,1)S(1)}, bf16[7,160,256]{2,1,0:T(8,128)(2,1)S(1)}, u32[]{:S(2)}, u32[]{:S(2)}) %collective-permute-start.7) | collective-permute-done | bytes 573472 | tf_op jit(solution)/shard_map/ppermute | solution.py:30
  73.5 4.4 %shard_map.102 = (f32[10,16,160,256]{3,2,1,0:T(8,128)S(1)}, bf16[7,144,256]{2,1,0:T(8,128)(2,1)S(1)}, bf16[7,144,256]{2,1,0:T(8,128)(2,1)S(1)}) custom-call(bf16[7,160,256]{2,1,0:T(8,128)(2,1)S(1)} %collective-permute-done.6.behind, bf16[7,160,256]{2,1,0:T(8,128)(2,1)S(1)} %collective-permute-done.7.ahead, ...), custom_call_target="tpu_custom_call", output_to_operand_aliasing={{0}: (2, {})} | custom-call | tf_op jit(solution)/shard_map/pallas_call | solution.py:543
  77.9 1.9 %collective-permute-start.8 = (bf16[7,144,256]{2,1,0:T(8,128)(2,1)S(1)}, bf16[7,144,256]{2,1,0:T(8,128)(2,1)S(1)}, u32[]{:S(2)}, u32[]{:S(2)}) collective-permute-start(bf16[7,144,256]{2,1,0:T(8,128)(2,1)S(1)} %get-tuple-element.36), channel_id=1, source_target_pairs={{0,4},{4,8},{8,12},{12,16},{16,20},{20,24},{24,28},{1,5},{5,9},{9,... | collective-permute-start | bytes 1548296 | tf_op jit(solution)/shard_map/ppermute | solution.py:30
  79.8 2.6 %collective-permute-start.9 = (bf16[7,144,256]{2,1,0:T(8,128)(2,1)S(1)}, bf16[7,144,256]{2,1,0:T(8,128)(2,1)S(1)}, u32[]{:S(2)}, u32[]{:S(2)}) collective-permute-start(bf16[7,144,256]{2,1,0:T(8,128)(2,1)S(1)} %get-tuple-element.37), channel_id=1, source_target_pairs={{4,0},{8,4},{12,8},{16,12},{20,16},{24,20},{28,24},{5,1},{9,5},{13... | collective-permute-start | bytes 1548296 | tf_op jit(solution)/shard_map/ppermute | solution.py:30
  82.4 1.5 %shard_map.103.store_i = f32[10,16,160,256]{3,2,1,0:T(8,128)S(1)} custom-call(f32[10,16,160,256]{3,2,1,0:T(8,128)S(1)} %get-tuple-element.38.store_i), custom_call_target="tpu_custom_call", output_to_operand_aliasing={{}: (0, {})} | custom-call | tf_op jit(solution)/shard_map/pallas_call | solution.py:527
  84.0 1.8 %collective-permute-done.8.behind = bf16[7,144,256]{2,1,0:T(8,128)(2,1)S(1)} collective-permute-done((bf16[7,144,256]{2,1,0:T(8,128)(2,1)S(1)}, bf16[7,144,256]{2,1,0:T(8,128)(2,1)S(1)}, u32[]{:S(2)}, u32[]{:S(2)}) %collective-permute-start.8) | collective-permute-done | bytes 516128 | tf_op jit(solution)/shard_map/ppermute | solution.py:30
  85.8 7.0 %collective-permute-done.9.ahead = bf16[7,144,256]{2,1,0:T(8,128)(2,1)S(1)} collective-permute-done((bf16[7,144,256]{2,1,0:T(8,128)(2,1)S(1)}, bf16[7,144,256]{2,1,0:T(8,128)(2,1)S(1)}, u32[]{:S(2)}, u32[]{:S(2)}) %collective-permute-start.9) | collective-permute-done | bytes 516128 | tf_op jit(solution)/shard_map/ppermute | solution.py:30
  92.8 4.0 %shard_map.104 = (f32[10,16,160,256]{3,2,1,0:T(8,128)S(1)}, bf16[7,144,256]{2,1,0:T(8,128)(2,1)S(1)}, bf16[7,144,256]{2,1,0:T(8,128)(2,1)S(1)}) custom-call(bf16[7,144,256]{2,1,0:T(8,128)(2,1)S(1)} %collective-permute-done.8.behind, bf16[7,144,256]{2,1,0:T(8,128)(2,1)S(1)} %collective-permute-done.9.ahead, ...), custom_call_target="tpu_custom_call", output_to_operand_aliasing={{0}: (2, {})} | custom-call | tf_op jit(solution)/shard_map/pallas_call | solution.py:543
  96.8 1.9 %collective-permute-start.10 = (bf16[7,144,256]{2,1,0:T(8,128)(2,1)S(1)}, bf16[7,144,256]{2,1,0:T(8,128)(2,1)S(1)}, u32[]{:S(2)}, u32[]{:S(2)}) collective-permute-start(bf16[7,144,256]{2,1,0:T(8,128)(2,1)S(1)} %get-tuple-element.39), channel_id=1, source_target_pairs={{0,4},{4,8},{8,12},{12,16},{16,20},{20,24},{24,28},{1,5},{5,9},{9,... | collective-permute-start | bytes 1548296 | tf_op jit(solution)/shard_map/ppermute | solution.py:30
  98.8 2.4 %collective-permute-start.11 = (bf16[7,144,256]{2,1,0:T(8,128)(2,1)S(1)}, bf16[7,144,256]{2,1,0:T(8,128)(2,1)S(1)}, u32[]{:S(2)}, u32[]{:S(2)}) collective-permute-start(bf16[7,144,256]{2,1,0:T(8,128)(2,1)S(1)} %get-tuple-element.40), channel_id=1, source_target_pairs={{4,0},{8,4},{12,8},{16,12},{20,16},{24,20},{28,24},{5,1},{9,5},{13... | collective-permute-start | bytes 1548296 | tf_op jit(solution)/shard_map/ppermute | solution.py:30
  101.2 1.5 %shard_map.105.store_i = f32[10,16,160,256]{3,2,1,0:T(8,128)S(1)} custom-call(f32[10,16,160,256]{3,2,1,0:T(8,128)S(1)} %get-tuple-element.41.store_i), custom_call_target="tpu_custom_call", output_to_operand_aliasing={{}: (0, {})} | custom-call | tf_op jit(solution)/shard_map/pallas_call | solution.py:527
  102.8 2.0 %collective-permute-done.10.behind = bf16[7,144,256]{2,1,0:T(8,128)(2,1)S(1)} collective-permute-done((bf16[7,144,256]{2,1,0:T(8,128)(2,1)S(1)}, bf16[7,144,256]{2,1,0:T(8,128)(2,1)S(1)}, u32[]{:S(2)}, u32[]{:S(2)}) %collective-permute-start.10) | collective-permute-done | bytes 516128 | tf_op jit(solution)/shard_map/ppermute | solution.py:30
  104.8 5.9 %collective-permute-done.11.ahead = bf16[7,144,256]{2,1,0:T(8,128)(2,1)S(1)} collective-permute-done((bf16[7,144,256]{2,1,0:T(8,128)(2,1)S(1)}, bf16[7,144,256]{2,1,0:T(8,128)(2,1)S(1)}, u32[]{:S(2)}, u32[]{:S(2)}) %collective-permute-start.11) | collective-permute-done | bytes 516128 | tf_op jit(solution)/shard_map/ppermute | solution.py:30
  110.6 6.5 %shard_map.106 = (f32[8,128,256]{2,1,0:T(8,128)}, f32[3,8,128,256]{3,2,1,0:T(8,128)}, f32[10,16,160,256]{3,2,1,0:T(8,128)S(1)}) custom-call(bf16[7,144,256]{2,1,0:T(8,128)(2,1)S(1)} %collective-permute-done.10.behind, bf16[7,144,256]{2,1,0:T(8,128)(2,1)S(1)} %collective-permute-done.11.ahead, f32[3,8,128,256]{3,2,1,0:T(8,128)} %v.3, ...), custom_call_target="tpu_custom_call", output_to_operand_aliasing={{2}: (3, {})} | custom-call | tf_op jit(solution)/shard_map/pallas_call | solution.py:554
  (4 shorter events, 0.1 us)
Async XLA Ops:
  0.6 0.7 copy-start.4
  1.3 0.7 copy-start.5
  2.7 9.8 %all-to-all-start = ((bf16[8,48,128]{2,1,0:T(8,128)(2,1)}), bf16[8,48,128]{2,1,0:T(8,128)(2,1)S(1)}, u32[]{:S(2)}, u32[]{:S(2)}) async-start(bf16[8,48,128]{2,1,0:T(8,128)(2,1)} %shard_map.95), calls=%async_computation | async-start | bytes 196608 | tf_op jit(solution)/shard_map/all_to_all | solution.py:444
  11.5 1.0 copy-start.3
  12.5 26.7 %copy-start.2 = (bf16[34,16,256]{2,1,0:T(8,128)(2,1)}, bf16[34,16,256]{2,1,0:T(8,128)(2,1)S(1)}, u32[]{:S(2)}) copy-start(bf16[34,16,256]{2,1,0:T(8,128)(2,1)S(1)} %get-tuple-element.27.own_ahead.refs_2_) | copy-start | bytes 835588
  12.5 33.8 %collective-permute-start = (bf16[15,128,256]{2,1,0:T(8,128)(2,1)S(1)}, bf16[15,128,256]{2,1,0:T(8,128)(2,1)}, u32[]{:S(2)}, u32[]{:S(2)}) collective-permute-start(bf16[15,128,256]{2,1,0:T(8,128)(2,1)S(1)} %get-tuple-element.25), channel_id=1, source_target_pairs={{0,4},{4,8},{8,12},{12,16},{16,20},{20,24},{24,28},{1,5},{5,9},{9,... | collective-permute-start | bytes 2949128 | tf_op jit(solution)/shard_map/ppermute | solution.py:30
  16.0 30.2 %collective-permute-start.1 = (bf16[13,128,256]{2,1,0:T(8,128)(2,1)S(1)}, bf16[13,128,256]{2,1,0:T(8,128)(2,1)}, u32[]{:S(2)}, u32[]{:S(2)}) collective-permute-start(bf16[13,128,256]{2,1,0:T(8,128)(2,1)S(1)} %get-tuple-element.26), channel_id=1, source_target_pairs={{4,0},{8,4},{12,8},{16,12},{20,16},{24,20},{28,24},{5,1},{9,5},{13... | collective-permute-start | bytes 2555912 | tf_op jit(solution)/shard_map/ppermute | solution.py:30
  17.9 13.5 %collective-permute-start.2 = (bf16[34,16,256]{2,1,0:T(8,128)(2,1)S(1)}, bf16[34,16,256]{2,1,0:T(8,128)(2,1)S(1)}, u32[]{:S(2)}, u32[]{:S(2)}) collective-permute-start(bf16[34,16,256]{2,1,0:T(8,128)(2,1)S(1)} %get-tuple-element.27.own_ahead.refs_2_), channel_id=1, source_target_pairs={{0,1},{1,2},{2,3},{4,5},{5,6},{6,7},{8,9},{9,10},{10,11},{12,13},{... | collective-permute-start | bytes 835592 | tf_op jit(solution)/shard_map/ppermute | solution.py:30
  21.1 10.3 %collective-permute-start.3 = (bf16[33,16,256]{2,1,0:T(8,128)(2,1)S(1)}, bf16[33,16,256]{2,1,0:T(8,128)(2,1)S(1)}, u32[]{:S(2)}, u32[]{:S(2)}) collective-permute-start(bf16[33,16,256]{2,1,0:T(8,128)(2,1)S(1)} %get-tuple-element.28.own_behind), channel_id=1, source_target_pairs={{1,0},{2,1},{3,2},{5,4},{6,5},{7,6},{9,8},{10,9},{11,10},{13,12},{... | collective-permute-start | bytes 811016 | tf_op jit(solution)/shard_map/ppermute | solution.py:30
  23.3 15.9 %all-to-all-start.1 = ((bf16[4,144,256]{2,1,0:T(8,128)(2,1)}), bf16[4,144,256]{2,1,0:T(8,128)(2,1)}, u32[]{:S(2)}, u32[]{:S(2)}) async-start(bf16[4,144,256]{2,1,0:T(8,128)(2,1)} %shard_map.98), calls=%async_computation.1 | async-start | bytes 589824 | tf_op jit(solution)/shard_map/all_to_all | solution.py:444
  31.4 7.8 %copy-start.1 = (bf16[33,16,256]{2,1,0:T(8,128)(2,1)}, bf16[33,16,256]{2,1,0:T(8,128)(2,1)S(1)}, u32[]{:S(2)}) copy-start(bf16[33,16,256]{2,1,0:T(8,128)(2,1)S(1)} %collective-permute-done.3.ahead.refs_1_.refs_5_) | copy-start | bytes 811012
  31.4 7.8 %copy-start = (bf16[34,16,256]{2,1,0:T(8,128)(2,1)}, bf16[34,16,256]{2,1,0:T(8,128)(2,1)S(1)}, u32[]{:S(2)}) copy-start(bf16[34,16,256]{2,1,0:T(8,128)(2,1)S(1)} %collective-permute-done.2.behind.refs_0_.refs_4_) | copy-start | bytes 835588
  31.5 14.7 %collective-permute-start.4 = (bf16[31,16,256]{2,1,0:T(8,128)(2,1)S(1)}, bf16[31,16,256]{2,1,0:T(8,128)(2,1)S(1)}, u32[]{:S(2)}, u32[]{:S(2)}) collective-permute-start(bf16[31,16,256]{2,1,0:T(8,128)(2,1)S(1)} %get-tuple-element.29), channel_id=1, source_target_pairs={{0,4},{4,8},{8,12},{12,16},{16,20},{20,24},{24,28},{1,5},{5,9},{9,... | collective-permute-start | bytes 761864 | tf_op jit(solution)/shard_map/ppermute | solution.py:30
  35.0 11.2 %collective-permute-start.5 = (bf16[27,16,256]{2,1,0:T(8,128)(2,1)S(1)}, bf16[27,16,256]{2,1,0:T(8,128)(2,1)}, u32[]{:S(2)}, u32[]{:S(2)}) collective-permute-start(bf16[27,16,256]{2,1,0:T(8,128)(2,1)S(1)} %get-tuple-element.30), channel_id=1, source_target_pairs={{4,0},{8,4},{12,8},{16,12},{20,16},{24,20},{28,24},{5,1},{9,5},{13... | collective-permute-start | bytes 663560 | tf_op jit(solution)/shard_map/ppermute | solution.py:30
  46.2 0.7 copy-start.6
  54.5 10.3 %collective-permute-start.6 = (bf16[7,160,256]{2,1,0:T(8,128)(2,1)S(1)}, bf16[7,160,256]{2,1,0:T(8,128)(2,1)S(1)}, u32[]{:S(2)}, u32[]{:S(2)}) collective-permute-start(bf16[7,160,256]{2,1,0:T(8,128)(2,1)S(1)} %get-tuple-element.33), channel_id=1, source_target_pairs={{0,4},{4,8},{8,12},{12,16},{16,20},{20,24},{24,28},{1,5},{5,9},{9,... | collective-permute-start | bytes 1720328 | tf_op jit(solution)/shard_map/ppermute | solution.py:30
  58.2 15.3 %collective-permute-start.7 = (bf16[7,160,256]{2,1,0:T(8,128)(2,1)S(1)}, bf16[7,160,256]{2,1,0:T(8,128)(2,1)S(1)}, u32[]{:S(2)}, u32[]{:S(2)}) collective-permute-start(bf16[7,160,256]{2,1,0:T(8,128)(2,1)S(1)} %get-tuple-element.34), channel_id=1, source_target_pairs={{4,0},{8,4},{12,8},{16,12},{20,16},{24,20},{28,24},{5,1},{9,5},{13... | collective-permute-start | bytes 1720328 | tf_op jit(solution)/shard_map/ppermute | solution.py:30
  77.9 7.9 %collective-permute-start.8 = (bf16[7,144,256]{2,1,0:T(8,128)(2,1)S(1)}, bf16[7,144,256]{2,1,0:T(8,128)(2,1)S(1)}, u32[]{:S(2)}, u32[]{:S(2)}) collective-permute-start(bf16[7,144,256]{2,1,0:T(8,128)(2,1)S(1)} %get-tuple-element.36), channel_id=1, source_target_pairs={{0,4},{4,8},{8,12},{12,16},{16,20},{20,24},{24,28},{1,5},{5,9},{9,... | collective-permute-start | bytes 1548296 | tf_op jit(solution)/shard_map/ppermute | solution.py:30
  79.8 13.0 %collective-permute-start.9 = (bf16[7,144,256]{2,1,0:T(8,128)(2,1)S(1)}, bf16[7,144,256]{2,1,0:T(8,128)(2,1)S(1)}, u32[]{:S(2)}, u32[]{:S(2)}) collective-permute-start(bf16[7,144,256]{2,1,0:T(8,128)(2,1)S(1)} %get-tuple-element.37), channel_id=1, source_target_pairs={{4,0},{8,4},{12,8},{16,12},{20,16},{24,20},{28,24},{5,1},{9,5},{13... | collective-permute-start | bytes 1548296 | tf_op jit(solution)/shard_map/ppermute | solution.py:30
  96.8 7.9 %collective-permute-start.10 = (bf16[7,144,256]{2,1,0:T(8,128)(2,1)S(1)}, bf16[7,144,256]{2,1,0:T(8,128)(2,1)S(1)}, u32[]{:S(2)}, u32[]{:S(2)}) collective-permute-start(bf16[7,144,256]{2,1,0:T(8,128)(2,1)S(1)} %get-tuple-element.39), channel_id=1, source_target_pairs={{0,4},{4,8},{8,12},{12,16},{16,20},{20,24},{24,28},{1,5},{5,9},{9,... | collective-permute-start | bytes 1548296 | tf_op jit(solution)/shard_map/ppermute | solution.py:30
  98.8 11.9 %collective-permute-start.11 = (bf16[7,144,256]{2,1,0:T(8,128)(2,1)S(1)}, bf16[7,144,256]{2,1,0:T(8,128)(2,1)S(1)}, u32[]{:S(2)}, u32[]{:S(2)}) collective-permute-start(bf16[7,144,256]{2,1,0:T(8,128)(2,1)S(1)} %get-tuple-element.40), channel_id=1, source_target_pairs={{4,0},{8,4},{12,8},{16,12},{20,16},{24,20},{28,24},{5,1},{9,5},{13... | collective-permute-start | bytes 1548296 | tf_op jit(solution)/shard_map/ppermute | solution.py:30

commit v4 on v3

--- a/solution.py
+++ b/solution.py
@@ -18,6 +18,7 @@
 BLOCK = 2
 S, C, K, B, O, A, AX, AY, AZ, D = range(10)
 FIELDS = 10
+FINE = (C, K)
 BF16 = jnp.bfloat16
 F32 = jnp.float32
 VM = pl.BlockSpec(memory_space=pltpu.VMEM)
@@ -44,9 +45,16 @@
     return [(f, x) for f, first, count in spans for x in range(first, first + count)]
 
 
-def pack_kernel(p, v, k, b, c, row_ahead, row_behind, plane_ahead, plane_behind, held, sems):
+def rest(value):
+    return (value - value.astype(BF16).astype(F32)).astype(BF16)
+
+
+def pack_kernel(p, v, k, b, c_out, row_ahead, row_behind, plane_ahead, plane_behind, held, sems, out_sems):
     planes, rows, depth = p.shape
-    p_e, k_e, b_e = (held.at[i] for i in range(3, 6))
+    p_e, k_e, b_e, c = (held.at[i] for i in range(3, 7))
+
+    def away(x):
+        return pltpu.make_async_copy(c.at[x], c_out.at[x], out_sems.at[x])
 
     def copies(x):
         pairs = [(v.at[i, x], held.at[i, x]) for i in range(3)]
@@ -76,6 +84,7 @@
             vz_prev = jnp.where(lane == 0, 0.0, pltpu.roll(vz, 1, 1))
             div = (vx - vx_prev) + (vy - vy_prev) + (vz - vz_prev)
             c[x, sl, :] = -TIME_STEP * k_e[x, sl, :] * div
+        away(x).start()
         for f, field in enumerate(fields):
             row_ahead[f * planes + x] = field[x, pl.ds(rows - HY, HY), :].astype(BF16)
             row_behind[f * planes + x] = field[x, pl.ds(0, HY), :].astype(BF16)
@@ -86,11 +95,21 @@
     for out, spans in ((plane_ahead, ahead), (plane_behind, behind)):
         for i, (f, x) in enumerate(unit_list(spans)):
             out[i] = fields[f][x - HX].astype(BF16)
-    plane_ahead[len(unit_list(ahead))] = held[0, planes - 1].astype(BF16)
+    vx_at = len(unit_list(ahead))
+    plane_ahead[vx_at] = held[0, planes - 1].astype(BF16)
+    for out, first, x in ((plane_ahead, vx_at + 1, planes - 1), (plane_behind, len(unit_list(behind)), 0)):
+        for i, f in enumerate(FINE):
+            out[first + i] = rest(fields[f][x])
     row_ahead[4 * planes] = held[0, planes - 1, pl.ds(rows - HY, HY), :].astype(BF16)
     row_behind[4 * planes] = held[0, planes - 1, pl.ds(0, HY), :].astype(BF16)
     edge = held[1, :, rows - 1, :]
     row_ahead[4 * planes + 1] = jnp.concatenate([edge, jnp.zeros((HY - planes, depth), F32)], 0).astype(BF16)
+
+    def finish(x, _):
+        away(x).wait()
+        return 0
+
+    lax.fori_loop(0, planes, finish, 0)
 
 
 def corner_kernel(behind, ahead, own_ahead, own_behind, to_ahead, to_behind):
@@ -120,7 +139,9 @@
     to_ahead[2 * at + 2] = ahead[4 * planes]
 
 
-def sensors_kernel(traces, lateral, copies):
+def sensors_kernel(traces_in, lateral_in, copies, traces, lateral, sems):
+    for copy in taken((traces_in, lateral_in), (traces, lateral), sems):
+        copy.wait()
     own = traces.shape[0]
     for i in range(copies.shape[0]):
         copies[i, pl.ds(0, own), :] = traces[...]
@@ -185,17 +206,19 @@
         here, up, down, down_prev = later, up_next, down_next, down
 
 
-def advance_some(store, done, inner):
+def advance_some(store, done, inner, first_step, end_step):
     planes, rows = store.shape[1:3]
     fields = [store.at[S], store.at[O]]
     coef = [store.at[f] for f in (C, A, AX, AY, AZ, D)]
     edge = planes - HX
-    for step in range(1, HX + 1):
+    for step in range(first_step, end_step):
         now, then = fields[(step - 1) % 2], fields[step % 2]
         skip = (done + step - 1) // SUB
         t0, t1 = skip, rows // SUB - skip
         if inner:
-            first, count, stride, block = HX + step, (planes - 2 * HX - 2 * step) // 2, 2, 2
+            inside = planes - 2 * HX - 2 * step
+            block = 3 if inside % 3 == 0 else 4 if inside % 4 == 0 else 2
+            first, count, stride = HX + step, inside // block, block
         else:
             first, count, stride, block = step, 2, edge - 2 * step, HX
 
@@ -209,14 +232,13 @@
 
 def pack_state(store, to_ahead, to_behind, skip):
     planes, rows = store.shape[1:3]
-    own = planes - 2 * HX
+    edge = planes - HX
     sl = pl.ds(skip, rows - 2 * skip)
-    for i in range(HX):
-        to_ahead[i] = store[S, own + i, sl, :].astype(BF16)
-        to_behind[i] = store[S, HX + i, sl, :].astype(BF16)
-    for i in range(1, HX):
-        for out, x in ((to_ahead, own + i), (to_behind, HX + i - 1)):
-            out[HX + i - 1] = (store[S, x, sl, :] - store[O, x, sl, :]).astype(BF16)
+    for depth in range(2, HX + 1):
+        for out, x in ((to_behind, HX - 1 + depth), (to_ahead, edge - depth)):
+            out[depth - 2] = store[S, x, sl, :].astype(BF16)
+            if depth < HX:
+                out[HX + depth - 3] = (store[S, x, sl, :] - store[O, x, sl, :]).astype(BF16)
 
 
 def set_coefficients(store, x):
@@ -236,38 +258,53 @@
         store[AY, x, sl, :] = kk * b_y
         store[AZ, x, sl, :] = kk * b_z
         store[D, x, sl, :] = 2.0 - kk * (3.0 * bb + b_x + b_y + b_z)
+        store[C, x, sl, :] += store[O, x, sl, :]
         store[O, x, sl, :] = jnp.zeros((CHUNK, depth), F32)
 
 
-def add_source(tables, gathered, store):
+def by_group(row, groups, own):
+    count = row.shape[1] // own
+    per = LANES // own
+    lane = lax.broadcasted_iota(jnp.int32, (1, LANES), 1) // own
+    order = [t * groups + g for g in range(groups) for t in range(count // groups)]
+    parts = []
+    for first in range(0, count, per):
+        part = jnp.zeros((1, LANES), row.dtype)
+        for i in range(per):
+            block, at = divmod(order[first + i], per)
+            piece = row[:, LANES * block : LANES * (block + 1)]
+            shift = own * (i - at) % LANES
+            part = jnp.where(lane == i, pltpu.roll(piece, shift, 1) if shift else piece, part)
+        parts.append(part)
+    return jnp.concatenate(parts, 1)
+
+
+def put_source(routes, centre, gathered, store, held):
     planes, rows, depth = store.shape[1:]
     own, own_rows = planes - 2 * HX, rows - 2 * HY
     groups = gathered.shape[0]
-    top = tables.shape[0] - 1
+    top = routes.shape[0]
     samples = gathered.shape[1] - top * own
     trace = jnp.concatenate([gathered[g, pl.ds(0, samples), :] for g in range(groups)], 1).astype(F32)
     sensors = trace.shape[1]
     row_at = lax.axis_index("grp") * own_rows - HY + lax.broadcasted_iota(jnp.int32, (rows, sensors), 0)
-    distance = jnp.abs(row_at - tables[pl.ds(top, 1), :]).astype(F32)
+    distance = jnp.abs(row_at - by_group(centre[...], groups, held)).astype(F32)
     band = jnp.maximum(0.0, 1.0 - distance / BAND)
     band = jnp.where((row_at >= 0) & (row_at < own_rows * groups), band, 0.0).astype(BF16)
     slab_at = lax.axis_index("slab")
     weights = [jnp.zeros((own, sensors), F32) for _ in range(3)]
     for i in range(top):
+        route = by_group(routes[pl.ds(i, 1), :], groups, held)
         lat = [gathered[g, pl.ds(samples + i * own, own), :] for g in range(groups)]
         lat = jnp.concatenate(lat, 1).astype(F32)
         for j in range(3):
-            weights[j] = weights[j] + jnp.where(tables[pl.ds(i, 1), :] == slab_at + (j - 1), lat, 0.0)
+            weights[j] = weights[j] + jnp.where(route == slab_at + (j - 1), lat, 0.0)
     for x in range(1, planes - 1):
         side, at = divmod(x + own - HX, own)
         outer = (trace * weights[side][at : at + 1]).astype(BF16)
-        src = TIME_STEP * lax.dot_general(band, outer, (((1,), (1,)), ((), ())), preferred_element_type=F32)
-        later = pl.ds(depth - samples, samples)
-        if side == 1:
-            store[C, x, :, later] += src
-        else:
-            store[C, x, :, pl.ds(0, depth - samples)] = jnp.zeros((rows, depth - samples), F32)
-            store[C, x, :, later] = src
+        src = lax.dot_general(band, outer, (((1,), (1,)), ((), ())), preferred_element_type=F32)
+        store[O, x, :, pl.ds(0, depth - samples)] = jnp.zeros((rows, depth - samples), F32)
+        store[O, x, :, pl.ds(depth - samples, samples)] = TIME_STEP * src
 
 
 def taken(given, held, sems):
@@ -277,103 +314,110 @@
     return copies
 
 
-def own_kernel(*refs):
-    given, (p, k, b, c), store = refs[:5], refs[5:9], refs[9]
-    held, sems = refs[10:15], refs[15]
-    row_behind, row_ahead, own_ahead, tables, gathered = held
+def own_kernel(*refs, held):
+    given, (p, k, b, c, v), store = refs[:6], refs[6:11], refs[11]
+    kept, sems = refs[12:18], refs[18]
+    routes, centre, gathered, row_behind, row_ahead, own_ahead = kept
     planes, rows, _ = store.shape[1:]
     own, own_rows = planes - 2 * HX, rows - 2 * HY
     low, middle, high = pl.ds(0, HY), pl.ds(HY, own_rows), pl.ds(HY + own_rows, HY)
-    here = [store.at[f, pl.ds(HX, own), middle, :] for f in (S, K, B, C)]
-    copies = taken(given + (p, k, b, c), held + tuple(here), sems)
+    here = [store.at[f, pl.ds(HX, own), middle, :] for f in (S, K, B, C)] + [store.at[K, 0, middle, :]]
+    copies = taken(given + (p, k, b, c, v.at[0, own - 1]), kept + tuple(here), sems)
     for copy in copies[:3]:
+        copy.wait()
+    put_source(routes, centre, gathered, store, held)
+    for copy in copies[3:]:
         copy.wait()
     for x in range(own):
         for f in (S, C, K, B):
             store[f, HX + x, low, :] = row_behind[f * own + x].astype(F32)
             store[f, HX + x, high, :] = row_ahead[f * own + x].astype(F32)
-    for copy in copies[3:]:
-        copy.wait()
+    store[K, 0, low, :] = row_behind[4 * own].astype(F32)
+    store[K, 0, high, :] = row_ahead[4 * own].astype(F32)
     vy_behind = row_behind[4 * own + 1].astype(F32)
     vy_last = own_ahead[4 * own + 1].astype(F32)
     for x in range(own):
         for at, vy in ((HY, vy_behind), (HY + own_rows, vy_last)):
             sl = pl.ds(at, 1)
             store[C, HX + x, sl, :] += TIME_STEP * store[K, HX + x, sl, :] * vy[x : x + 1]
-    add_source(tables, gathered, store)
 
     def one_plane(x, _):
         set_coefficients(store, x)
         return 0
 
     lax.fori_loop(HX + 1, HX + own, one_plane, 0)
-    advance_some(store, 0, True)
+    advance_some(store, 0, True, 1, HX)
 
 
 def first_round_kernel(*refs):
-    given, v, store, to_ahead, to_behind = refs[:6], refs[6], refs[8], refs[9], refs[10]
-    held, line, sems = refs[11:17], refs[17], refs[18]
-    behind, ahead, corner_behind, corner_ahead, row_behind, row_ahead = held
+    given, store, to_ahead, to_behind = refs[:4], refs[5], refs[6], refs[7]
+    held, sems = refs[8:12], refs[12]
+    behind, ahead, corner_behind, corner_ahead = held
     planes, rows, _ = store.shape[1:]
     edge = planes - HX
     own, own_rows = planes - 2 * HX, rows - 2 * HY
     low, middle, high = pl.ds(0, HY), pl.ds(HY, own_rows), pl.ds(HY + own_rows, HY)
-    copies = taken(given + (v.at[0, own - 1],), held + (line.at[middle, :],), sems)
+    copies = taken(given, held, sems)
     sent_ahead, sent_behind = main_planes(own)
     moves = ((behind, corner_behind, sent_ahead, -own), (ahead, corner_ahead, sent_behind, own))
-    for copy in copies:
-        copy.wait()
-    for main, corner, spans, shift in moves:
+    for side, (main, corner, spans, shift) in enumerate(moves):
+        copies[side].wait()
+        copies[2 + side].wait()
         units = unit_list(spans)
         for i, (f, x) in enumerate(units):
-            parts = ((low, corner[2 * i]), (middle, main[i]), (high, corner[2 * i + 1]))
-            for sl, part in parts:
-                part = part.astype(F32)
-                if f == C:
-                    part = part + store[C, x + shift, sl, :]
-                store[f, x + shift, sl, :] = part
+            store[f, x + shift, low, :] = corner[2 * i].astype(F32)
+            store[f, x + shift, middle, :] = main[i].astype(F32)
+            store[f, x + shift, high, :] = corner[2 * i + 1].astype(F32)
+        for i, f in enumerate(FINE):
+            first = len(units) + (1 if side == 0 else 0)
+            store[f, HX - 1 if side == 0 else edge, middle, :] += main[first + i].astype(F32)
         _, x, count = spans[1]
         fixed = corner[2 * len(units)].astype(F32)
         for i in range(count):
             store[C, x + shift + i, pl.ds(HY, 1), :] += fixed[i : i + 1]
-    line[low, :] = row_behind[4 * own].astype(F32)
-    line[high, :] = row_ahead[4 * own].astype(F32)
     at = len(unit_list(sent_ahead))
-    vx_parts = ((low, corner_behind[2 * at + 1]), (middle, behind[at]), (high, corner_behind[2 * at + 2]))
+    vx_parts = (
+        (low, corner_behind[2 * at + 1].astype(F32)),
+        (middle, behind[at].astype(F32)),
+        (high, corner_behind[2 * at + 2].astype(F32)),
+    )
     for sl, part in vx_parts:
-        store[C, HX, sl, :] += TIME_STEP * store[K, HX, sl, :] * part.astype(F32)
-        store[C, edge, sl, :] += TIME_STEP * store[K, edge, sl, :] * line[sl, :]
+        store[C, HX, sl, :] += TIME_STEP * store[K, HX, sl, :] * part
+        store[C, edge, sl, :] += TIME_STEP * store[K, edge, sl, :] * store[K, 0, sl, :]
 
     def one_plane(i, _):
         set_coefficients(store, jnp.where(i < HX, i + 1, i + edge - HX))
         return 0
 
     lax.fori_loop(0, 2 * HX - 1, one_plane, 0)
-    advance_some(store, 0, False)
+    advance_some(store, 0, False, 1, HX + 1)
     pack_state(store, to_ahead, to_behind, 0)
 
 
 def inner_kernel(store_i, store, *, done):
     del store_i
-    advance_some(store, done, True)
-
-
-def take_halo(behind, ahead, store, skip):
+    advance_some(store, done, True, 1, HX)
+
+
+def take_halo(behind, ahead, store, done, skip):
     planes, rows = store.shape[1:3]
     edge = planes - HX
     sl = pl.ds(skip, rows - 2 * skip)
-    for i in range(HX):
-        store[S, i, sl, :] = behind[i].astype(F32)
-        store[S, edge + i, sl, :] = ahead[i].astype(F32)
-    for i in range(1, HX):
-        for x, got in ((i, behind), (edge + i - 1, ahead)):
-            store[O, x, sl, :] = store[S, x, sl, :] - got[HX + i - 1].astype(F32)
+    for depth in range(2, HX + 1):
+        for x, got in ((HX - depth, behind), (edge - 1 + depth, ahead)):
+            store[S, x, sl, :] = got[depth - 2].astype(F32)
+            if depth < HX:
+                store[O, x, sl, :] = store[S, x, sl, :] - got[HX + depth - 3].astype(F32)
+    coef = [store.at[f] for f in (C, A, AX, AY, AZ, D)]
+    t0 = (done - 1) // SUB
+    for x in (HX - 1, edge):
+        advance_planes(store.at[O], store.at[S], coef, x, 1, t0, rows // SUB - t0)
 
 
 def middle_round_kernel(behind, ahead, store_i, store, to_ahead, to_behind, *, done, skips):
     del store_i
-    take_halo(behind, ahead, store, skips[0])
-    advance_some(store, done, False)
+    take_halo(behind, ahead, store, done, skips[0])
+    advance_some(store, done, False, 1, HX + 1)
     pack_state(store, to_ahead, to_behind, skips[1])
 
 
@@ -385,12 +429,11 @@
     def reads(x):
         return [pltpu.make_async_copy(v.at[i, x], held.at[i, x], in_sems.at[i, x]) for i in range(3)]
 
-    def writes(x):
-        pairs = [(f, v_out.at[i, x]) for i, f in enumerate((A, AX, AY))] + [(AZ, p_out.at[x])]
-        return [
-            pltpu.make_async_copy(store.at[f, HX + x, own, :], dst, out_sems.at[i, x])
-            for i, (f, dst) in enumerate(pairs)
-        ]
+    def velocity_away(x):
+        return [pltpu.make_async_copy(held.at[i, x], v_out.at[i, x], out_sems.at[i, x]) for i in range(3)]
+
+    def pressure_away(x):
+        return pltpu.make_async_copy(store.at[K, HX + x, own, :], p_out.at[x], out_sems.at[3, x])
 
     def start(x, _):
         for copy in reads(x):
@@ -398,10 +441,10 @@
         return 0
 
     lax.fori_loop(0, planes, start, 0)
-    take_halo(behind, ahead, store, skip)
-    advance_some(store, done, False)
-
-    def one_plane(x, _):
+    take_halo(behind, ahead, store, done, skip)
+    advance_some(store, done, False, 1, HX)
+
+    def last_velocity(x, _):
         for copy in reads(x):
             copy.wait()
         for r in range(0, rows, CHUNK):
@@ -413,19 +456,27 @@
             y_next = jnp.where(row == CHUNK - 1, below, pltpu.roll(total, CHUNK - 1, 0))
             z_next = jnp.where(lane == depth - 1, 0.0, pltpu.roll(total, depth - 1, 1))
             bb = TIME_STEP * store[B, HX + x, at, :]
-            store[A, HX + x, at, :] = held[0, x, sl, :] - bb * (store[O, HX + x + 1, at, :] - total)
-            store[AX, HX + x, at, :] = held[1, x, sl, :] - bb * (y_next - total)
-            store[AY, HX + x, at, :] = held[2, x, sl, :] - bb * (z_next - total)
-            store[AZ, HX + x, at, :] = store[S, HX + x, at, :] - total
-        for copy in writes(x):
+            held[0, x, sl, :] = held[0, x, sl, :] - bb * (store[O, HX + x + 1, at, :] - total)
+            held[1, x, sl, :] = held[1, x, sl, :] - bb * (y_next - total)
+            held[2, x, sl, :] = held[2, x, sl, :] - bb * (z_next - total)
+        for copy in velocity_away(x):
             copy.start()
         return 0
 
-    lax.fori_loop(0, planes, one_plane, 0)
+    lax.fori_loop(0, planes, last_velocity, 0)
+    advance_some(store, done, False, HX, HX + 1)
+
+    def last_pressure(x, _):
+        store[K, HX + x, own, :] = store[S, HX + x, own, :] - store[O, HX + x, own, :]
+        pressure_away(x).start()
+        return 0
+
+    lax.fori_loop(0, planes, last_pressure, 0)
 
     def finish(x, _):
-        for copy in writes(x):
+        for copy in velocity_away(x):
             copy.wait()
+        pressure_away(x).wait()
         return 0
 
     lax.fori_loop(0, planes, finish, 0)
@@ -442,6 +493,12 @@
 
     def everyones(copies, axis):
         return lax.all_to_all(copies, axis, split_axis=0, concat_axis=0, tiled=True)
+
+    def in_hbm(*values):
+        return [pltpu.with_memory_space_constraint(x, pltpu.HBM) for x in values]
+
+    def copied(given, extra):
+        return [pltpu.VMEM(x.shape, x.dtype) for x in given] + [pltpu.SemaphoreType.DMA((len(given) + extra,))]
 
     held, samples = traces.shape
     top = routes.shape[1]
@@ -449,26 +506,29 @@
     copies = pl.pallas_call(
         sensors_kernel,
         out_shape=jax.ShapeDtypeStruct((slabs, held + top * planes, samples), BF16),
-        in_specs=[VM] * 2,
+        in_specs=[HBM] * 2,
         out_specs=VM,
+        scratch_shapes=copied((traces, weights), 0),
         compiler_params=params(4),
-    )(traces, weights)
+    )(*in_hbm(traces, weights))
     got = everyones(copies, "slab")
-    tables = jnp.concatenate([routes.T, ycenter[None]], 0)
-    tables = jnp.swapaxes(tables.reshape(top + 1, slabs, groups, held), 1, 2).reshape(top + 1, -1)
 
     n_rows = 4 * planes
     n_ahead, n_behind = [len(unit_list(spans)) for spans in main_planes(planes)]
-    inputs = [pltpu.with_memory_space_constraint(x, pltpu.HBM) for x in (pressure, velocity, stiffness, buoyancy)]
+    inputs = in_hbm(pressure, velocity, stiffness, buoyancy)
     c, row_ahead, row_behind, plane_ahead, plane_behind = pl.pallas_call(
         pack_kernel,
         out_shape=(
-            jax.ShapeDtypeStruct(pressure.shape, F32), sent(n_rows + 2, HY), sent(n_rows + 1, HY),
-            sent(n_ahead + 1, rows), sent(n_behind, rows),
+            pltpu.HBM(pressure.shape, F32), sent(n_rows + 2, HY), sent(n_rows + 1, HY),
+            sent(n_ahead + 1 + len(FINE), rows), sent(n_behind + len(FINE), rows),
         ),
         in_specs=[HBM] * 4,
-        out_specs=[VM] * 5,
-        scratch_shapes=[pltpu.VMEM((6,) + pressure.shape, F32), pltpu.SemaphoreType.DMA((6, planes))],
+        out_specs=[HBM] + [VM] * 4,
+        scratch_shapes=[
+            pltpu.VMEM((7,) + pressure.shape, F32),
+            pltpu.SemaphoreType.DMA((6, planes)),
+            pltpu.SemaphoreType.DMA((planes,)),
+        ],
         compiler_params=params(24),
     )(*inputs)
     from_behind = passed_along(row_ahead, "grp", 1)
@@ -496,32 +556,25 @@
     corner_from_behind = passed_along(corner_ahead, "slab", 1)
     corner_from_ahead = passed_along(corner_behind, "slab", -1)
 
-    def in_hbm(*values):
-        return [pltpu.with_memory_space_constraint(x, pltpu.HBM) for x in values]
-
-    def copied(given, extra):
-        return [pltpu.VMEM(x.shape, x.dtype) for x in given] + [pltpu.SemaphoreType.DMA((len(given) + extra,))]
-
-    given = (from_behind, from_ahead, row_ahead, tables, gathered)
+    given = (routes.T, ycenter[None], gathered, from_behind, from_ahead, row_ahead)
     store = pl.pallas_call(
-        own_kernel,
+        functools.partial(own_kernel, held=held),
         out_shape=store_shape,
-        in_specs=[HBM] * 9,
+        in_specs=[HBM] * 11,
         out_specs=VM,
-        scratch_shapes=copied(given, 4),
+        scratch_shapes=copied(given, 5),
         compiler_params=params(14),
-    )(*in_hbm(*given), inputs[0], inputs[2], inputs[3], *in_hbm(c))
-    given = (main_behind, main_ahead, corner_from_behind, corner_from_ahead, from_behind, from_ahead)
-    scratch = copied(given, 1)
+    )(*in_hbm(*given), inputs[0], inputs[2], inputs[3], *in_hbm(c), inputs[1])
+    given = (main_behind, main_ahead, corner_from_behind, corner_from_ahead)
     store, plane_ahead, plane_behind = pl.pallas_call(
         first_round_kernel,
-        out_shape=(store_shape, sent(2 * HX - 1, tall), sent(2 * HX - 1, tall)),
-        in_specs=[HBM] * 7 + [VM],
+        out_shape=(store_shape, sent(2 * HX - 3, tall), sent(2 * HX - 3, tall)),
+        in_specs=[HBM] * 4 + [VM],
         out_specs=[VM] * 3,
-        input_output_aliases={7: 0},
-        scratch_shapes=scratch[:-1] + [pltpu.VMEM((tall, depth), F32), scratch[-1]],
+        input_output_aliases={4: 0},
+        scratch_shapes=copied(given, 0),
         compiler_params=params(14),
-    )(*in_hbm(*given), inputs[1], store)
+    )(*in_hbm(*given), store)
 
     def inner(store, done):
         return pl.pallas_call(
@@ -542,7 +595,7 @@
         height = tall - 2 * skips[r]
         store, plane_ahead, plane_behind = pl.pallas_call(
             functools.partial(middle_round_kernel, done=HX * r, skips=skips[r - 1 : r + 1]),
-            out_shape=(store_shape, sent(2 * HX - 1, height), sent(2 * HX - 1, height)),
+            out_shape=(store_shape, sent(2 * HX - 3, height), sent(2 * HX - 3, height)),
             in_specs=[VM] * 3,
             out_specs=[VM] * 3,
             input_output_aliases={2: 0},

time: 119 us -> 106 us (0.89)
  waiting for transfers between devices: 31.2 us -> 24.3 us
  local copies, waits for them, and re-layouts: 5.27 us -> 0.69 us
  starting transfers between devices: 40.4 us -> 39.1 us
    ppermute x12, waiting for transfers between devices: 31.2 us -> 24.3 us  [passed_along(): lax.ppermute(value, axis, [(source, source + steps) for source in range(f...]
    unnamed x14 -> x8, local copies, waits for them, and re-layouts: 3.02 us -> 0.69 us
    concatenate x4 -> x0, local copies, waits for them, and re-layouts: 1.57 us -> none  [local(): tables = jnp.concatenate([routes.T, ycenter[None]], 0)]
    ppermute x12, starting transfers between devices: 29.8 us -> 28.5 us  [passed_along(): lax.ppermute(value, axis, [(source, source + steps) for source in range(f...]
  transfers between devices with their start and end apart: 14 -> 14, of which waited for: 7 -> 8; matrix products, arithmetic and copies ran while one was open for 2% -> 0% of each run, Pallas kernels for 14% -> 15%
where the time goes in v4:
time: 106 us; the launch traced here: 105 us
  Pallas kernels  40.1 us (38%)
  starting transfers between devices  39.1 us (37%)
  waiting for transfers between devices  24.3 us (23%)
    ppermute x12, starting transfers between devices, passed_along(): lax.ppermute(value, axis, [(source, source + steps) for source in range(f...  28.5 us
    ppermute x12, waiting for transfers between devices, passed_along(): lax.ppermute(value, axis, [(source, source + steps) for source in range(f...  24.3 us
    all_to_all x2, starting transfers between devices, everyones(): return lax.all_to_all(copies, axis, split_axis=0, concat_axis=0, tiled=True)  10.6 us
    pallas_call x2, Pallas kernels, local(): pl.pallas_call(functools.partial(middle_round_kernel, done=HX * r, skips=...  8.77 us
    pallas_call x1, Pallas kernels, local(): pl.pallas_call(first_round_kernel, out_shape=(store_shape, sent(2 * HX -...  7.46 us
    pallas_call x1, Pallas kernels, local(): pl.pallas_call(functools.partial(last_round_kernel, done=HX * (rounds - 1...  6.5 us
    pallas_call x1, Pallas kernels, local(): pl.pallas_call(functools.partial(own_kernel, held=held), out_shape=store_...  5.61 us
    pallas_call x3, Pallas kernels, inner(): pl.pallas_call(functools.partial(inner_kernel, done=done), out_shape=stor...  4.44 us
  transfers between devices with their start and end apart: 14, of which 8 were waited for; matrix products, arithmetic and copies ran while one was open for 0% of the time, Pallas kernels for 15%

profile of v4, /device:TPU:1, one launch (start us, length us, event | category | flops | bytes accessed | tf_op | source)
XLA Modules:
  0.0 105.2 jit_solution(9585206954481544521)
XLA Ops:
  0.6 1.4 %shard_map.95 = bf16[8,48,128]{2,1,0:T(8,128)(2,1)} custom-call(bf16[32,128]{1,0:T(8,128)(2,1)} %traces_in.1, bf16[16,32]{1,0:T(8,128)(2,1)} %bitcast.7), custom_call_target="tpu_custom_call" | custom-call | tf_op jit(solution)/shard_map/pallas_call | solution.py:506
  2.0 5.2 %all-to-all-start = ((bf16[8,48,128]{2,1,0:T(8,128)(2,1)}), bf16[8,48,128]{2,1,0:T(8,128)(2,1)S(1)}, u32[]{:S(2)}, u32[]{:S(2)}) async-start(bf16[8,48,128]{2,1,0:T(8,128)(2,1)} %shard_map.95), calls=%async_computation | async-start | bytes 196608 | tf_op jit(solution)/shard_map/all_to_all | solution.py:495
  7.3 4.3 %shard_map.96 = (f32[8,128,256]{2,1,0:T(8,128)}, bf16[34,16,256]{2,1,0:T(8,128)(2,1)S(1)}, bf16[33,16,256]{2,1,0:T(8,128)(2,1)S(1)}, bf16[17,128,256]{2,1,0:T(8,128)(2,1)S(1)}, bf16[15,128,256]{2,1,0:T(8,128)(2,1)S(1)}) custom-call(f32[8,128,256]{2,1,0:T(8,128)} %refs_6_.1, f32[3,8,128,256]{3,2,1,0:T(8,128)} %v.3, f32[8,128,256]{2,1,0:T(8,128)} %refs_7_.1, ...), custom_call_target="tpu_custom_call" | custom-call | tf_op jit(solution)/shard_map/pallas_call | solution.py:519
  11.6 0.0 copy-start
  11.6 0.0 all-to-all-done.got
  11.6 3.5 %collective-permute-start = (bf16[17,128,256]{2,1,0:T(8,128)(2,1)S(1)}, bf16[17,128,256]{2,1,0:T(8,128)(2,1)}, u32[]{:S(2)}, u32[]{:S(2)}) collective-permute-start(bf16[17,128,256]{2,1,0:T(8,128)(2,1)S(1)} %get-tuple-element.25), channel_id=1, source_target_pairs={{0,4},{4,8},{8,12},{12,16},{16,20},{20,24},{24,28},{1,5},{5,9},{9,... | collective-permute-start | bytes 3342344 | tf_op jit(solution)/shard_map/ppermute | solution.py:31
  15.2 1.9 %collective-permute-start.1 = (bf16[15,128,256]{2,1,0:T(8,128)(2,1)S(1)}, bf16[15,128,256]{2,1,0:T(8,128)(2,1)}, u32[]{:S(2)}, u32[]{:S(2)}) collective-permute-start(bf16[15,128,256]{2,1,0:T(8,128)(2,1)S(1)} %get-tuple-element.26), channel_id=1, source_target_pairs={{4,0},{8,4},{12,8},{16,12},{20,16},{24,20},{28,24},{5,1},{9,5},{13... | collective-permute-start | bytes 2949128 | tf_op jit(solution)/shard_map/ppermute | solution.py:31
  17.1 3.2 %collective-permute-start.2 = (bf16[34,16,256]{2,1,0:T(8,128)(2,1)S(1)}, bf16[34,16,256]{2,1,0:T(8,128)(2,1)S(1)}, u32[]{:S(2)}, u32[]{:S(2)}) collective-permute-start(bf16[34,16,256]{2,1,0:T(8,128)(2,1)S(1)} %get-tuple-element.27.own_ahead.refs_5_), channel_id=1, source_target_pairs={{0,1},{1,2},{2,3},{4,5},{5,6},{6,7},{8,9},{9,10},{10,11},{12,13},{... | collective-permute-start | bytes 835592 | tf_op jit(solution)/shard_map/ppermute | solution.py:31
  20.3 1.3 %collective-permute-start.3 = (bf16[33,16,256]{2,1,0:T(8,128)(2,1)S(1)}, bf16[33,16,256]{2,1,0:T(8,128)(2,1)S(1)}, u32[]{:S(2)}, u32[]{:S(2)}) collective-permute-start(bf16[33,16,256]{2,1,0:T(8,128)(2,1)S(1)} %get-tuple-element.28.own_behind), channel_id=1, source_target_pairs={{1,0},{2,1},{3,2},{5,4},{6,5},{7,6},{9,8},{10,9},{11,10},{13,12},{... | collective-permute-start | bytes 811016 | tf_op jit(solution)/shard_map/ppermute | solution.py:31
  21.6 0.8 shard_map.98
  22.4 5.4 %all-to-all-start.1 = ((bf16[4,144,256]{2,1,0:T(8,128)(2,1)}), bf16[4,144,256]{2,1,0:T(8,128)(2,1)}, u32[]{:S(2)}, u32[]{:S(2)}) async-start(bf16[4,144,256]{2,1,0:T(8,128)(2,1)} %shard_map.98), calls=%async_computation.1 | async-start | bytes 589824 | tf_op jit(solution)/shard_map/all_to_all | solution.py:495
  27.8 2.9 %collective-permute-done.3.ahead.refs_4_ = bf16[33,16,256]{2,1,0:T(8,128)(2,1)S(1)} collective-permute-done((bf16[33,16,256]{2,1,0:T(8,128)(2,1)S(1)}, bf16[33,16,256]{2,1,0:T(8,128)(2,1)S(1)}, u32[]{:S(2)}, u32[]{:S(2)}) %collective-permute-start.3) | collective-permute-done | bytes 270368 | tf_op jit(solution)/shard_map/ppermute | solution.py:31
  30.7 0.0 copy-start.2
  30.7 0.0 collective-permute-done.2.behind.refs_3_
  30.7 0.0 copy-start.1
  30.7 0.8 shard_map.97
  31.5 3.4 %collective-permute-start.4 = (bf16[31,16,256]{2,1,0:T(8,128)(2,1)S(1)}, bf16[31,16,256]{2,1,0:T(8,128)(2,1)S(1)}, u32[]{:S(2)}, u32[]{:S(2)}) collective-permute-start(bf16[31,16,256]{2,1,0:T(8,128)(2,1)S(1)} %get-tuple-element.29), channel_id=1, source_target_pairs={{0,4},{4,8},{8,12},{12,16},{16,20},{20,24},{24,28},{1,5},{5,9},{9,... | collective-permute-start | bytes 761864 | tf_op jit(solution)/shard_map/ppermute | solution.py:31
  34.9 1.9 %collective-permute-start.5 = (bf16[27,16,256]{2,1,0:T(8,128)(2,1)}, bf16[27,16,256]{2,1,0:T(8,128)(2,1)}, u32[]{:S(2)}, u32[]{:S(2)}) collective-permute-start(bf16[27,16,256]{2,1,0:T(8,128)(2,1)} %get-tuple-element.30), channel_id=1, source_target_pairs={{4,0},{8,4},{12,8},{16,12},{20,16},{24,20},{28,24},{5,1},{9,5},{13... | collective-permute-start | bytes 663560 | tf_op jit(solution)/shard_map/ppermute | solution.py:31
  36.8 0.0 all-to-all-done.1.refs_2_
  36.8 0.0 copy-done
  36.8 0.0 copy-done.2
  36.8 0.0 copy-done.1
  36.8 5.6 %shard_map.99.refs_4_ = f32[10,16,160,256]{3,2,1,0:T(8,128)S(1)} custom-call(s32[2,1024]{1,0:T(2,128)} %bitcast.5, s32[1,1024]{1,0:T(1,128)} %bitcast.6, bf16[4,144,256]{2,1,0:T(8,128)(2,1)} %all-to-all-done.1.refs_2_, bf16[34,16,256]{2,1,0:T(8,128)(2,1)} %copy-done.1, bf16[33,16,256]{2,1,0:T(8,128)(2,1)} %copy-done.2, bf16[34,16,256]{2,1,0:T(8,128)(2,1)} %copy-done, ...), custom_call_target="tpu_custom_call" | custom-call | tf_op jit(solution)/shard_map/pallas_call | solution.py:560
  42.5 2.5 %collective-permute-done.5.refs_3_ = bf16[27,16,256]{2,1,0:T(8,128)(2,1)} collective-permute-done((bf16[27,16,256]{2,1,0:T(8,128)(2,1)}, bf16[27,16,256]{2,1,0:T(8,128)(2,1)}, u32[]{:S(2)}, u32[]{:S(2)}) %collective-permute-start.5) | collective-permute-done | bytes 221216 | tf_op jit(solution)/shard_map/ppermute | solution.py:31
  44.9 0.0 collective-permute-done.4.refs_2_
  44.9 0.0 copy-start.3
  44.9 0.0 collective-permute-done.1.refs_1_
  44.9 0.0 collective-permute-done.refs_0_
  44.9 0.7 copy-done.3
  45.6 7.5 %shard_map.100 = (f32[10,16,160,256]{3,2,1,0:T(8,128)S(1)}, bf16[5,160,256]{2,1,0:T(8,128)(2,1)S(1)}, bf16[5,160,256]{2,1,0:T(8,128)(2,1)S(1)}) custom-call(bf16[17,128,256]{2,1,0:T(8,128)(2,1)} %collective-permute-done.refs_0_, bf16[15,128,256]{2,1,0:T(8,128)(2,1)} %collective-permute-done.1.refs_1_, ...), custom_call_target="tpu_custom_call", output_to_operand_aliasing={{0}: (4, {})} | custom-call | tf_op jit(solution)/shard_map/pallas_call | solution.py:569
  53.1 2.2 %collective-permute-start.6 = (bf16[5,160,256]{2,1,0:T(8,128)(2,1)S(1)}, bf16[5,160,256]{2,1,0:T(8,128)(2,1)S(1)}, u32[]{:S(2)}, u32[]{:S(2)}) collective-permute-start(bf16[5,160,256]{2,1,0:T(8,128)(2,1)S(1)} %get-tuple-element.33), channel_id=1, source_target_pairs={{0,4},{4,8},{8,12},{12,16},{16,20},{20,24},{24,28},{1,5},{5,9},{9,... | collective-permute-start | bytes 1228808 | tf_op jit(solution)/shard_map/ppermute | solution.py:31
  55.3 2.1 %collective-permute-start.7 = (bf16[5,160,256]{2,1,0:T(8,128)(2,1)S(1)}, bf16[5,160,256]{2,1,0:T(8,128)(2,1)S(1)}, u32[]{:S(2)}, u32[]{:S(2)}) collective-permute-start(bf16[5,160,256]{2,1,0:T(8,128)(2,1)S(1)} %get-tuple-element.34), channel_id=1, source_target_pairs={{4,0},{8,4},{12,8},{16,12},{20,16},{24,20},{28,24},{5,1},{9,5},{13... | collective-permute-start | bytes 1228808 | tf_op jit(solution)/shard_map/ppermute | solution.py:31
  57.5 1.6 %shard_map.101.store_i = f32[10,16,160,256]{3,2,1,0:T(8,128)S(1)} custom-call(f32[10,16,160,256]{3,2,1,0:T(8,128)S(1)} %get-tuple-element.35.store_i), custom_call_target="tpu_custom_call", output_to_operand_aliasing={{}: (0, {})} | custom-call | tf_op jit(solution)/shard_map/pallas_call | solution.py:580
  59.0 1.2 %collective-permute-done.6.behind = bf16[5,160,256]{2,1,0:T(8,128)(2,1)S(1)} collective-permute-done((bf16[5,160,256]{2,1,0:T(8,128)(2,1)S(1)}, bf16[5,160,256]{2,1,0:T(8,128)(2,1)S(1)}, u32[]{:S(2)}, u32[]{:S(2)}) %collective-permute-start.6) | collective-permute-done | bytes 409632 | tf_op jit(solution)/shard_map/ppermute | solution.py:31
  60.2 6.3 %collective-permute-done.7.ahead = bf16[5,160,256]{2,1,0:T(8,128)(2,1)S(1)} collective-permute-done((bf16[5,160,256]{2,1,0:T(8,128)(2,1)S(1)}, bf16[5,160,256]{2,1,0:T(8,128)(2,1)S(1)}, u32[]{:S(2)}, u32[]{:S(2)}) %collective-permute-start.7) | collective-permute-done | bytes 409632 | tf_op jit(solution)/shard_map/ppermute | solution.py:31
  66.5 4.6 %shard_map.102 = (f32[10,16,160,256]{3,2,1,0:T(8,128)S(1)}, bf16[5,144,256]{2,1,0:T(8,128)(2,1)S(1)}, bf16[5,144,256]{2,1,0:T(8,128)(2,1)S(1)}) custom-call(bf16[5,160,256]{2,1,0:T(8,128)(2,1)S(1)} %collective-permute-done.6.behind, bf16[5,160,256]{2,1,0:T(8,128)(2,1)S(1)} %collective-permute-done.7.ahead, ...), custom_call_target="tpu_custom_call", output_to_operand_aliasing={{0}: (2, {})} | custom-call | tf_op jit(solution)/shard_map/pallas_call | solution.py:596
  71.1 1.9 %collective-permute-start.8 = (bf16[5,144,256]{2,1,0:T(8,128)(2,1)S(1)}, bf16[5,144,256]{2,1,0:T(8,128)(2,1)S(1)}, u32[]{:S(2)}, u32[]{:S(2)}) collective-permute-start(bf16[5,144,256]{2,1,0:T(8,128)(2,1)S(1)} %get-tuple-element.36), channel_id=1, source_target_pairs={{0,4},{4,8},{8,12},{12,16},{16,20},{20,24},{24,28},{1,5},{5,9},{9,... | collective-permute-start | bytes 1105928 | tf_op jit(solution)/shard_map/ppermute | solution.py:31
  73.0 2.6 %collective-permute-start.9 = (bf16[5,144,256]{2,1,0:T(8,128)(2,1)S(1)}, bf16[5,144,256]{2,1,0:T(8,128)(2,1)S(1)}, u32[]{:S(2)}, u32[]{:S(2)}) collective-permute-start(bf16[5,144,256]{2,1,0:T(8,128)(2,1)S(1)} %get-tuple-element.37), channel_id=1, source_target_pairs={{4,0},{8,4},{12,8},{16,12},{20,16},{24,20},{28,24},{5,1},{9,5},{13... | collective-permute-start | bytes 1105928 | tf_op jit(solution)/shard_map/ppermute | solution.py:31
  75.6 1.4 %shard_map.103.store_i = f32[10,16,160,256]{3,2,1,0:T(8,128)S(1)} custom-call(f32[10,16,160,256]{3,2,1,0:T(8,128)S(1)} %get-tuple-element.38.store_i), custom_call_target="tpu_custom_call", output_to_operand_aliasing={{}: (0, {})} | custom-call | tf_op jit(solution)/shard_map/pallas_call | solution.py:580
  77.0 0.4 collective-permute-done.8.behind
  77.4 5.3 %collective-permute-done.9.ahead = bf16[5,144,256]{2,1,0:T(8,128)(2,1)S(1)} collective-permute-done((bf16[5,144,256]{2,1,0:T(8,128)(2,1)S(1)}, bf16[5,144,256]{2,1,0:T(8,128)(2,1)S(1)}, u32[]{:S(2)}, u32[]{:S(2)}) %collective-permute-start.9) | collective-permute-done | bytes 368672 | tf_op jit(solution)/shard_map/ppermute | solution.py:31
  82.7 4.2 %shard_map.104 = (f32[10,16,160,256]{3,2,1,0:T(8,128)S(1)}, bf16[5,144,256]{2,1,0:T(8,128)(2,1)S(1)}, bf16[5,144,256]{2,1,0:T(8,128)(2,1)S(1)}) custom-call(bf16[5,144,256]{2,1,0:T(8,128)(2,1)S(1)} %collective-permute-done.8.behind, bf16[5,144,256]{2,1,0:T(8,128)(2,1)S(1)} %collective-permute-done.9.ahead, ...), custom_call_target="tpu_custom_call", output_to_operand_aliasing={{0}: (2, {})} | custom-call | tf_op jit(solution)/shard_map/pallas_call | solution.py:596
  86.9 1.9 %collective-permute-start.10 = (bf16[5,144,256]{2,1,0:T(8,128)(2,1)S(1)}, bf16[5,144,256]{2,1,0:T(8,128)(2,1)S(1)}, u32[]{:S(2)}, u32[]{:S(2)}) collective-permute-start(bf16[5,144,256]{2,1,0:T(8,128)(2,1)S(1)} %get-tuple-element.39), channel_id=1, source_target_pairs={{0,4},{4,8},{8,12},{12,16},{16,20},{20,24},{24,28},{1,5},{5,9},{9,... | collective-permute-start | bytes 1105928 | tf_op jit(solution)/shard_map/ppermute | solution.py:31
  88.8 2.4 %collective-permute-start.11 = (bf16[5,144,256]{2,1,0:T(8,128)(2,1)S(1)}, bf16[5,144,256]{2,1,0:T(8,128)(2,1)S(1)}, u32[]{:S(2)}, u32[]{:S(2)}) collective-permute-start(bf16[5,144,256]{2,1,0:T(8,128)(2,1)S(1)} %get-tuple-element.40), channel_id=1, source_target_pairs={{4,0},{8,4},{12,8},{16,12},{20,16},{24,20},{28,24},{5,1},{9,5},{13... | collective-permute-start | bytes 1105928 | tf_op jit(solution)/shard_map/ppermute | solution.py:31
  91.3 1.4 %shard_map.105.store_i = f32[10,16,160,256]{3,2,1,0:T(8,128)S(1)} custom-call(f32[10,16,160,256]{3,2,1,0:T(8,128)S(1)} %get-tuple-element.41.store_i), custom_call_target="tpu_custom_call", output_to_operand_aliasing={{}: (0, {})} | custom-call | tf_op jit(solution)/shard_map/pallas_call | solution.py:580
  92.7 0.6 collective-permute-done.10.behind
  93.3 5.3 %collective-permute-done.11.ahead = bf16[5,144,256]{2,1,0:T(8,128)(2,1)S(1)} collective-permute-done((bf16[5,144,256]{2,1,0:T(8,128)(2,1)S(1)}, bf16[5,144,256]{2,1,0:T(8,128)(2,1)S(1)}, u32[]{:S(2)}, u32[]{:S(2)}) %collective-permute-start.11) | collective-permute-done | bytes 368672 | tf_op jit(solution)/shard_map/ppermute | solution.py:31
  98.6 6.5 %shard_map.106 = (f32[8,128,256]{2,1,0:T(8,128)}, f32[3,8,128,256]{3,2,1,0:T(8,128)}, f32[10,16,160,256]{3,2,1,0:T(8,128)S(1)}) custom-call(bf16[5,144,256]{2,1,0:T(8,128)(2,1)S(1)} %collective-permute-done.10.behind, bf16[5,144,256]{2,1,0:T(8,128)(2,1)S(1)} %collective-permute-done.11.ahead, f32[3,8,128,256]{3,2,1,0:T(8,128)} %v.3, ...), custom_call_target="tpu_custom_call", output_to_operand_aliasing={{2}: (3, {})} | custom-call | tf_op jit(solution)/shard_map/pallas_call | solution.py:607
Async XLA Ops:
  2.0 9.6 %all-to-all-start = ((bf16[8,48,128]{2,1,0:T(8,128)(2,1)}), bf16[8,48,128]{2,1,0:T(8,128)(2,1)S(1)}, u32[]{:S(2)}, u32[]{:S(2)}) async-start(bf16[8,48,128]{2,1,0:T(8,128)(2,1)} %shard_map.95), calls=%async_computation | async-start | bytes 196608 | tf_op jit(solution)/shard_map/all_to_all | solution.py:495
  11.6 25.2 %copy-start = (bf16[34,16,256]{2,1,0:T(8,128)(2,1)}, bf16[34,16,256]{2,1,0:T(8,128)(2,1)S(1)}, u32[]{:S(2)}) copy-start(bf16[34,16,256]{2,1,0:T(8,128)(2,1)S(1)} %get-tuple-element.27.own_ahead.refs_5_) | copy-start | bytes 835588
  11.6 33.3 %collective-permute-start = (bf16[17,128,256]{2,1,0:T(8,128)(2,1)S(1)}, bf16[17,128,256]{2,1,0:T(8,128)(2,1)}, u32[]{:S(2)}, u32[]{:S(2)}) collective-permute-start(bf16[17,128,256]{2,1,0:T(8,128)(2,1)S(1)} %get-tuple-element.25), channel_id=1, source_target_pairs={{0,4},{4,8},{8,12},{12,16},{16,20},{20,24},{24,28},{1,5},{5,9},{9,... | collective-permute-start | bytes 3342344 | tf_op jit(solution)/shard_map/ppermute | solution.py:31
  15.2 29.8 %collective-permute-start.1 = (bf16[15,128,256]{2,1,0:T(8,128)(2,1)S(1)}, bf16[15,128,256]{2,1,0:T(8,128)(2,1)}, u32[]{:S(2)}, u32[]{:S(2)}) collective-permute-start(bf16[15,128,256]{2,1,0:T(8,128)(2,1)S(1)} %get-tuple-element.26), channel_id=1, source_target_pairs={{4,0},{8,4},{12,8},{16,12},{20,16},{24,20},{28,24},{5,1},{9,5},{13... | collective-permute-start | bytes 2949128 | tf_op jit(solution)/shard_map/ppermute | solution.py:31
  17.1 13.6 %collective-permute-start.2 = (bf16[34,16,256]{2,1,0:T(8,128)(2,1)S(1)}, bf16[34,16,256]{2,1,0:T(8,128)(2,1)S(1)}, u32[]{:S(2)}, u32[]{:S(2)}) collective-permute-start(bf16[34,16,256]{2,1,0:T(8,128)(2,1)S(1)} %get-tuple-element.27.own_ahead.refs_5_), channel_id=1, source_target_pairs={{0,1},{1,2},{2,3},{4,5},{5,6},{6,7},{8,9},{9,10},{10,11},{12,13},{... | collective-permute-start | bytes 835592 | tf_op jit(solution)/shard_map/ppermute | solution.py:31
  20.3 10.4 %collective-permute-start.3 = (bf16[33,16,256]{2,1,0:T(8,128)(2,1)S(1)}, bf16[33,16,256]{2,1,0:T(8,128)(2,1)S(1)}, u32[]{:S(2)}, u32[]{:S(2)}) collective-permute-start(bf16[33,16,256]{2,1,0:T(8,128)(2,1)S(1)} %get-tuple-element.28.own_behind), channel_id=1, source_target_pairs={{1,0},{2,1},{3,2},{5,4},{6,5},{7,6},{9,8},{10,9},{11,10},{13,12},{... | collective-permute-start | bytes 811016 | tf_op jit(solution)/shard_map/ppermute | solution.py:31
  22.4 14.4 %all-to-all-start.1 = ((bf16[4,144,256]{2,1,0:T(8,128)(2,1)}), bf16[4,144,256]{2,1,0:T(8,128)(2,1)}, u32[]{:S(2)}, u32[]{:S(2)}) async-start(bf16[4,144,256]{2,1,0:T(8,128)(2,1)} %shard_map.98), calls=%async_computation.1 | async-start | bytes 589824 | tf_op jit(solution)/shard_map/all_to_all | solution.py:495
  30.7 6.1 %copy-start.2 = (bf16[33,16,256]{2,1,0:T(8,128)(2,1)}, bf16[33,16,256]{2,1,0:T(8,128)(2,1)S(1)}, u32[]{:S(2)}) copy-start(bf16[33,16,256]{2,1,0:T(8,128)(2,1)S(1)} %collective-permute-done.3.ahead.refs_4_) | copy-start | bytes 811012
  30.7 6.1 %copy-start.1 = (bf16[34,16,256]{2,1,0:T(8,128)(2,1)}, bf16[34,16,256]{2,1,0:T(8,128)(2,1)S(1)}, u32[]{:S(2)}) copy-start(bf16[34,16,256]{2,1,0:T(8,128)(2,1)S(1)} %collective-permute-done.2.behind.refs_3_) | copy-start | bytes 835588
  31.5 13.4 %collective-permute-start.4 = (bf16[31,16,256]{2,1,0:T(8,128)(2,1)S(1)}, bf16[31,16,256]{2,1,0:T(8,128)(2,1)S(1)}, u32[]{:S(2)}, u32[]{:S(2)}) collective-permute-start(bf16[31,16,256]{2,1,0:T(8,128)(2,1)S(1)} %get-tuple-element.29), channel_id=1, source_target_pairs={{0,4},{4,8},{8,12},{12,16},{16,20},{20,24},{24,28},{1,5},{5,9},{9,... | collective-permute-start | bytes 761864 | tf_op jit(solution)/shard_map/ppermute | solution.py:31
  34.9 10.1 %collective-permute-start.5 = (bf16[27,16,256]{2,1,0:T(8,128)(2,1)}, bf16[27,16,256]{2,1,0:T(8,128)(2,1)}, u32[]{:S(2)}, u32[]{:S(2)}) collective-permute-start(bf16[27,16,256]{2,1,0:T(8,128)(2,1)} %get-tuple-element.30), channel_id=1, source_target_pairs={{4,0},{8,4},{12,8},{16,12},{20,16},{24,20},{28,24},{5,1},{9,5},{13... | collective-permute-start | bytes 663560 | tf_op jit(solution)/shard_map/ppermute | solution.py:31
  44.9 0.7 copy-start.3
  53.1 7.1 %collective-permute-start.6 = (bf16[5,160,256]{2,1,0:T(8,128)(2,1)S(1)}, bf16[5,160,256]{2,1,0:T(8,128)(2,1)S(1)}, u32[]{:S(2)}, u32[]{:S(2)}) collective-permute-start(bf16[5,160,256]{2,1,0:T(8,128)(2,1)S(1)} %get-tuple-element.33), channel_id=1, source_target_pairs={{0,4},{4,8},{8,12},{12,16},{16,20},{20,24},{24,28},{1,5},{5,9},{9,... | collective-permute-start | bytes 1228808 | tf_op jit(solution)/shard_map/ppermute | solution.py:31
  55.3 11.1 %collective-permute-start.7 = (bf16[5,160,256]{2,1,0:T(8,128)(2,1)S(1)}, bf16[5,160,256]{2,1,0:T(8,128)(2,1)S(1)}, u32[]{:S(2)}, u32[]{:S(2)}) collective-permute-start(bf16[5,160,256]{2,1,0:T(8,128)(2,1)S(1)} %get-tuple-element.34), channel_id=1, source_target_pairs={{4,0},{8,4},{12,8},{16,12},{20,16},{24,20},{28,24},{5,1},{9,5},{13... | collective-permute-start | bytes 1228808 | tf_op jit(solution)/shard_map/ppermute | solution.py:31
  71.1 6.4 %collective-permute-start.8 = (bf16[5,144,256]{2,1,0:T(8,128)(2,1)S(1)}, bf16[5,144,256]{2,1,0:T(8,128)(2,1)S(1)}, u32[]{:S(2)}, u32[]{:S(2)}) collective-permute-start(bf16[5,144,256]{2,1,0:T(8,128)(2,1)S(1)} %get-tuple-element.36), channel_id=1, source_target_pairs={{0,4},{4,8},{8,12},{12,16},{16,20},{20,24},{24,28},{1,5},{5,9},{9,... | collective-permute-start | bytes 1105928 | tf_op jit(solution)/shard_map/ppermute | solution.py:31
  73.0 9.7 %collective-permute-start.9 = (bf16[5,144,256]{2,1,0:T(8,128)(2,1)S(1)}, bf16[5,144,256]{2,1,0:T(8,128)(2,1)S(1)}, u32[]{:S(2)}, u32[]{:S(2)}) collective-permute-start(bf16[5,144,256]{2,1,0:T(8,128)(2,1)S(1)} %get-tuple-element.37), channel_id=1, source_target_pairs={{4,0},{8,4},{12,8},{16,12},{20,16},{24,20},{28,24},{5,1},{9,5},{13... | collective-permute-start | bytes 1105928 | tf_op jit(solution)/shard_map/ppermute | solution.py:31
  86.9 6.4 %collective-permute-start.10 = (bf16[5,144,256]{2,1,0:T(8,128)(2,1)S(1)}, bf16[5,144,256]{2,1,0:T(8,128)(2,1)S(1)}, u32[]{:S(2)}, u32[]{:S(2)}) collective-permute-start(bf16[5,144,256]{2,1,0:T(8,128)(2,1)S(1)} %get-tuple-element.39), channel_id=1, source_target_pairs={{0,4},{4,8},{8,12},{12,16},{16,20},{20,24},{24,28},{1,5},{5,9},{9,... | collective-permute-start | bytes 1105928 | tf_op jit(solution)/shard_map/ppermute | solution.py:31
  88.8 9.7 %collective-permute-start.11 = (bf16[5,144,256]{2,1,0:T(8,128)(2,1)S(1)}, bf16[5,144,256]{2,1,0:T(8,128)(2,1)S(1)}, u32[]{:S(2)}, u32[]{:S(2)}) collective-permute-start(bf16[5,144,256]{2,1,0:T(8,128)(2,1)S(1)} %get-tuple-element.40), channel_id=1, source_target_pairs={{4,0},{8,4},{12,8},{16,12},{20,16},{24,20},{28,24},{5,1},{9,5},{13... | collective-permute-start | bytes 1105928 | tf_op jit(solution)/shard_map/ppermute | solution.py:31
